TPU v7x, 32 devices: a whole 2x2x4 slice. The times are simulated.
32 devices in a mesh: ctx: 8 (over y, x, core), head: 4 (over z).
Axes of the slice: x: 2, y: 2, z: 4, core: 2. Of those that a mesh axis runs over, the one named last changes fastest.
Arguments:
- q_lin: bfloat16 [3072, 4096], P('ctx', 'head'), may hold values from -6 to 6
- k_lin: bfloat16 [3072, 4096], P('ctx', 'head'), may hold values from -6 to 6
- v_lin: bfloat16 [3072, 4096], P('ctx', 'head'), may hold values from -33 to 33
- gate_log: float32 [32, 3072], P('head', 'ctx'), may hold values from -0.7 to 0
- lin_gain: float32 [4096], P('head'), may hold values from 0.1 to 1.9
- q_soft: bfloat16 [3072, 4096], P('ctx', 'head'), may hold values from -27 to 27
- k_soft: bfloat16 [3072, 4096], P('ctx', 'head'), may hold values from -27 to 27
- v_soft: bfloat16 [3072, 4096], P('ctx', 'head'), may hold values from -6 to 6
- doc_ids: int32 [3072], P('ctx'), may hold values from 0 to 7, never falling along the last dimension, each value on 1 to 1536 neighbouring positions
Outputs:
- lin_out: bfloat16 [3072, 4096], P('ctx', 'head')
- soft_out: bfloat16 [3072, 4096], P('ctx', 'head')
Inputs may be any that keep to these rules, and one draw needn't show every extreme that they name: `doc_ids`: document ids never fall along the tokens; every document holds 1 to 1536 tokens and one holds exactly 1536.
All inputs are finite; a program needn't handle non-finite values.
Results may differ from a plain program's by a relative error of at most 0.0065.
Values may be sent and summed in bfloat16 or wider, within the bound.
No kernel may reach another device: no remote copies, remote signals or barrier semaphores. Data moves between devices by JAX's collectives and lax.ppermute only.
A program may use at most 256 MiB of HBM per device.

v0:
```python
import jax
import jax.numpy as jnp
from jax import lax
from jax.sharding import PartitionSpec as P

ATTENTION_HEADS = 32
HD = 128


highest = lax.Precision.HIGHEST
epsilon = 1e-05
neg_large = -1e30


def carried_in(shard, axis, join, neutral):
    place = lax.axis_index(axis)
    gathered = jax.tree.map(
        lambda a, kind: lax.all_gather(a.astype(kind), axis),
        shard,
        jax.tree.map(lambda a: jnp.bfloat16 if a.dtype == jnp.float32 else a.dtype, shard),
    )
    state = jax.tree.map(lambda a, e: jnp.zeros_like(a) + jnp.asarray(e, a.dtype), shard, neutral)

    def one(turn, state):
        return join(
            state,
            jax.tree.map(
                lambda a, own: lax.dynamic_index_in_dim(a, turn, 0, False).astype(own.dtype),
                gathered,
                shard,
            ),
        )

    return lax.fori_loop(0, place, one, state)


def chain_combine(earlier, later):
    early_first, early_last, early_factor, early_state = earlier
    late_first, late_last, late_factor, late_state = later
    linked = (early_last[0] == late_first[0]) | (early_last[0] < 0) | (late_first[0] < 0)
    link_factor = jnp.where(linked, 1.0, 0.0).astype(jnp.float32)
    joined_first = jnp.where(early_first < 0, late_first, early_first)
    joined_last = jnp.where(late_last < 0, early_last, late_last)
    joined_factor = early_factor * late_factor * link_factor
    joined_state = late_state + (late_factor * link_factor)[:, None, None] * early_state
    return (joined_first, joined_last, joined_factor, joined_state)


def linear_core(q_lin, k_lin, v_lin, gate_log, lin_gain, doc_ids):
    block_rows = q_lin.shape[0]
    head_count = gate_log.shape[0]
    head_dim = q_lin.shape[1] // head_count
    queries = q_lin.reshape(block_rows, head_count, head_dim)
    key_heads = k_lin.reshape(block_rows, head_count, head_dim)
    valued = v_lin.reshape(block_rows, head_count, head_dim).astype(jnp.float32)
    cumulated = jnp.cumsum(gate_log, axis=1)
    positions = jnp.arange(block_rows)
    same_doc = (doc_ids[:, None] == doc_ids[None, :]) & (positions[:, None] >= positions[None, :])
    spread = jnp.minimum(cumulated[:, :, None] - cumulated[:, None, :], 0.0)
    decay_table = jnp.where(same_doc[None], jnp.exp(spread), 0.0)
    scores = (
        jnp.einsum("thd,shd->hts", queries, key_heads, preferred_element_type=jnp.float32)
        * decay_table
    )
    local_term = jnp.einsum("hts,shd->thd", scores, valued, precision=highest)
    end_doc = doc_ids[-1]
    end_weight = jnp.where(doc_ids[None, :] == end_doc, jnp.exp(cumulated[:, -1:] - cumulated), 0.0)
    weighted = key_heads.astype(jnp.float32) * end_weight.T[:, :, None]
    local_state = jnp.einsum("shd,she->hde", weighted, valued, precision=highest)
    through = jnp.exp(cumulated[:, -1]) * jnp.where(doc_ids[0] == end_doc, 1.0, 0.0)
    element = (doc_ids[:1], doc_ids[-1:], through, local_state)
    identity = (
        jnp.full((1,), -1, jnp.int32),
        jnp.full((1,), -1, jnp.int32),
        jnp.ones_like(through),
        jnp.zeros_like(local_state),
    )
    prefix = carried_in(element, "ctx", chain_combine, identity)
    prefix_last = prefix[1][0]
    prefix_state = prefix[3]
    carried = jnp.where(doc_ids[None, :] == prefix_last, jnp.exp(cumulated), 0.0)
    incoming_term = (
        jnp.einsum("thd,hde->the", queries.astype(jnp.float32), prefix_state, precision=highest)
        * carried.T[:, :, None]
    )
    raw_output = (local_term + incoming_term).reshape(block_rows, head_count * head_dim)
    square_sum = lax.psum(jnp.sum(raw_output * raw_output, axis=1), "head")
    mean_square = square_sum / (ATTENTION_HEADS * HD)
    return (raw_output * lax.rsqrt(mean_square + epsilon)[:, None] * lin_gain[None, :]).astype(
        jnp.bfloat16
    )


def soft_core(q_soft, k_soft, v_soft, doc_ids, head_count):
    block_rows = q_soft.shape[0]
    head_dim = q_soft.shape[1] // head_count
    ctx_index = lax.axis_index("ctx")
    queries = q_soft.reshape(block_rows, head_count, head_dim)
    my_start = ctx_index * block_rows
    query_pos = my_start + jnp.arange(block_rows)
    score_scale = head_dim ** (-0.5)
    key_piece = lax.all_gather(k_soft, "ctx", axis=0, tiled=True)
    run_max = jnp.full((head_count, block_rows), neg_large, jnp.float32)
    piece_rows = key_piece.shape[0]
    key_pos = jnp.arange(piece_rows)
    allowed = (
        (key_pos[None, :] <= query_pos[:, None])
        & (lax.all_gather(doc_ids, "ctx", axis=0, tiled=True)[None, :] == doc_ids[:, None])
        & True
    )
    scores = (
        jnp.einsum(
            "qhd,khd->hqk",
            queries,
            key_piece.reshape(piece_rows, head_count, head_dim),
            preferred_element_type=jnp.float32,
        )
        * score_scale
    )
    new_max = jnp.maximum(run_max, jnp.max(jnp.where(allowed[None], scores, neg_large), axis=2))
    weights = jnp.where(allowed[None], jnp.exp(scores - new_max[:, :, None]), 0.0)
    new_total = jnp.sum(weights, axis=2)
    update = jnp.einsum(
        "hqk,khd->hqd",
        weights.astype(jnp.bfloat16),
        lax.all_gather(v_soft, "ctx", axis=0, tiled=True).reshape(piece_rows, head_count, head_dim),
        preferred_element_type=jnp.float32,
    )
    finished = (new_max, new_total, update)
    run_max, run_total, run_accum = finished
    normalized = run_accum / run_total[:, :, None]
    return (
        normalized.transpose(1, 0, 2)
        .reshape(block_rows, head_count * head_dim)
        .astype(jnp.bfloat16)
    )


def on_device(q_lin, k_lin, v_lin, gate_log, lin_gain, q_soft, k_soft, v_soft, doc_ids):
    lin_out = linear_core(q_lin, k_lin, v_lin, gate_log, lin_gain, doc_ids)
    soft_out = soft_core(q_soft, k_soft, v_soft, doc_ids, gate_log.shape[0])
    return (lin_out, soft_out)


def solution(mesh):
    in_specs = (
        P("ctx", "head"),
        P("ctx", "head"),
        P("ctx", "head"),
        P("head", "ctx"),
        P("head"),
        P("ctx", "head"),
        P("ctx", "head"),
        P("ctx", "head"),
        P("ctx"),
    )
    out_specs = (P("ctx", "head"), P("ctx", "head"))
    return jax.shard_map(
        on_device, mesh=mesh, in_specs=in_specs, out_specs=out_specs, check_vma=False
    )
```

profile of v0, /device:TPU:0, one launch (start us, length us, event | category | flops | bytes accessed | tf_op | source)
XLA Modules:
  0.0 179.9 jit_solution(18056344617477050425)
XLA Ops:
  7.3 1.4 dynamic-slice
  8.7 2.1 %fusion.50 = (s32[1]{0:T(128)}, s32[8]{0:T(128)S(1)}, s32[1]{0:T(128)}) fusion(s32[384]{0:T(512)} %param.19, s32[8]{0:T(128)S(1)} %broadcast.96.clone, u32[]{:T(128)} %bitcast.8), kind=kLoop, calls=%fused_computation.68 | loop fusion | bytes 52 | tf_op jit(solution)/shard_map/slice | solution.py:71
  10.7 1.3 broadcast_compare_fusion.1
  12.1 1.9 %reduce-window.6 = f32[8,3,128]{2,0,1:T(8,128)S(1)} reduce-window(f32[8,3,128]{2,0,1:T(8,128)} %bitcast.101, f32[]{:T(128)} %constant.28.clone.1), window={size=1x1x128 pad=0_0x0_0x127_0}, to_apply=%region_0.0 | reduce-window | flops 390144 | bytes 24580 | tf_op jit(solution)/shard_map/reduce-window
  14.4 1.5 copy.63
  16.0 2.8 %fusion.28 = bf16[8,128,128]{2,1,0:T(8,128)(2,1)} fusion(bf16[384,8,128]{0,2,1:T(8,128)(2,1)S(1)} %bitcast.92, f32[384,8]{0,1:T(8,128)S(1)} %select_bitcast_fusion.1, bf16[384,1024]{1,0:T(8,128)(2,1)} %param.13), kind=kOutput, calls=%fused_computation.34 | convolution fusion | flops 604897280 | bytes 1847296 | tf_op jit(solution)/shard_map/shd,she->hde/dot_general | solution.py:69
  18.9 2.3 %copy.56 = bf16[384,1024]{0,1:T(8,128)(2,1)} copy(bf16[384,1024]{1,0:T(8,128)(2,1)} %param.17) | data formatting | bytes 1572864 | tf_op args[6]
  22.8 9.5 %all-reduce.3 = (s32[8]{0:T(128)S(1)}, s32[8]{0:T(128)S(1)}) all-reduce(s32[8]{0:T(128)S(1)} %get-tuple-element.103, s32[8]{0:T(128)S(1)} %slice_dynamic-update-slice_fusion), channel_id=2, replica_groups=mesh['ctx'=8,'head'=4] {'ctx'}, use_global_device_ids=true, to_apply=%add | all-reduce | flops 16 | bytes 128
  34.6 12.0 %all-reduce.1 = bf16[64]{0:T(256)(128)(2,1)S(1)} all-reduce(bf16[64]{0:T(256)(128)(2,1)S(1)} %dynamic-update-slice.1), channel_id=4, replica_groups=mesh['ctx'=8,'head'=4] {'ctx'}, use_global_device_ids=true, to_apply=%add.1 | all-reduce | flops 64 | bytes 256
  46.7 7.9 %all-gather.4 = s32[8,1,384]{2,1,0:T(1,128)S(1)} all-gather(s32[1,1,384]{2,1,0:T(1,128)S(1)} %reshape.217), channel_id=1, replica_groups=mesh['ctx'=8,'head'=4] {'ctx'}, dimensions={0}, use_global_device_ids=true | all-gather | bytes 13824 | tf_op jit(solution)/shard_map/all_gather | solution.py:108
  54.7 2.9 %fusion.38 = f32[8,384,384]{2,1,0:T(8,128)} fusion(bf16[384,8,128]{0,2,1:T(8,128)(2,1)S(1)} %bitcast.93, bf16[384,1024]{1,0:T(8,128)(2,1)S(1)} %copy-done.2), kind=kOutput, calls=%fused_computation.42 | convolution fusion | flops 301989888 | bytes 6291456 | tf_op jit(solution)/shard_map/thd,shd->hts/dot_general | solution.py:62
  57.6 1.3 fusion.14
  59.1 1.0 fusion.36
  60.1 7.9 %multiply_reduce_fusion = (f32[384]{0:T(512)S(1)}, f32[384,8,128]{0,2,1:T(8,128)}) fusion(f32[384,8]{0,1:T(8,128)S(1)} %select_bitcast_fusion, f32[8,128,384]{2,1,0:T(8,128)S(1)} %fusion.36, f32[8,384,384]{2,1,0:T(8,128)} %fusion.38, f32[8,384]{1,0:T(8,128)S(1)} %add_bitcast_fusion, pred[384,384]{1,0:T(8,128)(4,1)S(1)} %fusion.45, bf16[384,1024]{1,0:T(8,128)(2,1)} %param.13), kind=kOutput, calls=%fused_computation.30 | convolution fusion | flops 1818230400 | bytes 8824320 | tf_op jit(solution)/shard_map/hts,shd->thd/dot_general | solution.py:65
  68.0 1.9 %copy.55 = f32[384,1024]{1,0:T(8,128)S(1)} copy(f32[384,1024]{0,1:T(8,128)} %bitcast.94) | data formatting | bytes 3145728 | tf_op jit(solution)/shard_map/reshape | solution.py:86
  69.8 12.2 %psum.7 = f32[384]{0:T(512)S(1)} all-reduce(f32[384]{0:T(512)S(1)} %get-tuple-element.105), channel_id=1, replica_groups=mesh['ctx'=8,'head'=4] {'head'}, use_global_device_ids=true, to_apply=%region_5.6 | all-reduce | flops 384 | bytes 3072 | tf_op jit(solution)/shard_map/psum | solution.py:87
  82.0 1.1 multiply_convert_fusion
  83.1 15.8 %all-gather.9.cloned.1.call-done = bf16[3072,1024]{0,1:T(8,128)(2,1)} async-done(((bf16[384,1024]{0,1:T(8,128)(2,1)}), bf16[3072,1024]{0,1:T(8,128)(2,1)}) %all-gather.9.cloned.1.call-update) | async-done | bytes 6291472 | tf_op jit(solution)/shard_map/all_gather | solution.py:102
  98.9 18.4 %select_reduce_fusion = (f32[8,384]{1,0:T(8,128)S(1)}, f32[8,384,3072]{2,1,0:T(8,128)}) fusion(pred[384,3072]{1,0:T(8,128)(4,1)S(1)} %fusion.14, bf16[3072,8,128]{0,2,1:T(8,128)(2,1)} %bitcast.90, bf16[384,1024]{1,0:T(8,128)(2,1)S(1)} %copy-done), kind=kOutput, calls=%fused_computation.8 | convolution fusion | flops 2444227584 | bytes 46018560 | tf_op jit(solution)/shard_map/qhd,khd->hqk/dot_general | solution.py:112
  117.3 17.9 %fusion.3 = f32[8,384]{1,0:T(8,128)S(1)} fusion(f32[8,384,3072]{2,1,0:T(8,128)} %get-tuple-element.108, f32[8,384]{1,0:T(8,128)S(1)} %broadcast_maximum_fusion, pred[384,3072]{1,0:T(8,128)(4,1)S(1)} %fusion.14), kind=kLoop, calls=%fused_computation.9 | loop fusion | flops 37745664 | bytes 38952960 | tf_op jit(solution)/shard_map/reduce_sum | solution.py:122
  135.2 11.1 %all-gather.11.cloned.1.call-done = bf16[3072,1024]{1,0:T(8,128)(2,1)} async-done(((bf16[384,1024]{1,0:T(8,128)(2,1)}), bf16[3072,1024]{1,0:T(8,128)(2,1)}) %all-gather.11.cloned.1.call-update) | async-done | bytes 6291472 | tf_op jit(solution)/shard_map/all_gather | solution.py:126
  146.4 8.7 %copy.59 = bf16[3072,1024]{0,1:T(8,128)(2,1)} copy(bf16[3072,1024]{1,0:T(8,128)(2,1)} %all-gather.11.cloned.1.call-done) | data formatting | bytes 12582912 | tf_op jit(solution)/shard_map/all_gather | solution.py:126
  155.0 17.2 %fusion.19 = bf16[384,8,128]{0,2,1:T(8,128)(2,1)S(1)} fusion(bf16[3072,8,128]{0,2,1:T(8,128)(2,1)} %bitcast.91, f32[8,384,3072]{2,1,0:T(8,128)} %get-tuple-element.108, f32[8,384]{1,0:T(8,128)S(1)} %broadcast_maximum_fusion, pred[384,3072]{1,0:T(8,128)(4,1)S(1)} %fusion.14, f32[384,8]{0,1:T(8,128)S(1)} %bitcast.100), kind=kOutput, calls=%fused_computation.26 | convolution fusion | flops 2454454272 | bytes 46030848 | tf_op jit(solution)/shard_map/hqk,khd->hqd/dot_general | solution.py:123
  172.2 1.2 copy.60
  (38 shorter events, 2.9 us)
Async XLA Ops:
  7.2 91.7 %copy-start = (bf16[384,1024]{1,0:T(8,128)(2,1)S(1)}, bf16[384,1024]{1,0:T(8,128)(2,1)}, u32[]{:S(2)}) copy-start(bf16[384,1024]{1,0:T(8,128)(2,1)} %param.16) | copy-start | bytes 2359300
  7.2 14.8 %copy-start.3 = (s32[384]{0:T(512)S(1)}, s32[384]{0:T(512)}, u32[]{:S(2)}) copy-start(s32[384]{0:T(512)} %param.19) | copy-start | bytes 4612
  7.2 47.5 %copy-start.2 = (bf16[384,1024]{1,0:T(8,128)(2,1)S(1)}, bf16[384,1024]{1,0:T(8,128)(2,1)}, u32[]{:S(2)}) copy-start(bf16[384,1024]{1,0:T(8,128)(2,1)} %param.11) | copy-start | bytes 2359300
  7.2 51.8 %all-gather.13.cloned.1.call-start = ((), (), s32[]{:S(2)}) async-start(), calls=%async_computation.2 | async-start | bytes 2359296 | tf_op jit(solution)/shard_map/all_gather | solution.py:18
  18.9 80.0 %all-gather.9.cloned.1.call-start = ((), (), s32[]{:S(2)}) async-start(), calls=%async_computation | async-start | bytes 7077888 | tf_op jit(solution)/shard_map/all_gather | solution.py:102
  21.2 125.1 %all-gather.11.cloned.1.call-start = ((), (), s32[]{:S(2)}) async-start(), calls=%async_computation.1 | async-start | bytes 7077888 | tf_op jit(solution)/shard_map/all_gather | solution.py:126
  60.1 21.9 %copy-start.4 = (f32[1024]{0:T(1024)S(1)}, f32[1024]{0:T(1024)}, u32[]{:S(2)}) copy-start(f32[1024]{0:T(1024)} %param.15) | copy-start | bytes 12292
  155.0 18.4 %copy-start.1 = (bf16[384,1024]{1,0:T(8,128)(2,1)S(1)}, bf16[384,1024]{1,0:T(8,128)(2,1)}, u32[]{:S(2)}) copy-start(bf16[384,1024]{1,0:T(8,128)(2,1)} %param.16) | copy-start | bytes 2359300
Sparse Core Ops, SparseCore 0:
  19.0 30.6 all-gather.12
  52.2 46.6 all-gather.8
  100.8 45.5 all-gather.10
where the time goes:
time: 181 us; the launch traced here: 180 us
  matrix products  50.2 us (28%)
  blocking collectives  41.5 us (23%)
  waiting for transfers between devices  27.7 us (15%)
  other arithmetic  24.1 us (13%)
  local copies, waits for them, and re-layouts  20.5 us (11%)
  between operations  15.8 us (9%)
    unnamed x2, blocking collectives  21.5 us
    dot_general x1, matrix products, soft_core(): jnp.einsum('qhd,khd->hqk', queries, key_piece.reshape(piece_rows, head_co...  18.4 us
    reduce_sum x1, other arithmetic, soft_core(): new_total = jnp.sum(weights, axis=2)  17.9 us
    dot_general x1, matrix products, soft_core(): jnp.einsum('hqk,khd->hqd', weights.astype(jnp.bfloat16), lax.all_gather(v...  17.2 us
    all_gather x1, waiting for transfers between devices, soft_core(): key_piece = lax.all_gather(k_soft, 'ctx', axis=0, tiled=True)  15.8 us
    psum x1, blocking collectives, linear_core(): square_sum = lax.psum(jnp.sum(raw_output * raw_output, axis=1), 'head')  12.2 us
    all_gather x1, waiting for transfers between devices, soft_core(): lax.all_gather(v_soft, 'ctx', axis=0, tiled=True)  11.1 us
    all_gather x1, local copies, waits for them, and re-layouts, soft_core(): lax.all_gather(v_soft, 'ctx', axis=0, tiled=True)  8.66 us
  transfers between devices with their start and end apart: 3, of which 2 were waited for; matrix products, arithmetic and copies ran while one was open for 31% of the time, Pallas kernels for 0%

commit v1 on v0

v1 whole, which is shorter than its diff:
```python
import functools
import math

import jax
import jax.numpy as jnp
from jax import lax
from jax.experimental import pallas as pl
from jax.experimental.pallas import tpu as pltpu
from jax.sharding import PartitionSpec as P

EPSILON = 1e-05
MASKED = -1e30
LANES = 128
META = 16
TILE = 256
F32 = jnp.float32
BF16 = jnp.bfloat16
HIGHEST = lax.Precision.HIGHEST
VMEM_LIMIT = 48 << 20


def nt_dot(a, b, precision=None):
    return lax.dot_general(
        a, b, (((1,), (1,)), ((), ())), precision=precision, preferred_element_type=F32
    )


def column_of(row):
    return jnp.transpose(jnp.broadcast_to(row, (LANES, LANES)))


def cumulate(gates):
    rows = gates.shape[1]
    upper = lax.broadcasted_iota(jnp.int32, (rows, rows), 0) <= lax.broadcasted_iota(
        jnp.int32, (rows, rows), 1
    )
    return jnp.dot(gates, jnp.where(upper, 1.0, 0.0), precision=HIGHEST, preferred_element_type=F32)


def pack_kernel(q_ref, k_ref, v_ref, doc_ref, out_ref):
    rows = q_ref.shape[0]
    out_ref[0, 0:rows] = q_ref[...]
    out_ref[0, rows : 2 * rows] = k_ref[...]
    out_ref[0, 2 * rows : 3 * rows] = v_ref[...]
    doc = doc_ref[...].astype(F32)
    line = lax.broadcasted_iota(jnp.int32, (META, LANES), 0)
    block = jnp.zeros((META, LANES), F32)
    for i in range(rows // LANES):
        block = jnp.where(line == i, doc[:, i * LANES : (i + 1) * LANES], block)
    out_ref[0, 3 * rows : 3 * rows + META] = block.astype(BF16)


def pack(q, k, v, doc_row, heads):
    rows = q.shape[0]
    total = 3 * rows + META
    block = pl.BlockSpec((rows, LANES), lambda h: (0, h))
    return pl.pallas_call(
        pack_kernel,
        grid=(heads,),
        in_specs=[block, block, block, pl.BlockSpec((1, rows), lambda h: (0, 0))],
        out_specs=pl.BlockSpec((1, total, LANES), lambda h: (h, 0, 0)),
        out_shape=jax.ShapeDtypeStruct((heads, total, LANES), BF16),
        cost_estimate=pl.CostEstimate(
            flops=0, bytes_accessed=4 * heads * total * LANES, transcendentals=0
        ),
        name="pack",
    )(q, k, v, doc_row)


def attend_kernel(rows, window, x_ref, o_ref, s_ref):
    parts = x_ref.shape[0]
    tokens = parts * rows
    per = rows // LANES
    factor = LANES ** (-0.5) * math.log2(math.e)
    docs = x_ref[:, 3 * rows : 3 * rows + META, :].astype(F32)
    used = lax.broadcasted_iota(jnp.int32, docs.shape, 1) < per
    starts = [
        jnp.sum(jnp.where(used & (docs < d), 1, 0).astype(jnp.int32)) for d in range(1, 8)
    ]

    def chunk(which, g):
        offset = pl.multiple_of(which * rows + (g % per) * LANES, LANES)
        return x_ref[g // per, pl.ds(offset, LANES), :]

    def tile(which, t):
        n = TILE // LANES
        return jnp.concatenate([chunk(which, t * n + j) for j in range(n)], axis=0)

    wide = (TILE, LANES)
    ones = jnp.ones(wide, BF16)
    lane = lax.broadcasted_iota(jnp.int32, wide, 1)
    sub = lax.broadcasted_iota(jnp.int32, wide, 0)

    def body(i, carry):
        first = i * TILE
        queries = tile(0, i)
        qpos = first + sub
        begin = jnp.zeros(wide, jnp.int32)
        low = 0
        for s in starts:
            begin = jnp.where(qpos >= s, s, begin)
            low = jnp.where(first >= s, s, low)
        count = i - low // TILE + 1

        def run(n):
            top = jnp.full(wide, MASKED, F32)
            for j in range(n):
                t = i - (n - 1) + j
                s = nt_dot(queries, tile(1, t))
                pieces = []
                for c in range(TILE // LANES):
                    kpos = t * TILE + c * LANES + lane
                    ok = kpos >= begin
                    if j == n - 1:
                        ok = ok & (kpos <= qpos)
                    piece = jnp.where(ok, s[:, c * LANES : (c + 1) * LANES], MASKED)
                    top = jnp.maximum(top, piece)
                    pieces.append(piece)
                s_ref[j] = jnp.concatenate(pieces, axis=1)
            row_max = jnp.max(top, axis=1, keepdims=True)
            total = jnp.zeros((TILE, 2 * LANES), F32)
            for j in range(n):
                t = i - (n - 1) + j
                w = jnp.exp2((s_ref[j] - row_max) * factor).astype(BF16)
                total += jnp.dot(
                    w, jnp.concatenate([tile(2, t), ones], axis=1), preferred_element_type=F32
                )
            o_ref[pl.ds(pl.multiple_of(first, TILE), TILE), :] = (
                total[:, :LANES] / total[:, LANES:]
            ).astype(BF16)

        for n in range(1, window + 1):
            pl.when(count == n)(functools.partial(run, n))
        return carry

    lax.fori_loop(0, tokens // TILE, body, 0)


def attend(x, rows, longest):
    parts, total, _ = x.shape
    tokens = parts * rows
    window = min((longest - 1 + TILE - 1) // TILE + 1, tokens // TILE)
    return pl.pallas_call(
        functools.partial(attend_kernel, rows, window),
        in_specs=[pl.BlockSpec(memory_space=pltpu.VMEM)],
        out_specs=pl.BlockSpec(memory_space=pltpu.VMEM),
        out_shape=jax.ShapeDtypeStruct((tokens, LANES), BF16),
        scratch_shapes=[pltpu.VMEM((window, TILE, TILE), F32)],
        cost_estimate=pl.CostEstimate(
            flops=2 * tokens * longest * LANES * 2,
            bytes_accessed=2 * (x.size + tokens * LANES),
            transcendentals=tokens * longest,
        ),
        compiler_params=pltpu.CompilerParams(vmem_limit_bytes=VMEM_LIMIT),
        name="attend",
    )(x)


def attend_gathered(q, k, v, doc_ids, heads):
    rows = q.shape[0]
    keys = lax.all_gather(k, "ctx", axis=0, tiled=True)
    values = lax.all_gather(v, "ctx", axis=0, tiled=True)
    docs = lax.all_gather(doc_ids, "ctx", axis=0, tiled=True)
    position = lax.axis_index("ctx") * rows + jnp.arange(rows)
    allowed = (jnp.arange(docs.shape[0])[None, :] <= position[:, None]) & (
        docs[None, :] == doc_ids[:, None]
    )

    def one(h):
        queries, head_keys, head_values = (
            lax.dynamic_slice_in_dim(a, h * LANES, LANES, 1) for a in (q, keys, values)
        )
        scores = jnp.where(allowed, nt_dot(queries, head_keys) * LANES ** (-0.5), MASKED)
        weights = jnp.exp(scores - jnp.max(scores, axis=1, keepdims=True))
        mixed = jnp.dot(weights.astype(BF16), head_values, preferred_element_type=F32)
        return (mixed / jnp.sum(weights, axis=1, keepdims=True)).astype(BF16)

    return lax.map(one, jnp.arange(heads)).transpose(1, 0, 2).reshape(rows, heads * LANES)


def meta_block(first, last, factors):
    line = lax.broadcasted_iota(jnp.int32, (META, LANES), 0)
    block = jnp.zeros((META, LANES), F32)
    n = len(factors)
    for i, f in enumerate(factors):
        high = f.astype(BF16).astype(F32)
        block = jnp.where(line == i, high, block)
        block = jnp.where(line == n + i, f - high, block)
    block = jnp.where(line == 2 * n, first, block)
    block = jnp.where(line == 2 * n + 1, last, block)
    return block.astype(BF16)


def read_meta(ref, n):
    block = ref[n * LANES : n * LANES + META, :].astype(F32)
    factors = [block[i : i + 1] + block[n + i : n + i + 1] for i in range(n)]
    return block[2 * n : 2 * n + 1], block[2 * n + 1 : 2 * n + 2], factors


def local_state_kernel(half, core_ref, gate_ref, doc_ref, k_ref, v_ref, mine_ref, other_ref, w_ref, f_ref):
    i = pl.program_id(0)
    rows = k_ref.shape[0]
    core = core_ref[0]

    @pl.when(i == 0)
    def _():
        cumulated = cumulate(gate_ref[...])
        last = cumulated[:, rows - 1 : rows]
        doc = doc_ref[...]
        end = doc[:, rows - 1 : rows]
        w_ref[...] = jnp.where(doc == end, jnp.exp(last - cumulated), 0.0)
        whole = jnp.where(doc[:, 0:1] == end, 1.0, 0.0)
        f_ref[...] = jnp.broadcast_to(jnp.exp(last) * whole, f_ref.shape)
        first_doc = jnp.broadcast_to(doc[:, 0:1].astype(F32), (1, LANES))
        last_doc = jnp.broadcast_to(end.astype(F32), (1, LANES))
        for ref, base in ((mine_ref, core * half), (other_ref, (1 - core) * half)):
            factors = [f_ref[pl.ds(base + j, 1), :] for j in range(half)]
            ref[half * LANES : half * LANES + META, :] = meta_block(first_doc, last_doc, factors)

    head = lax.rem(core * half + i, 2 * half)
    weighted = jnp.transpose(k_ref[...].astype(F32)) * w_ref[pl.ds(head, 1), :]
    state = jnp.dot(weighted.astype(BF16), v_ref[...], preferred_element_type=F32).astype(BF16)
    place = pl.ds(pl.multiple_of(lax.rem(i, half) * LANES, LANES), LANES)

    @pl.when(i < half)
    def _():
        mine_ref[place, :] = state

    @pl.when(i >= half)
    def _():
        other_ref[place, :] = state


def local_state(k, v, gates, doc_row, core, heads):
    rows = k.shape[0]
    half = heads // 2
    block = pl.BlockSpec((rows, LANES), lambda i, c: (0, lax.rem(c[0] * half + i, heads)))
    fixed = lambda i, c: (0, 0)
    sent = (half * LANES + META, LANES)
    return pl.pallas_call(
        functools.partial(local_state_kernel, half),
        grid_spec=pltpu.PrefetchScalarGridSpec(
            num_scalar_prefetch=1,
            grid=(heads,),
            in_specs=[
                pl.BlockSpec((heads, rows), fixed),
                pl.BlockSpec((1, rows), fixed),
                block,
                block,
            ],
            out_specs=[pl.BlockSpec(sent, fixed), pl.BlockSpec(sent, fixed)],
            scratch_shapes=[pltpu.VMEM((heads, rows), F32), pltpu.VMEM((heads, LANES), F32)],
        ),
        out_shape=[jax.ShapeDtypeStruct(sent, BF16)] * 2,
        cost_estimate=pl.CostEstimate(
            flops=2 * heads * rows * LANES * LANES,
            bytes_accessed=4 * heads * rows * LANES + 4 * heads * LANES * LANES,
            transcendentals=heads * rows,
        ),
        name="local_state",
    )(core, gates, doc_row, k, v)


def join(n, early, late, out_ref):
    early_first, early_last, early_factor = read_meta(early, n)
    late_first, late_last, late_factor = read_meta(late, n)
    linked = (early_last == late_first) | (early_last < 0) | (late_first < 0)
    link = jnp.where(linked, 1.0, 0.0)
    first = jnp.where(early_first < 0, late_first, early_first)
    last = jnp.where(late_last < 0, early_last, late_last)
    for i in range(n):
        at = slice(i * LANES, (i + 1) * LANES)
        out_ref[at, :] = (
            late[at, :].astype(F32) + (late_factor[i] * link) * early[at, :].astype(F32)
        ).astype(BF16)
    factors = [early_factor[i] * late_factor[i] * link for i in range(n)]
    out_ref[n * LANES : n * LANES + META, :] = meta_block(first, last, factors)


def set_neutral(n, ref):
    ref[0 : n * LANES, :] = jnp.zeros((n * LANES, LANES), BF16)
    away = jnp.full((1, LANES), -1.0, F32)
    ref[n * LANES : n * LANES + META, :] = meta_block(away, away, [jnp.ones((1, LANES), F32)] * n)


def join_pair_kernel(n, flag_ref, mine_ref, came_ref, out_ref):
    @pl.when(flag_ref[0] == 0)
    def _():
        join(n, mine_ref, came_ref, out_ref)

    @pl.when(flag_ref[0] != 0)
    def _():
        join(n, came_ref, mine_ref, out_ref)


def join_pair(mine, came, flag, n):
    return pl.pallas_call(
        functools.partial(join_pair_kernel, n),
        in_specs=[pl.BlockSpec(memory_space=pltpu.SMEM)]
        + [pl.BlockSpec(memory_space=pltpu.VMEM)] * 2,
        out_specs=pl.BlockSpec(memory_space=pltpu.VMEM),
        out_shape=jax.ShapeDtypeStruct(mine.shape, BF16),
        cost_estimate=pl.CostEstimate(
            flops=2 * mine.size, bytes_accessed=6 * mine.size, transcendentals=0
        ),
        name="join_pair",
    )(flag, mine, came)


def before_kernel(n, bits, flag_ref, mine_ref, mate_ref, *refs):
    came, (keep_ref, send_ref), (a_ref, b_ref) = refs[:bits], refs[bits : bits + 2], refs[bits + 2 :]
    set_neutral(n, a_ref)
    now, spare = a_ref, b_ref
    for b in range(bits):
        late = flag_ref[b + 1] != 0

        def put(source=now, target=spare):
            target[...] = source[...]

        def add(other=came[b], source=now, target=spare):
            join(n, other, source, target)

        pl.when(late)(add)
        pl.when(jnp.logical_not(late))(put)
        now, spare = spare, now

    @pl.when(flag_ref[0] == 0)
    def _():
        keep_ref[...] = now[...]
        join(n, now, mine_ref, send_ref)

    @pl.when(flag_ref[0] != 0)
    def _():
        join(n, now, mate_ref, keep_ref)
        send_ref[...] = now[...]


def before(mine, mate, came, flags, n):
    return pl.pallas_call(
        functools.partial(before_kernel, n, len(came)),
        in_specs=[pl.BlockSpec(memory_space=pltpu.SMEM)]
        + [pl.BlockSpec(memory_space=pltpu.VMEM)] * (2 + len(came)),
        out_specs=[pl.BlockSpec(memory_space=pltpu.VMEM)] * 2,
        out_shape=[jax.ShapeDtypeStruct(mine.shape, BF16)] * 2,
        scratch_shapes=[pltpu.VMEM(mine.shape, BF16)] * 2,
        cost_estimate=pl.CostEstimate(
            flops=4 * mine.size, bytes_accessed=12 * mine.size, transcendentals=0
        ),
        name="before",
    )(flags, mine, mate, *came)


def carried_in(mine, other, place, size, n):
    def swap(x, bit):
        return lax.ppermute(x, "ctx", [(i, i ^ (1 << bit)) for i in range(size)])

    bits = size.bit_length() - 1
    flags = (place >> jnp.arange(bits)) & 1
    mate = swap(other, 0)
    block = join_pair(mine, mate, flags[0:1], n)
    came = []
    for b in range(1, bits):
        came.append(swap(block, b))
        if b < bits - 1:
            block = join_pair(block, came[-1], flags[b : b + 1], n)
    keep, send = before(mine, mate, came, flags, n)
    return keep, swap(send, 0)


def linear_kernel(half, core_ref, gate_ref, doc_ref, q_ref, k_ref, v_ref, keep_ref, came_ref, raw_ref, square_ref, cum_ref, bias_ref, doc_col_ref, sum_ref):
    h = pl.program_id(0)
    rows = q_ref.shape[0]
    count = rows // LANES

    @pl.when(h == 0)
    def _():
        cum_ref[...] = cumulate(gate_ref[...])
        doc = doc_ref[...].astype(F32)
        for a in range(count):
            column = column_of(doc[:, a * LANES : (a + 1) * LANES])
            doc_col_ref[a * LANES : (a + 1) * LANES, :] = column
            for b in range(a + 1):
                ok = column == doc[:, b * LANES : (b + 1) * LANES]
                if a == b:
                    ok = ok & (
                        lax.broadcasted_iota(jnp.int32, (LANES, LANES), 0)
                        >= lax.broadcasted_iota(jnp.int32, (LANES, LANES), 1)
                    )
                bias_ref[a * LANES : (a + 1) * LANES, b * LANES : (b + 1) * LANES] = jnp.where(
                    ok, 0.0, MASKED
                )
        sum_ref[...] = jnp.zeros_like(sum_ref)

    row = cum_ref[pl.ds(h, 1), :]
    own = (h // half) == core_ref[0]
    place = pl.ds(pl.multiple_of(lax.rem(h, half) * LANES, LANES), LANES)
    state = jnp.where(own, keep_ref[place, :].astype(F32), came_ref[place, :].astype(F32)).astype(BF16)
    _, before_doc, _ = read_meta(keep_ref, half)
    for a in range(count):
        at = slice(a * LANES, (a + 1) * LANES)
        width = (a + 1) * LANES
        column = column_of(row[:, at])
        q = q_ref[at, :]
        scores = nt_dot(q, k_ref[0:width, :])
        decay = jnp.concatenate(
            [
                jnp.exp(
                    jnp.minimum(column - row[:, b * LANES : (b + 1) * LANES], 0.0)
                    + bias_ref[at, b * LANES : (b + 1) * LANES]
                )
                for b in range(a + 1)
            ],
            axis=1,
        )
        raw = jnp.dot((scores * decay).astype(BF16), v_ref[0:width, :], preferred_element_type=F32)
        carried = jnp.where(doc_col_ref[at, :] == before_doc, jnp.exp(column), 0.0)
        raw = raw + jnp.dot(q, state, preferred_element_type=F32) * carried
        raw_ref[at, :] = raw
        sum_ref[at, :] += raw * raw

    @pl.when(h == pl.num_programs(0) - 1)
    def _():
        square_ref[...] = nt_dot(jnp.ones((8, LANES), F32), sum_ref[...], HIGHEST)


def linear(q, k, v, gates, doc_row, keep, came, core, heads):
    rows = q.shape[0]
    half = heads // 2
    block = pl.BlockSpec((rows, LANES), lambda h, c: (0, h))
    fixed = lambda h, c: (0, 0)
    return pl.pallas_call(
        functools.partial(linear_kernel, half),
        grid_spec=pltpu.PrefetchScalarGridSpec(
            num_scalar_prefetch=1,
            grid=(heads,),
            in_specs=[
                pl.BlockSpec((heads, rows), fixed),
                pl.BlockSpec((1, rows), fixed),
                block,
                block,
                block,
                pl.BlockSpec(keep.shape, fixed),
                pl.BlockSpec(came.shape, fixed),
            ],
            out_specs=[block, pl.BlockSpec((8, rows), fixed)],
            scratch_shapes=[
                pltpu.VMEM((heads, rows), F32),
                pltpu.VMEM((rows, rows), F32),
                pltpu.VMEM((rows, LANES), F32),
                pltpu.VMEM((rows, LANES), F32),
            ],
        ),
        out_shape=[
            jax.ShapeDtypeStruct((rows, heads * LANES), F32),
            jax.ShapeDtypeStruct((8, rows), F32),
        ],
        cost_estimate=pl.CostEstimate(
            flops=4 * heads * rows * rows * LANES,
            bytes_accessed=10 * heads * rows * LANES,
            transcendentals=heads * rows * rows,
        ),
        name="linear",
    )(core, gates, doc_row, q, k, v, keep, came)


def on_device(size, head_parts, q_lin, k_lin, v_lin, gate_log, lin_gain, q_soft, k_soft, v_soft, doc_ids):
    heads, rows = gate_log.shape
    place = lax.axis_index("ctx")
    core = (place & 1)[None]
    doc_row = doc_ids.reshape(1, rows)

    whole_heads = heads == size
    if whole_heads:
        sent = pack(q_soft, k_soft, v_soft, doc_row, heads)
        held = lax.all_to_all(sent, "ctx", split_axis=0, concat_axis=0, tiled=True)

    mine, other = local_state(k_lin, v_lin, gate_log, doc_row, core, heads)
    keep, came = carried_in(mine, other, place, size, heads // 2)
    raw, square = linear(q_lin, k_lin, v_lin, gate_log, doc_row, keep, came, core, heads)

    if whole_heads:
        mixed = attend(held, rows, rows * size // 2)
        mixed = lax.all_to_all(
            mixed.reshape(size, rows, LANES), "ctx", split_axis=0, concat_axis=0, tiled=True
        )
        soft_out = mixed.transpose(1, 0, 2).reshape(rows, heads * LANES)
    else:
        soft_out = attend_gathered(q_soft, k_soft, v_soft, doc_ids, heads)

    own = square[0]
    total = own
    for d in range(1, head_parts):
        total = total + lax.ppermute(own, "head", [(i, (i + d) % head_parts) for i in range(head_parts)])
    scale = lax.rsqrt(total / (heads * head_parts * LANES) + EPSILON)
    lin_out = (raw * scale[:, None] * lin_gain[None, :]).astype(BF16)
    return lin_out, soft_out


def solution(mesh):
    split = P("ctx", "head")
    in_specs = (split, split, split, P("head", "ctx"), P("head"), split, split, split, P("ctx"))
    return jax.shard_map(
        functools.partial(on_device, mesh.shape["ctx"], mesh.shape["head"]),
        mesh=mesh,
        in_specs=in_specs,
        out_specs=(split, split),
        check_vma=False,
    )
```

time: 181 us -> 94 us (0.52)
  matrix products: 50.2 us -> 0 us
  blocking collectives: 41.5 us -> 0 us
  Pallas kernels: 0 us -> 38.4 us
  other arithmetic: 24.1 us -> 2.5 us
  starting transfers between devices: 0.12 us -> 17.2 us
  between operations: 15.8 us -> 0.69 us
  local copies, waits for them, and re-layouts: 20.5 us -> 6.1 us
    dot_general x6 -> x0, matrix products: 50.2 us -> none  [the longest x1 18.4 us: soft_core(): jnp.einsum('qhd,khd->hqk', queries, key_piece.reshape(piece_rows, head_co...]
    pallas_call x0 -> x7, Pallas kernels: none -> 38.4 us  [the longest x1 11.3 us: attend(): pl.pallas_call(functools.partial(attend_kernel, rows, window), in_specs=[...]
    ppermute x0 -> x7, waiting for transfers between devices: none -> 27.9 us  [the longest x4 23.5 us: swap(): return lax.ppermute(x, 'ctx', [(i, i ^ 1 << bit) for i in range(size)])]
    all_gather x3 -> x0, waiting for transfers between devices: 26.9 us -> none  [the longest x1 15.8 us: soft_core(): key_piece = lax.all_gather(k_soft, 'ctx', axis=0, tiled=True)]
    unnamed x2 -> x0, blocking collectives: 21.5 us -> none
    reduce_sum x1 -> x0, other arithmetic: 17.9 us -> none  [soft_core(): new_total = jnp.sum(weights, axis=2)]
    psum x1 -> x0, blocking collectives: 12.2 us -> none  [linear_core(): square_sum = lax.psum(jnp.sum(raw_output * raw_output, axis=1), 'head')]
    all_gather x2 -> x0, local copies, waits for them, and re-layouts: 8.75 us -> none  [the longest x1 8.66 us: soft_core(): lax.all_gather(v_soft, 'ctx', axis=0, tiled=True)]
  transfers between devices with their start and end apart: 3 -> 9, of which waited for: 2 -> 6; matrix products, arithmetic and copies ran while one was open for 31% -> 4% of each run, Pallas kernels for 0% -> 35%
where the time goes in v1:
time: 94 us; the launch traced here: 92.8 us
  Pallas kernels  38.4 us (41%)
  waiting for transfers between devices  27.9 us (30%)
  starting transfers between devices  17.2 us (18%)
  local copies, waits for them, and re-layouts  6.1 us (6%)
  other arithmetic  2.5 us (3%)
    ppermute x4, waiting for transfers between devices, swap(): return lax.ppermute(x, 'ctx', [(i, i ^ 1 << bit) for i in range(size)])  23.5 us
    pallas_call x1, Pallas kernels, attend(): pl.pallas_call(functools.partial(attend_kernel, rows, window), in_specs=[...  11.3 us
    pallas_call x1, Pallas kernels, linear(): pl.pallas_call(functools.partial(linear_kernel, half), grid_spec=pltpu.Pr...  8.44 us
    pallas_call x1, Pallas kernels, local_state(): pl.pallas_call(functools.partial(local_state_kernel, half), grid_spec=plt...  6.24 us
    pallas_call x1, Pallas kernels, pack(): pl.pallas_call(pack_kernel, grid=(heads,), in_specs=[block, block, block,...  5.95 us
    all_to_all x1, starting transfers between devices, on_device(): held = lax.all_to_all(sent, 'ctx', split_axis=0, concat_axis=0, tiled=True)  5.17 us
    ppermute x3, starting transfers between devices, on_device(): lax.ppermute(own, 'head', [(i, (i + d) % head_parts) for i in range(head_...  4.66 us
    pallas_call x2, Pallas kernels, join_pair(): pl.pallas_call(functools.partial(join_pair_kernel, n), in_specs=[pl.Block...  4.54 us
  transfers between devices with their start and end apart: 9, of which 6 were waited for; matrix products, arithmetic and copies ran while one was open for 4% of the time, Pallas kernels for 35%

profile of v1, /device:TPU:0, one launch (start us, length us, event | category | flops | bytes accessed | tf_op | source)
XLA Modules:
  0.0 92.8 jit_solution(6261191217845812244)
XLA Ops:
  0.6 1.2 %reshape.15.doc_ref = s32[1,384]{1,0:T(1,128)} reshape(s32[384]{0:T(512)} %param.17) | data formatting | bytes 3072 | tf_op jit(solution)/shard_map/reshape | solution.py:470
  1.8 5.9 %pack.1 = bf16[8,1168,128]{2,1,0:T(8,128)(2,1)} custom-call(bf16[384,1024]{1,0:T(8,128)(2,1)} %q_ref.3, bf16[384,1024]{1,0:T(8,128)(2,1)} %k_ref.5, bf16[384,1024]{1,0:T(8,128)(2,1)} %v_ref.5, s32[1,384]{1,0:T(1,128)} %reshape.15.doc_ref), custom_call_target="tpu_custom_call" | custom-call | bytes 4784128 | tf_op jit(solution)/shard_map/pack/pallas_call | solution.py:57
  7.8 5.2 %all-to-all-start = ((bf16[8,1168,128]{2,1,0:T(8,128)(2,1)}), bf16[8,1168,128]{2,1,0:T(8,128)(2,1)S(1)}, u32[]{:S(2)}, u32[]{:S(2)}) async-start(bf16[8,1168,128]{2,1,0:T(8,128)(2,1)} %pack.1), calls=%async_computation | async-start | bytes 4784128 | tf_op jit(solution)/shard_map/all_to_all | solution.py:475
  13.0 6.2 %local_state.1 = (bf16[528,128]{1,0:T(8,128)(2,1)}, bf16[528,128]{1,0:T(8,128)(2,1)}) custom-call(s32[1]{0:T(128)} %bitcast.core_ref, f32[8,384]{1,0:T(8,128)} %gate_ref.3, s32[1,384]{1,0:T(1,128)} %reshape.15.doc_ref, bf16[384,1024]{1,0:T(8,128)(2,1)} %k_ref.4, bf16[384,1024]{1,0:T(8,128)(2,1)} %v_ref.4), custom_call_target="tpu_custom_call" | custom-call | flops 100663296 | bytes 2097152 | tf_op jit(solution)/shard_map/local_state/pallas_call | solution.py:240
  20.9 0.7 copy-done
  21.6 2.3 %join_pair.2.mine_ref = bf16[528,128]{1,0:T(8,128)(2,1)} custom-call(s32[1]{0:T(128)} %get-tuple-element.15.flag_ref, bf16[528,128]{1,0:T(8,128)(2,1)} %get-tuple-element.8.mine_ref, bf16[528,128]{1,0:T(8,128)(2,1)} %copy-done), custom_call_target="tpu_custom_call" | custom-call | flops 135168 | bytes 405504 | tf_op jit(solution)/shard_map/join_pair/pallas_call | solution.py:297
  23.9 1.9 %collective-permute-start.1 = (bf16[528,128]{1,0:T(8,128)(2,1)}, bf16[528,128]{1,0:T(8,128)(2,1)S(1)}, u32[]{:S(2)}, u32[]{:S(2)}) collective-permute-start(bf16[528,128]{1,0:T(8,128)(2,1)} %join_pair.2.mine_ref), channel_id=1, source_target_pairs={{0,8},{4,12},{8,0},{12,4},{16,24},{20,28},{24,16},{28,20},{1,9},{5... | collective-permute-start | bytes 405512 | tf_op jit(solution)/shard_map/ppermute | solution.py:355
  25.7 19.0 %collective-permute-done.1.came_ref.refs_0_ = bf16[528,128]{1,0:T(8,128)(2,1)S(1)} collective-permute-done((bf16[528,128]{1,0:T(8,128)(2,1)}, bf16[528,128]{1,0:T(8,128)(2,1)S(1)}, u32[]{:S(2)}, u32[]{:S(2)}) %collective-permute-start.1) | collective-permute-done | bytes 135200 | tf_op jit(solution)/shard_map/ppermute | solution.py:355
  44.8 0.6 copy-done.1
  45.4 2.2 %join_pair.3 = bf16[528,128]{1,0:T(8,128)(2,1)} custom-call(s32[1]{0:T(128)} %get-tuple-element.14.flag_ref, bf16[528,128]{1,0:T(8,128)(2,1)} %join_pair.2.mine_ref, bf16[528,128]{1,0:T(8,128)(2,1)} %copy-done.1), custom_call_target="tpu_custom_call" | custom-call | flops 135168 | bytes 405504 | tf_op jit(solution)/shard_map/join_pair/pallas_call | solution.py:297
  47.6 1.5 %collective-permute-start.2 = (bf16[528,128]{1,0:T(8,128)(2,1)}, bf16[528,128]{1,0:T(8,128)(2,1)S(1)}, u32[]{:S(2)}, u32[]{:S(2)}) collective-permute-start(bf16[528,128]{1,0:T(8,128)(2,1)} %join_pair.3), channel_id=1, source_target_pairs={{0,16},{4,20},{8,24},{12,28},{16,0},{20,4},{24,8},{28,12},{1,17},{... | collective-permute-start | bytes 405512 | tf_op jit(solution)/shard_map/ppermute | solution.py:355
  49.1 3.9 %collective-permute-done.2.refs_1_ = bf16[528,128]{1,0:T(8,128)(2,1)S(1)} collective-permute-done((bf16[528,128]{1,0:T(8,128)(2,1)}, bf16[528,128]{1,0:T(8,128)(2,1)S(1)}, u32[]{:S(2)}, u32[]{:S(2)}) %collective-permute-start.2) | collective-permute-done | bytes 135200 | tf_op jit(solution)/shard_map/ppermute | solution.py:355
  53.6 2.0 %before.1 = (bf16[528,128]{1,0:T(8,128)(2,1)}, bf16[528,128]{1,0:T(8,128)(2,1)}) custom-call(s32[3]{0:T(128)} %copy-done.4, bf16[528,128]{1,0:T(8,128)(2,1)} %get-tuple-element.8.mine_ref, bf16[528,128]{1,0:T(8,128)(2,1)} %copy-done, bf16[528,128]{1,0:T(8,128)(2,1)} %copy-done.1, bf16[528,128]{1,0:T(8,128)(2,1)} %copy-done.3), custom_call_target="tpu_custom_call" | custom-call | flops 270336 | bytes 811008 | tf_op jit(solution)/shard_map/before/pallas_call | solution.py:339
  55.6 11.3 %attend.1 = bf16[3072,128]{1,0:T(8,128)(2,1)} custom-call(bf16[8,1168,128]{2,1,0:T(8,128)(2,1)S(1)} %all-to-all-done.x_ref), custom_call_target="tpu_custom_call" | custom-call | flops 2415919104 | bytes 3178496 | tf_op jit(solution)/shard_map/attend/pallas_call | solution.py:143
  66.9 3.5 %all-to-all-start.1 = ((bf16[8,384,128]{2,1,0:T(8,128)(2,1)}), bf16[8,384,128]{2,1,0:T(8,128)(2,1)S(1)}, u32[]{:S(2)}, u32[]{:S(2)}) async-start(bf16[8,384,128]{2,1,0:T(8,128)(2,1)} %bitcast.1), calls=%async_computation.1 | async-start | bytes 1572864 | tf_op jit(solution)/shard_map/all_to_all | solution.py:483
  70.5 0.6 copy-done.2
  71.1 8.4 %linear.1 = (f32[384,1024]{1,0:T(8,128)}, f32[8,384]{1,0:T(8,128)}) custom-call(s32[1]{0:T(128)} %bitcast.core_ref, f32[8,384]{1,0:T(8,128)} %gate_ref.3, s32[1,384]{1,0:T(1,128)} %reshape.15.doc_ref, bf16[384,1024]{1,0:T(8,128)(2,1)} %q_ref.2, bf16[384,1024]{1,0:T(8,128)(2,1)} %k_ref.4, bf16[384,1024]{1,0:T(8,128)(2,1)} %v_ref.4, ...), custom_call_target="tpu_custom_call" | custom-call | flops 603979776 | bytes 3932160 | tf_op jit(solution)/shard_map/linear/pallas_call | solution.py:431
  79.5 0.7 slice_reduce_fusion
  80.3 3.7 %collective-permute-start.6 = (f32[384]{0:T(512)S(1)}, f32[384]{0:T(512)S(1)}, u32[]{:S(2)}, u32[]{:S(2)}) collective-permute-start(f32[384]{0:T(512)S(1)} %slice_reduce_fusion), channel_id=1, source_target_pairs={{0,3},{1,0},{2,1},{3,2},{4,7},{5,4},{6,5},{7,6},{8,11},{9,8},{10,9... | collective-permute-start | bytes 4616 | tf_op jit(solution)/shard_map/ppermute | solution.py:493
  83.9 1.0 %collective-permute-start.4 = (f32[384]{0:T(512)S(1)}, f32[384]{0:T(512)S(1)}, u32[]{:S(2)}, u32[]{:S(2)}) collective-permute-start(f32[384]{0:T(512)S(1)} %slice_reduce_fusion), channel_id=1, source_target_pairs={{0,1},{1,2},{2,3},{3,0},{4,5},{5,6},{6,7},{7,4},{8,9},{9,10},{10,1... | collective-permute-start | bytes 4616 | tf_op jit(solution)/shard_map/ppermute | solution.py:493
  85.2 3.2 %collective-permute-done.5 = f32[384]{0:T(512)S(1)} collective-permute-done((f32[384]{0:T(512)S(1)}, f32[384]{0:T(512)S(1)}, u32[]{:S(2)}, u32[]{:S(2)}) %collective-permute-start.5) | collective-permute-done | bytes 1568 | tf_op jit(solution)/shard_map/ppermute | solution.py:493
  88.4 0.9 collective-permute-done.4
  89.3 2.5 %multiply_convert_fusion = bf16[384,1024]{1,0:T(8,128)(2,1)} fusion(f32[384,1024]{1,0:T(8,128)} %get-tuple-element.12, f32[1024]{0:T(1024)S(1)} %copy-done.5, f32[384]{0:T(512)S(1)} %add_rsqrt_fusion), kind=kLoop, calls=%fused_computation | loop fusion | flops 1179648 | bytes 2364928 | tf_op jit(solution)/shard_map/convert_element_type | solution.py:495
  91.8 1.0 %copy_bitcast_fusion = bf16[384,1024]{1,0:T(8,128)(2,1)} fusion(bf16[8,384,128]{2,1,0:T(8,128)(2,1)S(1)} %all-to-all-done.1), kind=kLoop, calls=%fused_computation.1 | loop fusion | bytes 1572864 | tf_op jit(solution)/shard_map/reshape | solution.py:486
  (20 shorter events, 2.7 us)
Async XLA Ops:
  7.8 47.8 %all-to-all-start = ((bf16[8,1168,128]{2,1,0:T(8,128)(2,1)}), bf16[8,1168,128]{2,1,0:T(8,128)(2,1)S(1)}, u32[]{:S(2)}, u32[]{:S(2)}) async-start(bf16[8,1168,128]{2,1,0:T(8,128)(2,1)} %pack.1), calls=%async_computation | async-start | bytes 4784128 | tf_op jit(solution)/shard_map/all_to_all | solution.py:475
  19.2 1.7 %collective-permute-start = (bf16[528,128]{1,0:T(8,128)(2,1)}, bf16[528,128]{1,0:T(8,128)(2,1)S(1)}, u32[]{:S(2)}, u32[]{:S(2)}) collective-permute-start(bf16[528,128]{1,0:T(8,128)(2,1)} %get-tuple-element.9), channel_id=1, source_target_pairs={{0,4},{4,0},{8,12},{12,8},{16,20},{20,16},{24,28},{28,24},{1,5},{5... | collective-permute-start | bytes 405512 | tf_op jit(solution)/shard_map/ppermute | solution.py:355
  19.7 33.3 %copy-start.4 = (s32[3]{0:T(128)}, s32[3]{0:T(128)S(1)}, u32[]{:S(2)}) copy-start(s32[3]{0:T(128)S(1)} %shift-right-arithmetic_and_fusion.flag_ref) | copy-start | bytes 40
  20.9 0.7 copy-start
  23.9 20.9 %collective-permute-start.1 = (bf16[528,128]{1,0:T(8,128)(2,1)}, bf16[528,128]{1,0:T(8,128)(2,1)S(1)}, u32[]{:S(2)}, u32[]{:S(2)}) collective-permute-start(bf16[528,128]{1,0:T(8,128)(2,1)} %join_pair.2.mine_ref), channel_id=1, source_target_pairs={{0,8},{4,12},{8,0},{12,4},{16,24},{20,28},{24,16},{28,20},{1,9},{5... | collective-permute-start | bytes 405512 | tf_op jit(solution)/shard_map/ppermute | solution.py:355
  44.8 0.6 copy-start.1
  47.6 5.3 %collective-permute-start.2 = (bf16[528,128]{1,0:T(8,128)(2,1)}, bf16[528,128]{1,0:T(8,128)(2,1)S(1)}, u32[]{:S(2)}, u32[]{:S(2)}) collective-permute-start(bf16[528,128]{1,0:T(8,128)(2,1)} %join_pair.3), channel_id=1, source_target_pairs={{0,16},{4,20},{8,24},{12,28},{16,0},{20,4},{24,8},{28,12},{1,17},{... | collective-permute-start | bytes 405512 | tf_op jit(solution)/shard_map/ppermute | solution.py:355
  53.0 0.6 copy-start.3
  55.6 14.8 %collective-permute-start.3 = (bf16[528,128]{1,0:T(8,128)(2,1)}, bf16[528,128]{1,0:T(8,128)(2,1)S(1)}, u32[]{:S(2)}, u32[]{:S(2)}) collective-permute-start(bf16[528,128]{1,0:T(8,128)(2,1)} %get-tuple-element.11), channel_id=1, source_target_pairs={{0,4},{4,0},{8,12},{12,8},{16,20},{20,16},{24,28},{28,24},{1,5},{5... | collective-permute-start | bytes 405512 | tf_op jit(solution)/shard_map/ppermute | solution.py:355
  66.9 24.9 %all-to-all-start.1 = ((bf16[8,384,128]{2,1,0:T(8,128)(2,1)}), bf16[8,384,128]{2,1,0:T(8,128)(2,1)S(1)}, u32[]{:S(2)}, u32[]{:S(2)}) async-start(bf16[8,384,128]{2,1,0:T(8,128)(2,1)} %bitcast.1), calls=%async_computation.1 | async-start | bytes 1572864 | tf_op jit(solution)/shard_map/all_to_all | solution.py:483
  70.4 18.9 %copy-start.5 = (f32[1024]{0:T(1024)S(1)}, f32[1024]{0:T(1024)}, u32[]{:S(2)}) copy-start(f32[1024]{0:T(1024)} %param.13) | copy-start | bytes 12292
  70.4 0.7 copy-start.2
  80.3 5.0 %collective-permute-start.6 = (f32[384]{0:T(512)S(1)}, f32[384]{0:T(512)S(1)}, u32[]{:S(2)}, u32[]{:S(2)}) collective-permute-start(f32[384]{0:T(512)S(1)} %slice_reduce_fusion), channel_id=1, source_target_pairs={{0,3},{1,0},{2,1},{3,2},{4,7},{5,4},{6,5},{7,6},{8,11},{9,8},{10,9... | collective-permute-start | bytes 4616 | tf_op jit(solution)/shard_map/ppermute | solution.py:493
  83.9 4.5 %collective-permute-start.5 = (f32[384]{0:T(512)S(1)}, f32[384]{0:T(512)S(1)}, u32[]{:S(2)}, u32[]{:S(2)}) collective-permute-start(f32[384]{0:T(512)S(1)} %slice_reduce_fusion), channel_id=1, source_target_pairs={{0,2},{1,3},{2,0},{3,1},{4,6},{5,7},{6,4},{7,5},{8,10},{9,11},{10,... | collective-permute-start | bytes 4616 | tf_op jit(solution)/shard_map/ppermute | solution.py:493
  83.9 5.4 %collective-permute-start.4 = (f32[384]{0:T(512)S(1)}, f32[384]{0:T(512)S(1)}, u32[]{:S(2)}, u32[]{:S(2)}) collective-permute-start(f32[384]{0:T(512)S(1)} %slice_reduce_fusion), channel_id=1, source_target_pairs={{0,1},{1,2},{2,3},{3,0},{4,5},{5,6},{6,7},{7,4},{8,9},{9,10},{10,1... | collective-permute-start | bytes 4616 | tf_op jit(solution)/shard_map/ppermute | solution.py:493

commit v2 on v0

v2 whole, which is shorter than its diff:
```python
import functools
import math

import jax
import jax.numpy as jnp
from jax import lax
from jax.experimental import pallas as pl
from jax.experimental.pallas import tpu as pltpu
from jax.sharding import PartitionSpec as P

EPSILON = 1e-05
MASKED = -1e30
LANES = 128
META = 16
DOC_LINE = 4
LAST_DOC_ID = 7
TILE = 256
F32 = jnp.float32
BF16 = jnp.bfloat16
HIGHEST = lax.Precision.HIGHEST
IN_VMEM = pl.BlockSpec(memory_space=pltpu.VMEM)
PARAMS = pltpu.CompilerParams(vmem_limit_bytes=48 << 20)


def nt_dot(a, b, precision=None):
    return lax.dot_general(
        a, b, (((1,), (1,)), ((), ())), precision=precision, preferred_element_type=F32
    )


def head_at(h):
    return slice(h * LANES, (h + 1) * LANES)


def column_of(row):
    return jnp.transpose(jnp.broadcast_to(row, (LANES, LANES)))


def three_parts(x):
    a = x.astype(BF16).astype(F32)
    b = (x - a).astype(BF16).astype(F32)
    return a, b, x - a - b


def cumulate(gates):
    heads, rows = gates.shape
    lower = lax.broadcasted_iota(jnp.int32, (rows, rows), 0) <= lax.broadcasted_iota(
        jnp.int32, (rows, rows), 1
    )
    parts = jnp.concatenate([*three_parts(gates), jnp.zeros_like(gates)], axis=0).astype(BF16)
    sums = jnp.dot(parts, jnp.where(lower, 1.0, 0.0).astype(BF16), preferred_element_type=F32)
    return sums[:heads] + sums[heads : 2 * heads] + sums[2 * heads : 3 * heads]


def columns(x):
    heads, rows = x.shape
    filler = jnp.zeros((LANES - 3 * heads, rows), F32)
    parts = jnp.concatenate([*three_parts(x), filler], axis=0)
    turned = jnp.concatenate(
        [jnp.transpose(parts[:, head_at(a)]) for a in range(rows // LANES)], axis=0
    ).astype(BF16)
    line = lax.broadcasted_iota(jnp.int32, (LANES, heads * LANES), 0)
    lane = lax.broadcasted_iota(jnp.int32, (LANES, heads * LANES), 1)
    pick = (line < 3 * heads) & (lax.rem(line, heads) == lane // LANES)
    return jnp.dot(turned, jnp.where(pick, 1.0, 0.0).astype(BF16), preferred_element_type=F32)


def moved(*shapes):
    return sum(math.prod(s.shape) * jnp.dtype(s.dtype).itemsize for s in shapes)


def pack_kernel(order, me_ref, q_ref, k_ref, v_ref, *out_refs):
    for d, out_ref in zip(order, out_refs):
        lanes = pl.ds(pl.multiple_of(lax.bitwise_xor(me_ref[0], d) * LANES, LANES), LANES)
        for i, ref in enumerate((q_ref, k_ref, v_ref)):
            out_ref[i] = ref[:, lanes]


def pack(me, q, k, v, order, pieces=3):
    rows, width = q.shape
    piece = rows // pieces
    outs = [jax.ShapeDtypeStruct((3, rows, LANES), BF16)] * len(order)
    return pl.pallas_call(
        functools.partial(pack_kernel, order),
        grid_spec=pltpu.PrefetchScalarGridSpec(
            num_scalar_prefetch=1,
            grid=(pieces,),
            in_specs=[pl.BlockSpec((piece, width), lambda r, me: (r, 0))] * 3,
            out_specs=[pl.BlockSpec((3, piece, LANES), lambda r, me: (0, r, 0))] * len(order),
        ),
        out_shape=outs,
        cost_estimate=pl.CostEstimate(flops=0, bytes_accessed=2 * moved(*outs), transcendentals=0),
        name="pack",
    )(me, q, k, v)


def attend_kernel(order, rows, window, me_ref, *refs):
    came = refs[: len(order)]
    held_ref, o_ref, q_ref, k_ref, v_ref, s_ref, p_ref, start_ref = refs[len(order) :]
    parts = len(order)
    per = rows // LANES
    factor = LANES ** (-0.5) * math.log2(math.e)
    i = pl.program_id(0)

    @pl.when(i == 0)
    def _():
        for d, ref in zip(order, came):
            at = pl.ds(pl.multiple_of(lax.bitwise_xor(me_ref[0], d) * rows, LANES), rows)
            q_ref[at, :] = ref[0]
            k_ref[at, :] = ref[1]
            v_ref[at, :LANES] = ref[2]
        v_ref[:, LANES:] = jnp.ones((parts * rows, LANES), BF16)
        docs = held_ref[:, LANES : LANES + META, :].astype(F32)
        line = lax.broadcasted_iota(jnp.int32, docs.shape, 1)
        used = (line >= DOC_LINE) & (line < DOC_LINE + per)
        for d in range(LAST_DOC_ID):
            start_ref[d] = jnp.sum(jnp.where(used & (docs < d + 1), 1.0, 0.0)).astype(jnp.int32)

    wide = (TILE, LANES)
    lane = lax.broadcasted_iota(jnp.int32, wide, 1)
    sub = lax.broadcasted_iota(jnp.int32, wide, 0)
    first = pl.multiple_of(i * TILE, TILE)
    low, high = 0, 0
    for d in range(LAST_DOC_ID):
        low = jnp.where(first >= start_ref[d], start_ref[d], low)
        high = jnp.where(first + TILE - 1 >= start_ref[d], start_ref[d], high)
    count = i - low // TILE + 1

    def run(n, mixed):
        base = pl.multiple_of((i - (n - 1)) * TILE, TILE)
        keys = pl.ds(base, n * TILE)
        queries = q_ref[pl.ds(first, TILE), :]
        if mixed:
            begin = jnp.zeros(wide, jnp.int32)
            for d in range(LAST_DOC_ID):
                begin = jnp.where(sub >= start_ref[d] - first, start_ref[d], begin)
            begin = begin - lane
        else:
            begin = low - lane
        top = jnp.full(wide, MASKED, F32)
        scores = nt_dot(queries, k_ref[keys, :])
        for c in range(n * TILE // LANES):
            at = head_at(c)
            piece = scores[:, at]
            if mixed or c < TILE // LANES:
                piece = jnp.where(begin <= base + c * LANES, piece, MASKED)
            ahead = c * LANES - (n - 1) * TILE
            if ahead >= 0:
                piece = jnp.where(lane - sub <= -ahead, piece, MASKED)
            top = jnp.maximum(top, piece)
            s_ref[:, at] = piece
        row_max = jnp.max(top, axis=1, keepdims=True) * factor
        for c in range(n * TILE // LANES):
            at = head_at(c)
            p_ref[:, at] = jnp.exp2(s_ref[:, at] * factor - row_max).astype(BF16)
        total = jnp.dot(p_ref[:, : n * TILE], v_ref[keys, :], preferred_element_type=F32)
        o_ref[...] = (total[:, :LANES] / total[:, LANES:]).astype(BF16)

    for n in range(1, window + 1):
        pl.when((count == n) & (low == high))(functools.partial(run, n, False))
        pl.when((count == n) & (low != high))(functools.partial(run, n, True))


def attend(me, came, held, order, longest):
    rows = came[0].shape[1]
    tokens = len(order) * rows
    window = min((longest - 1 + TILE - 1) // TILE + 1, tokens // TILE)
    out = jax.ShapeDtypeStruct((tokens, LANES), BF16)
    return pl.pallas_call(
        functools.partial(attend_kernel, order, rows, window),
        grid=(tokens // TILE,),
        in_specs=[pl.BlockSpec(memory_space=pltpu.SMEM)] + [IN_VMEM] * (len(order) + 1),
        out_specs=pl.BlockSpec((TILE, LANES), lambda i: (i, 0)),
        out_shape=out,
        scratch_shapes=[
            pltpu.VMEM((tokens, LANES), BF16),
            pltpu.VMEM((tokens, LANES), BF16),
            pltpu.VMEM((tokens, 2 * LANES), BF16),
            pltpu.VMEM((TILE, window * TILE), F32),
            pltpu.VMEM((TILE, window * TILE), BF16),
            pltpu.SMEM((LAST_DOC_ID,), jnp.int32),
        ],
        cost_estimate=pl.CostEstimate(
            flops=2 * tokens * longest * LANES * 2,
            bytes_accessed=moved(*came, held, out),
            transcendentals=tokens * longest // 2,
        ),
        compiler_params=PARAMS,
        name="attend",
    )(me, *came, held)


def attend_gathered(q, k, v, doc_ids, heads):
    rows = q.shape[0]
    keys = lax.all_gather(k, "ctx", axis=0, tiled=True)
    values = lax.all_gather(v, "ctx", axis=0, tiled=True)
    docs = lax.all_gather(doc_ids, "ctx", axis=0, tiled=True)
    position = lax.axis_index("ctx") * rows + jnp.arange(rows)
    allowed = (jnp.arange(docs.shape[0])[None, :] <= position[:, None]) & (
        docs[None, :] == doc_ids[:, None]
    )

    def one(h):
        queries, head_keys, head_values = (
            lax.dynamic_slice_in_dim(a, h * LANES, LANES, 1) for a in (q, keys, values)
        )
        scores = jnp.where(allowed, nt_dot(queries, head_keys) * LANES ** (-0.5), MASKED)
        weights = jnp.exp(scores - jnp.max(scores, axis=1, keepdims=True))
        mixed = jnp.dot(weights.astype(BF16), head_values, preferred_element_type=F32)
        return (mixed / jnp.sum(weights, axis=1, keepdims=True)).astype(BF16)

    return lax.map(one, jnp.arange(heads)).transpose(1, 0, 2).reshape(rows, heads * LANES)


def local_state_kernel(gate_ref, doc_ref, k_ref, v_ref, out_ref, cum_ref):
    heads, rows = gate_ref.shape
    cumulated = cumulate(gate_ref[...])
    cum_ref[...] = cumulated
    last = cumulated[:, rows - 1 : rows]
    doc = doc_ref[...]
    start, end = doc[:, 0:1], doc[:, rows - 1 : rows]
    weight = jnp.where(doc == end, jnp.exp(last - cumulated), 0.0)
    through = jnp.exp(last) * jnp.where(start == end, 1.0, 0.0)
    line = lax.broadcasted_iota(jnp.int32, (META, LANES), 0)
    common = jnp.where(line == 2, start.astype(F32), jnp.where(line == 3, end.astype(F32), 0.0))
    for a in range(rows // LANES):
        common = jnp.where(line == DOC_LINE + a, doc[:, head_at(a)].astype(F32), common)
    for h in range(heads):
        at = head_at(h)
        turned = jnp.transpose(k_ref[:, at]).astype(F32)
        weighted = (turned * weight[h : h + 1, :]).astype(BF16)
        out_ref[h, :LANES] = jnp.dot(weighted, v_ref[:, at], preferred_element_type=F32).astype(BF16)
        whole = through[h : h + 1, :]
        high = whole.astype(BF16).astype(F32)
        meta = jnp.where(line == 0, high, jnp.where(line == 1, whole - high, common))
        out_ref[h, LANES:] = meta.astype(BF16)


def local_state(k, v, gates, doc_row):
    heads, rows = gates.shape
    outs = [
        jax.ShapeDtypeStruct((heads, LANES + META, LANES), BF16),
        jax.ShapeDtypeStruct((heads, rows), F32),
    ]
    return pl.pallas_call(
        local_state_kernel,
        in_specs=[IN_VMEM] * 4,
        out_specs=[IN_VMEM] * 2,
        out_shape=outs,
        cost_estimate=pl.CostEstimate(
            flops=2 * heads * rows * LANES * LANES,
            bytes_accessed=moved(k, v, gates, *outs),
            transcendentals=heads * rows,
        ),
        compiler_params=PARAMS,
        name="local_state",
    )(gates, doc_row, k, v)


def carry_kernel(held_ref, out_ref):
    parts = held_ref.shape[0]
    line = lax.broadcasted_iota(jnp.int32, (META, LANES), 0)
    state = jnp.zeros((LANES, LANES), F32)
    before = jnp.full((1, LANES), -1.0, F32)
    for j in range(parts):
        out_ref[j, :LANES] = state.astype(BF16)
        out_ref[j, LANES:] = jnp.where(line == 3, before, 0.0).astype(BF16)
        meta = held_ref[j, LANES:].astype(F32)
        through = jnp.where(meta[2:3] == before, meta[0:1] + meta[1:2], 0.0)
        state = state * through + held_ref[j, :LANES].astype(F32)
        before = meta[3:4]


def carry(held):
    return pl.pallas_call(
        carry_kernel,
        in_specs=[IN_VMEM],
        out_specs=IN_VMEM,
        out_shape=jax.ShapeDtypeStruct(held.shape, BF16),
        cost_estimate=pl.CostEstimate(
            flops=2 * held.size, bytes_accessed=2 * moved(held), transcendentals=0
        ),
        name="carry",
    )(held)


def carry_gathered(block):
    every = lax.all_gather(block, "ctx")
    state = jnp.zeros(block[:, :LANES].shape, F32)
    before = jnp.full((LANES,), -1.0, F32)

    def one(j, carried):
        state, before = carried
        here = lax.dynamic_index_in_dim(every, j, 0, False).astype(F32)
        meta = here[:, LANES:]
        through = jnp.where(meta[:, 2] == before, meta[:, 0] + meta[:, 1], 0.0)
        return state * through[:, None, :] + here[:, :LANES], meta[0, 3]

    state, before = lax.fori_loop(0, lax.axis_index("ctx"), one, (state, before))
    tail = jnp.zeros((block.shape[0], META, LANES), F32).at[:, 3].set(before)
    return jnp.concatenate([state, tail], axis=1).astype(BF16)


def inside_kernel(cum_ref, doc_ref, q_ref, k_ref, v_ref, raw_ref, column_ref, bias_ref):
    heads, rows = cum_ref.shape
    count = rows // LANES
    column_ref[...] = columns(cum_ref[...])
    doc = doc_ref[...].astype(F32)
    square = (LANES, LANES)
    upto = lax.broadcasted_iota(jnp.int32, square, 0) >= lax.broadcasted_iota(jnp.int32, square, 1)
    for a in range(count):
        doc_column = column_of(doc[:, head_at(a)])
        for b in range(a + 1):
            ok = doc_column == doc[:, head_at(b)]
            ok = ok & upto if a == b else ok
            bias_ref[head_at(a), head_at(b)] = jnp.where(ok, 0.0, MASKED)
    for h in range(heads):
        at = head_at(h)
        row = cum_ref[h : h + 1, :]
        for a in range(count):
            lines = head_at(a)
            width = (a + 1) * LANES
            scores = nt_dot(q_ref[lines, at], k_ref[0:width, at])
            spread = jnp.concatenate([column_ref[lines, at]] * (a + 1), axis=1) - row[:, :width]
            decayed = scores * jnp.exp(spread + bias_ref[lines, 0:width])
            raw_ref[lines, at] = jnp.dot(
                decayed.astype(BF16), v_ref[0:width, at], preferred_element_type=F32
            )


def inside(q, k, v, cumulated, doc_row):
    heads, rows = cumulated.shape
    out = jax.ShapeDtypeStruct(q.shape, F32)
    return pl.pallas_call(
        inside_kernel,
        in_specs=[IN_VMEM] * 5,
        out_specs=IN_VMEM,
        out_shape=out,
        scratch_shapes=[pltpu.VMEM(q.shape, F32), pltpu.VMEM((rows, rows), F32)],
        cost_estimate=pl.CostEstimate(
            flops=3 * heads * rows * rows * LANES,
            bytes_accessed=moved(q, k, v, out),
            transcendentals=heads * rows * rows // 2,
        ),
        compiler_params=PARAMS,
        name="inside",
    )(cumulated, doc_row, q, k, v)


def incoming_kernel(cum_ref, doc_ref, q_ref, before_ref, raw_ref, out_ref, square_ref):
    heads, rows = cum_ref.shape
    factor = columns(jnp.exp(cum_ref[...]))
    doc = doc_ref[...].astype(F32)
    meta = before_ref[0, LANES:].astype(F32)
    linked = jnp.concatenate(
        [jnp.where(column_of(doc[:, head_at(a)]) == meta[3:4], 1.0, 0.0) for a in range(rows // LANES)],
        axis=0,
    )
    total = jnp.zeros((rows, LANES), F32)
    for h in range(heads):
        at = head_at(h)
        came = jnp.dot(q_ref[:, at], before_ref[h, :LANES], preferred_element_type=F32)
        raw = raw_ref[:, at] + came * (factor[:, at] * linked)
        out_ref[:, at] = raw
        total = total + raw * raw
    square_ref[...] = nt_dot(jnp.ones((8, LANES), F32), total, HIGHEST)


def incoming(q, cumulated, doc_row, before, raw):
    heads, rows = cumulated.shape
    outs = [jax.ShapeDtypeStruct(q.shape, F32), jax.ShapeDtypeStruct((8, rows), F32)]
    return pl.pallas_call(
        incoming_kernel,
        in_specs=[IN_VMEM] * 5,
        out_specs=[IN_VMEM] * 2,
        out_shape=outs,
        cost_estimate=pl.CostEstimate(
            flops=2 * heads * rows * LANES * LANES,
            bytes_accessed=moved(q, before, raw, *outs),
            transcendentals=heads * rows,
        ),
        compiler_params=PARAMS,
        name="incoming",
    )(cumulated, doc_row, q, before, raw)


def normalize_kernel(features, raw_ref, gain_ref, *refs):
    *squares, out_ref = refs
    total = squares[0][...]
    for ref in squares[1:]:
        total = total + ref[...]
    scale = column_of(lax.rsqrt(total / features + EPSILON)[0:1])
    for h in range(raw_ref.shape[1] // LANES):
        at = head_at(h)
        out_ref[:, at] = (raw_ref[:, at] * scale * gain_ref[:, at]).astype(BF16)


def normalize(raw, gain_row, squares, features):
    rows, width = raw.shape
    line = pl.BlockSpec((LANES, width), lambda r: (r, 0))
    out = jax.ShapeDtypeStruct((rows, width), BF16)
    return pl.pallas_call(
        functools.partial(normalize_kernel, features),
        grid=(rows // LANES,),
        in_specs=[line, pl.BlockSpec((1, width), lambda r: (0, 0))]
        + [pl.BlockSpec((8, LANES), lambda r: (0, r))] * len(squares),
        out_specs=line,
        out_shape=out,
        cost_estimate=pl.CostEstimate(
            flops=3 * raw.size, bytes_accessed=moved(raw, out), transcendentals=rows
        ),
        name="normalize",
    )(raw, gain_row, *squares)


def after(x, *earlier):
    return lax.optimization_barrier((x, *earlier))[0]


def exchange(x):
    return lax.all_to_all(x, "ctx", split_axis=0, concat_axis=0, tiled=True)


def on_device(size, head_parts, q_lin, k_lin, v_lin, gate_log, lin_gain, q_soft, k_soft, v_soft, doc_ids):
    heads, rows = gate_log.shape
    doc_row = doc_ids.reshape(1, rows)

    if heads == size and size & (size - 1) == 0:
        me = lax.axis_index("ctx").reshape(1)

        def swap(x, d):
            return lax.ppermute(x, "ctx", [(i, i ^ d) for i in range(size)])

        order = [d for d in range(size - 2, 0, -2)] + [d for d in range(size - 1, 0, -2)] + [0]
        early = size // 2 - 1
        sent = pack(me, q_soft, k_soft, v_soft, order)
        came = [swap(sent[i], order[i]) for i in range(early)]
        states, cumulated = local_state(after(k_lin, sent[-1]), v_lin, gate_log, doc_row)
        held_states = exchange(states)
        late, _ = lax.optimization_barrier((sent[early:-1], states))
        came += [swap(x, d) for x, d in zip(late, order[early:])]
        passed = carry(held_states)
        before = exchange(passed)
        raw = inside(after(q_lin, passed), k_lin, v_lin, cumulated, doc_row)
        mixed = attend(me, [*came, after(sent[-1], raw)], held_states, order, rows * size // 2)
        back = exchange(mixed.reshape(size, rows, LANES))
        raw, square = incoming(q_lin, cumulated, doc_row, after(before, mixed), raw)
        soft_out = back.transpose(1, 0, 2).reshape(rows, heads * LANES)
    else:
        states, cumulated = local_state(k_lin, v_lin, gate_log, doc_row)
        raw = inside(q_lin, k_lin, v_lin, cumulated, doc_row)
        raw, square = incoming(q_lin, cumulated, doc_row, carry_gathered(states), raw)
        soft_out = attend_gathered(q_soft, k_soft, v_soft, doc_ids, heads)

    squares = [square]
    for d in range(1, head_parts):
        turn = [(i, (i + d) % head_parts) for i in range(head_parts)]
        squares.append(lax.ppermute(square, "head", turn))
    lin_out = normalize(raw, lin_gain.reshape(1, -1), squares, heads * head_parts * LANES)
    return lin_out, soft_out


def solution(mesh):
    split = P("ctx", "head")
    in_specs = (split, split, split, P("head", "ctx"), P("head"), split, split, split, P("ctx"))
    return jax.shard_map(
        functools.partial(on_device, mesh.shape["ctx"], mesh.shape["head"]),
        mesh=mesh,
        in_specs=in_specs,
        out_specs=(split, split),
        check_vma=False,
    )
```

time: 181 us -> 79.5 us (0.44)
  matrix products: 50.2 us -> 0 us
  blocking collectives: 41.5 us -> 0 us
  starting transfers between devices: 0.12 us -> 30 us
  Pallas kernels: 0 us -> 29.1 us
  other arithmetic: 24.1 us -> 0 us
  waiting for transfers between devices: 27.7 us -> 11.5 us
  between operations: 15.8 us -> 0.78 us
  local copies, waits for them, and re-layouts: 20.5 us -> 7.24 us
    dot_general x6 -> x0, matrix products: 50.2 us -> none  [the longest x1 18.4 us: soft_core(): jnp.einsum('qhd,khd->hqk', queries, key_piece.reshape(piece_rows, head_co...]
    pallas_call x0 -> x7, Pallas kernels: none -> 29.1 us  [the longest x1 13.2 us: attend(): pl.pallas_call(functools.partial(attend_kernel, order, rows, window), gri...]
    all_gather x3 -> x0, waiting for transfers between devices: 26.9 us -> none  [the longest x1 15.8 us: soft_core(): key_piece = lax.all_gather(k_soft, 'ctx', axis=0, tiled=True)]
    unnamed x2 -> x0, blocking collectives: 21.5 us -> none
    ppermute x0 -> x10, starting transfers between devices: none -> 18.2 us  [the longest x3 9.11 us: on_device(): squares.append(lax.ppermute(square, 'head', turn))]
    reduce_sum x1 -> x0, other arithmetic: 17.9 us -> none  [soft_core(): new_total = jnp.sum(weights, axis=2)]
    psum x1 -> x0, blocking collectives: 12.2 us -> none  [linear_core(): square_sum = lax.psum(jnp.sum(raw_output * raw_output, axis=1), 'head')]
    all_to_all x0 -> x3, starting transfers between devices: none -> 11.8 us  [exchange(): return lax.all_to_all(x, 'ctx', split_axis=0, concat_axis=0, tiled=True)]
  transfers between devices with their start and end apart: 3 -> 13, of which waited for: 2 -> 7; matrix products, arithmetic and copies ran while one was open for 31% -> 0% of each run, Pallas kernels for 0% -> 32%
where the time goes in v2:
time: 79.5 us; the launch traced here: 78.6 us
  starting transfers between devices  30 us (38%)
  Pallas kernels  29.1 us (37%)
  waiting for transfers between devices  11.5 us (14%)
  local copies, waits for them, and re-layouts  7.24 us (9%)
    pallas_call x1, Pallas kernels, attend(): pl.pallas_call(functools.partial(attend_kernel, order, rows, window), gri...  13.2 us
    all_to_all x3, starting transfers between devices, exchange(): return lax.all_to_all(x, 'ctx', split_axis=0, concat_axis=0, tiled=True)  11.8 us
    ppermute x3, starting transfers between devices, on_device(): squares.append(lax.ppermute(square, 'head', turn))  9.11 us
    ppermute x7, starting transfers between devices, swap(): return lax.ppermute(x, 'ctx', [(i, i ^ d) for i in range(size)])  9.09 us
    ppermute x7, waiting for transfers between devices, swap(): return lax.ppermute(x, 'ctx', [(i, i ^ d) for i in range(size)])  6.2 us
    unnamed x36, local copies, waits for them, and re-layouts  5.11 us
    ppermute x3, waiting for transfers between devices, on_device(): squares.append(lax.ppermute(square, 'head', turn))  4.48 us
    pallas_call x1, Pallas kernels, pack(): pl.pallas_call(functools.partial(pack_kernel, order), grid_spec=pltpu.Pre...  4.2 us
  transfers between devices with their start and end apart: 13, of which 7 were waited for; matrix products, arithmetic and copies ran while one was open for 0% of the time, Pallas kernels for 32%

profile of v2, /device:TPU:0, one launch (start us, length us, event | category | flops | bytes accessed | tf_op | source)
XLA Modules:
  0.0 78.6 jit_solution(3770063433099671425)
XLA Ops:
  0.7 4.2 %pack.1 = (bf16[3,384,128]{2,1,0:T(8,128)(2,1)}, bf16[3,384,128]{2,1,0:T(8,128)(2,1)}, bf16[3,384,128]{2,1,0:T(8,128)(2,1)}, bf16[3,384,128]{2,1,0:T(8,128)(2,1)...) custom-call(s32[1]{0:T(128)} %bitcast.me_ref, ...), custom_call_target="tpu_custom_call" | custom-call | bytes 4718592 | tf_op jit(solution)/shard_map/pack/pallas_call | solution.py:83
  4.9 4.0 %collective-permute-start = (bf16[3,384,128]{2,1,0:T(8,128)(2,1)}, bf16[3,384,128]{2,1,0:T(8,128)(2,1)S(1)}, u32[]{:S(2)}, u32[]{:S(2)}) collective-permute-start(bf16[3,384,128]{2,1,0:T(8,128)(2,1)} %get-tuple-element.26), channel_id=1, source_target_pairs={{0,24},{4,28},{8,16},{12,20},{16,8},{20,12},{24,0},{28,4},{1,25},{... | collective-permute-start | bytes 884744 | tf_op jit(solution)/shard_map/ppermute | solution.py:432
  9.4 1.4 %local_state.1 = (bf16[8,144,128]{2,1,0:T(8,128)(2,1)}, f32[8,384]{1,0:T(8,128)S(1)}) custom-call(f32[8,384]{1,0:T(8,128)S(1)} %copy-done.7, s32[1,384]{1,0:T(1,128)S(1)} %reshape.19.doc_ref, bf16[384,1024]{1,0:T(8,128)(2,1)S(1)} %copy-done, bf16[384,1024]{1,0:T(8,128)(2,1)S(1)} %copy-done.1), custom_call_target="tpu_custom_call" | custom-call | flops 100663296 | bytes 1892352 | tf_op jit(solution)/shard_map/local_state/pallas_call | solution.py:245
  10.7 3.4 %all-to-all-start = ((bf16[8,144,128]{2,1,0:T(8,128)(2,1)}), bf16[8,144,128]{2,1,0:T(8,128)(2,1)S(1)}, u32[]{:S(2)}, u32[]{:S(2)}) async-start(bf16[8,144,128]{2,1,0:T(8,128)(2,1)} %get-tuple-element.25), calls=%async_computation | async-start | bytes 589824 | tf_op jit(solution)/shard_map/all_to_all | solution.py:421
  14.2 1.9 %collective-permute-start.2 = (bf16[3,384,128]{2,1,0:T(8,128)(2,1)}, bf16[3,384,128]{2,1,0:T(8,128)(2,1)}, u32[]{:S(2)}, u32[]{:S(2)}) collective-permute-start(bf16[3,384,128]{2,1,0:T(8,128)(2,1)} %get-tuple-element.28), channel_id=1, source_target_pairs={{0,8},{4,12},{8,0},{12,4},{16,24},{20,28},{24,16},{28,20},{1,9},{5... | collective-permute-start | bytes 884744 | tf_op jit(solution)/shard_map/ppermute | solution.py:432
  16.1 0.9 %collective-permute-start.3 = (bf16[3,384,128]{2,1,0:T(8,128)(2,1)}, bf16[3,384,128]{2,1,0:T(8,128)(2,1)}, u32[]{:S(2)}, u32[]{:S(2)}) collective-permute-start(bf16[3,384,128]{2,1,0:T(8,128)(2,1)} %get-tuple-element.33), channel_id=1, source_target_pairs={{0,28},{4,24},{8,20},{12,16},{16,12},{20,8},{24,4},{28,0},{1,29},{... | collective-permute-start | bytes 884744 | tf_op jit(solution)/shard_map/ppermute | solution.py:432
  18.2 1.3 %collective-permute-start.5 = (bf16[3,384,128]{2,1,0:T(8,128)(2,1)}, bf16[3,384,128]{2,1,0:T(8,128)(2,1)}, u32[]{:S(2)}, u32[]{:S(2)}) collective-permute-start(bf16[3,384,128]{2,1,0:T(8,128)(2,1)} %get-tuple-element.35), channel_id=1, source_target_pairs={{0,12},{4,8},{8,4},{12,0},{16,28},{20,24},{24,20},{28,16},{1,13},{... | collective-permute-start | bytes 884744 | tf_op jit(solution)/shard_map/ppermute | solution.py:432
  19.5 4.5 %collective-permute-done.1.refs_1_ = bf16[3,384,128]{2,1,0:T(8,128)(2,1)S(1)} collective-permute-done((bf16[3,384,128]{2,1,0:T(8,128)(2,1)}, bf16[3,384,128]{2,1,0:T(8,128)(2,1)S(1)}, u32[]{:S(2)}, u32[]{:S(2)}) %collective-permute-start.1) | collective-permute-done | bytes 294944 | tf_op jit(solution)/shard_map/ppermute | solution.py:432
  24.8 0.9 %all-to-all-done.held_ref.refs_8_ = bf16[8,144,128]{2,1,0:T(8,128)(2,1)S(1)} async-done(((bf16[8,144,128]{2,1,0:T(8,128)(2,1)}), bf16[8,144,128]{2,1,0:T(8,128)(2,1)S(1)}, u32[]{:S(2)}, u32[]{:S(2)}) %all-to-all-start) | async-done | bytes 294944 | tf_op jit(solution)/shard_map/all_to_all | solution.py:421
  26.3 1.7 %carry.1 = bf16[8,144,128]{2,1,0:T(8,128)(2,1)} custom-call(bf16[8,144,128]{2,1,0:T(8,128)(2,1)} %copy-done.5), custom_call_target="tpu_custom_call" | custom-call | flops 294912 | bytes 589824 | tf_op jit(solution)/shard_map/carry/pallas_call | solution.py:275
  28.1 4.1 %all-to-all-start.1 = ((bf16[8,144,128]{2,1,0:T(8,128)(2,1)}), bf16[8,144,128]{2,1,0:T(8,128)(2,1)S(1)}, u32[]{:S(2)}, u32[]{:S(2)}) async-start(bf16[8,144,128]{2,1,0:T(8,128)(2,1)} %carry.1), calls=%async_computation.1 | async-start | bytes 589824 | tf_op jit(solution)/shard_map/all_to_all | solution.py:421
  32.1 1.1 %copy-done.2 = bf16[384,1024]{1,0:T(8,128)(2,1)S(1)} copy-done((bf16[384,1024]{1,0:T(8,128)(2,1)S(1)}, bf16[384,1024]{1,0:T(8,128)(2,1)}, u32[]{:S(2)}) %copy-start.2) | copy-done | bytes 786456
  33.3 4.1 %inside.1.raw_ref = f32[384,1024]{1,0:T(8,128)S(1)} custom-call(f32[8,384]{1,0:T(8,128)S(1)} %get-tuple-element.24.cum_ref, s32[1,384]{1,0:T(1,128)S(1)} %reshape.19.doc_ref, bf16[384,1024]{1,0:T(8,128)(2,1)S(1)} %copy-done.2, bf16[384,1024]{1,0:T(8,128)(2,1)S(1)} %copy-done, bf16[384,1024]{1,0:T(8,128)(2,1)S(1)} %copy-done.1), custom_call_target="tpu_custom_call" | custom-call | flops 452984832 | bytes 3932160 | tf_op jit(solution)/shard_map/inside/pallas_call | solution.py:334
  38.2 0.9 %collective-permute-done.5.refs_5_ = bf16[3,384,128]{2,1,0:T(8,128)(2,1)} collective-permute-done((bf16[3,384,128]{2,1,0:T(8,128)(2,1)}, bf16[3,384,128]{2,1,0:T(8,128)(2,1)}, u32[]{:S(2)}, u32[]{:S(2)}) %collective-permute-start.5) | collective-permute-done | bytes 294944 | tf_op jit(solution)/shard_map/ppermute | solution.py:432
  39.1 13.2 %attend.1 = bf16[3072,128]{1,0:T(8,128)(2,1)} custom-call(s32[1]{0:T(128)} %bitcast.me_ref, bf16[3,384,128]{2,1,0:T(8,128)(2,1)S(1)} %copy-done.11, bf16[3,384,128]{2,1,0:T(8,128)(2,1)S(1)} %copy-done.13, bf16[3,384,128]{2,1,0:T(8,128)(2,1)} %collective-permute-done.2.refs_2_, bf16[3,384,128]{2,1,0:T(8,128)(2,1)} %collective-permute-done.3.refs_3_, ...), custom_call_target="tpu_custom_call" | custom-call | flops 2415919104 | bytes 3440640 | tf_op jit(solution)/shard_map/attend/pallas_call | solution.py:169
  52.3 4.3 %all-to-all-start.2 = ((bf16[8,384,128]{2,1,0:T(8,128)(2,1)}), bf16[8,384,128]{2,1,0:T(8,128)(2,1)}, u32[]{:S(2)}, u32[]{:S(2)}) async-start(bf16[8,384,128]{2,1,0:T(8,128)(2,1)} %bitcast.2), calls=%async_computation.2 | async-start | bytes 1572864 | tf_op jit(solution)/shard_map/all_to_all | solution.py:421
  56.7 1.1 %incoming.1 = (f32[384,1024]{1,0:T(8,128)S(1)}, f32[8,384]{1,0:T(8,128)S(1)}) custom-call(f32[8,384]{1,0:T(8,128)S(1)} %get-tuple-element.24.cum_ref, s32[1,384]{1,0:T(1,128)S(1)} %reshape.19.doc_ref, bf16[384,1024]{1,0:T(8,128)(2,1)S(1)} %copy-done.3, bf16[8,144,128]{2,1,0:T(8,128)(2,1)S(1)} %all-to-all-done.1.before_ref, f32[384,1024]{1,0:T(8,128)S(1)} %inside.1.raw_ref), custom_call_target="tpu_custom_call" | custom-call | flops 100663296 | bytes 4239360 | tf_op jit(solution)/shard_map/incoming/pallas_call | solution.py:372
  57.8 1.2 %copy-done.4 = f32[384,1024]{1,0:T(8,128)} copy-done((f32[384,1024]{1,0:T(8,128)}, f32[384,1024]{1,0:T(8,128)S(1)}, u32[]{:S(2)}) %copy-start.4) | copy-done | bytes 1572888
  59.0 8.1 %collective-permute-start.9 = (f32[8,384]{1,0:T(8,128)S(1)}, f32[8,384]{1,0:T(8,128)S(1)}, u32[]{:S(2)}, u32[]{:S(2)}) collective-permute-start(f32[8,384]{1,0:T(8,128)S(1)} %get-tuple-element.41.refs_0_), channel_id=1, source_target_pairs={{0,3},{1,0},{2,1},{3,2},{4,7},{5,4},{6,5},{7,6},{8,11},{9,8},{10,9... | collective-permute-start | bytes 36872 | tf_op jit(solution)/shard_map/ppermute | solution.py:458
  67.1 1.0 %collective-permute-start.7 = (f32[8,384]{1,0:T(8,128)S(1)}, f32[8,384]{1,0:T(8,128)S(1)}, u32[]{:S(2)}, u32[]{:S(2)}) collective-permute-start(f32[8,384]{1,0:T(8,128)S(1)} %get-tuple-element.41.refs_0_), channel_id=1, source_target_pairs={{0,1},{1,2},{2,3},{3,0},{4,5},{5,6},{6,7},{7,4},{8,9},{9,10},{10,1... | collective-permute-start | bytes 36872 | tf_op jit(solution)/shard_map/ppermute | solution.py:458
  68.5 3.2 %collective-permute-done.8.refs_2_ = f32[8,384]{1,0:T(8,128)S(1)} collective-permute-done((f32[8,384]{1,0:T(8,128)S(1)}, f32[8,384]{1,0:T(8,128)S(1)}, u32[]{:S(2)}, u32[]{:S(2)}) %collective-permute-start.8) | collective-permute-done | bytes 12320 | tf_op jit(solution)/shard_map/ppermute | solution.py:458
  71.7 0.9 %collective-permute-done.7.refs_1_ = f32[8,384]{1,0:T(8,128)S(1)} collective-permute-done((f32[8,384]{1,0:T(8,128)S(1)}, f32[8,384]{1,0:T(8,128)S(1)}, u32[]{:S(2)}, u32[]{:S(2)}) %collective-permute-start.7) | collective-permute-done | bytes 12320 | tf_op jit(solution)/shard_map/ppermute | solution.py:458
  73.2 3.3 %normalize.1 = bf16[384,1024]{1,0:T(8,128)(2,1)} custom-call(f32[384,1024]{1,0:T(8,128)} %copy-done.4, f32[1,1024]{1,0:T(1,128)} %bitcast.9, f32[8,384]{1,0:T(8,128)} %copy-done.8, f32[8,384]{1,0:T(8,128)} %copy-done.16, f32[8,384]{1,0:T(8,128)} %copy-done.15, f32[8,384]{1,0:T(8,128)} %copy-done.14), custom_call_target="tpu_custom_call" | custom-call | flops 1179648 | bytes 2359296 | tf_op jit(solution)/shard_map/normalize/pallas_call | solution.py:402
  76.5 2.1 %copy_bitcast_fusion = bf16[384,1024]{1,0:T(8,128)(2,1)} fusion(bf16[8,384,128]{2,1,0:T(8,128)(2,1)} %all-to-all-done.2), kind=kLoop, calls=%fused_computation | loop fusion | bytes 1572864 | tf_op jit(solution)/shard_map/reshape | solution.py:448
  (47 shorter events, 4.9 us)
Async XLA Ops:
  0.6 8.7 %copy-start.17 = (s32[384]{0:T(512)S(1)}, s32[384]{0:T(512)}, u32[]{:S(2)}) copy-start(s32[384]{0:T(512)} %param.17) | copy-start | bytes 4612
  0.6 8.7 %copy-start = (bf16[384,1024]{1,0:T(8,128)(2,1)S(1)}, bf16[384,1024]{1,0:T(8,128)(2,1)}, u32[]{:S(2)}) copy-start(bf16[384,1024]{1,0:T(8,128)(2,1)} %k_ref.4) | copy-start | bytes 2359300
  0.7 8.7 %copy-start.1 = (bf16[384,1024]{1,0:T(8,128)(2,1)S(1)}, bf16[384,1024]{1,0:T(8,128)(2,1)}, u32[]{:S(2)}) copy-start(bf16[384,1024]{1,0:T(8,128)(2,1)} %v_ref.5) | copy-start | bytes 2359300
  0.7 8.7 %copy-start.7 = (f32[8,384]{1,0:T(8,128)S(1)}, f32[8,384]{1,0:T(8,128)}, u32[]{:S(2)}) copy-start(f32[8,384]{1,0:T(8,128)} %gate_ref.1) | copy-start | bytes 36868
  4.9 12.6 %collective-permute-start = (bf16[3,384,128]{2,1,0:T(8,128)(2,1)}, bf16[3,384,128]{2,1,0:T(8,128)(2,1)S(1)}, u32[]{:S(2)}, u32[]{:S(2)}) collective-permute-start(bf16[3,384,128]{2,1,0:T(8,128)(2,1)} %get-tuple-element.26), channel_id=1, source_target_pairs={{0,24},{4,28},{8,16},{12,20},{16,8},{20,12},{24,0},{28,4},{1,25},{... | collective-permute-start | bytes 884744 | tf_op jit(solution)/shard_map/ppermute | solution.py:432
  8.8 15.2 %collective-permute-start.1 = (bf16[3,384,128]{2,1,0:T(8,128)(2,1)}, bf16[3,384,128]{2,1,0:T(8,128)(2,1)S(1)}, u32[]{:S(2)}, u32[]{:S(2)}) collective-permute-start(bf16[3,384,128]{2,1,0:T(8,128)(2,1)} %get-tuple-element.27), channel_id=1, source_target_pairs={{0,16},{4,20},{8,24},{12,28},{16,0},{20,4},{24,8},{28,12},{1,17},{... | collective-permute-start | bytes 884744 | tf_op jit(solution)/shard_map/ppermute | solution.py:432
  10.7 14.9 %all-to-all-start = ((bf16[8,144,128]{2,1,0:T(8,128)(2,1)}), bf16[8,144,128]{2,1,0:T(8,128)(2,1)S(1)}, u32[]{:S(2)}, u32[]{:S(2)}) async-start(bf16[8,144,128]{2,1,0:T(8,128)(2,1)} %get-tuple-element.25), calls=%async_computation | async-start | bytes 589824 | tf_op jit(solution)/shard_map/all_to_all | solution.py:421
  14.2 23.2 %collective-permute-start.2 = (bf16[3,384,128]{2,1,0:T(8,128)(2,1)}, bf16[3,384,128]{2,1,0:T(8,128)(2,1)}, u32[]{:S(2)}, u32[]{:S(2)}) collective-permute-start(bf16[3,384,128]{2,1,0:T(8,128)(2,1)} %get-tuple-element.28), channel_id=1, source_target_pairs={{0,8},{4,12},{8,0},{12,4},{16,24},{20,28},{24,16},{28,20},{1,9},{5... | collective-permute-start | bytes 884744 | tf_op jit(solution)/shard_map/ppermute | solution.py:432
  16.1 21.3 %collective-permute-start.3 = (bf16[3,384,128]{2,1,0:T(8,128)(2,1)}, bf16[3,384,128]{2,1,0:T(8,128)(2,1)}, u32[]{:S(2)}, u32[]{:S(2)}) collective-permute-start(bf16[3,384,128]{2,1,0:T(8,128)(2,1)} %get-tuple-element.33), channel_id=1, source_target_pairs={{0,28},{4,24},{8,20},{12,16},{16,12},{20,8},{24,4},{28,0},{1,29},{... | collective-permute-start | bytes 884744 | tf_op jit(solution)/shard_map/ppermute | solution.py:432
  17.0 21.1 %collective-permute-start.4 = (bf16[3,384,128]{2,1,0:T(8,128)(2,1)}, bf16[3,384,128]{2,1,0:T(8,128)(2,1)}, u32[]{:S(2)}, u32[]{:S(2)}) collective-permute-start(bf16[3,384,128]{2,1,0:T(8,128)(2,1)} %get-tuple-element.34), channel_id=1, source_target_pairs={{0,20},{4,16},{8,28},{12,24},{16,4},{20,0},{24,12},{28,8},{1,21},{... | collective-permute-start | bytes 884744 | tf_op jit(solution)/shard_map/ppermute | solution.py:432
  18.2 20.9 %collective-permute-start.5 = (bf16[3,384,128]{2,1,0:T(8,128)(2,1)}, bf16[3,384,128]{2,1,0:T(8,128)(2,1)}, u32[]{:S(2)}, u32[]{:S(2)}) collective-permute-start(bf16[3,384,128]{2,1,0:T(8,128)(2,1)} %get-tuple-element.35), channel_id=1, source_target_pairs={{0,12},{4,8},{8,4},{12,0},{16,28},{20,24},{24,20},{28,16},{1,13},{... | collective-permute-start | bytes 884744 | tf_op jit(solution)/shard_map/ppermute | solution.py:432
  24.7 14.4 %collective-permute-start.6 = (bf16[3,384,128]{2,1,0:T(8,128)(2,1)}, bf16[3,384,128]{2,1,0:T(8,128)(2,1)}, u32[]{:S(2)}, u32[]{:S(2)}) collective-permute-start(bf16[3,384,128]{2,1,0:T(8,128)(2,1)} %get-tuple-element.36), channel_id=1, source_target_pairs={{0,4},{4,0},{8,12},{12,8},{16,20},{20,16},{24,28},{28,24},{1,5},{5... | collective-permute-start | bytes 884744 | tf_op jit(solution)/shard_map/ppermute | solution.py:432
  28.1 24.3 %all-to-all-start.1 = ((bf16[8,144,128]{2,1,0:T(8,128)(2,1)}), bf16[8,144,128]{2,1,0:T(8,128)(2,1)S(1)}, u32[]{:S(2)}, u32[]{:S(2)}) async-start(bf16[8,144,128]{2,1,0:T(8,128)(2,1)} %carry.1), calls=%async_computation.1 | async-start | bytes 589824 | tf_op jit(solution)/shard_map/all_to_all | solution.py:421
  33.3 5.8 %copy-start.6 = (bf16[8,144,128]{2,1,0:T(8,128)(2,1)S(1)}, bf16[8,144,128]{2,1,0:T(8,128)(2,1)}, u32[]{:S(2)}) copy-start(bf16[8,144,128]{2,1,0:T(8,128)(2,1)} %copy-done.5) | copy-start | bytes 884740
  33.3 5.8 %copy-start.9 = (bf16[3,384,128]{2,1,0:T(8,128)(2,1)S(1)}, bf16[3,384,128]{2,1,0:T(8,128)(2,1)}, u32[]{:S(2)}) copy-start(bf16[3,384,128]{2,1,0:T(8,128)(2,1)} %get-tuple-element.38.refs_7_) | copy-start | bytes 884740
  33.3 5.8 %copy-start.11 = (bf16[3,384,128]{2,1,0:T(8,128)(2,1)S(1)}, bf16[3,384,128]{2,1,0:T(8,128)(2,1)}, u32[]{:S(2)}) copy-start(bf16[3,384,128]{2,1,0:T(8,128)(2,1)} %copy-done.10) | copy-start | bytes 884740
  33.3 5.8 %copy-start.13 = (bf16[3,384,128]{2,1,0:T(8,128)(2,1)S(1)}, bf16[3,384,128]{2,1,0:T(8,128)(2,1)}, u32[]{:S(2)}) copy-start(bf16[3,384,128]{2,1,0:T(8,128)(2,1)} %copy-done.12) | copy-start | bytes 884740
  52.3 4.4 %copy-start.3 = (bf16[384,1024]{1,0:T(8,128)(2,1)S(1)}, bf16[384,1024]{1,0:T(8,128)(2,1)}, u32[]{:S(2)}) copy-start(bf16[384,1024]{1,0:T(8,128)(2,1)} %q_ref.4) | copy-start | bytes 2359300
  52.3 24.2 %all-to-all-start.2 = ((bf16[8,384,128]{2,1,0:T(8,128)(2,1)}), bf16[8,384,128]{2,1,0:T(8,128)(2,1)}, u32[]{:S(2)}, u32[]{:S(2)}) async-start(bf16[8,384,128]{2,1,0:T(8,128)(2,1)} %bitcast.2), calls=%async_computation.2 | async-start | bytes 1572864 | tf_op jit(solution)/shard_map/all_to_all | solution.py:421
  59.0 13.6 %copy-start.8 = (f32[8,384]{1,0:T(8,128)}, f32[8,384]{1,0:T(8,128)S(1)}, u32[]{:S(2)}) copy-start(f32[8,384]{1,0:T(8,128)S(1)} %get-tuple-element.41.refs_0_) | copy-start | bytes 36868
  59.0 9.5 %collective-permute-start.9 = (f32[8,384]{1,0:T(8,128)S(1)}, f32[8,384]{1,0:T(8,128)S(1)}, u32[]{:S(2)}, u32[]{:S(2)}) collective-permute-start(f32[8,384]{1,0:T(8,128)S(1)} %get-tuple-element.41.refs_0_), channel_id=1, source_target_pairs={{0,3},{1,0},{2,1},{3,2},{4,7},{5,4},{6,5},{7,6},{8,11},{9,8},{10,9... | collective-permute-start | bytes 36872 | tf_op jit(solution)/shard_map/ppermute | solution.py:458
  67.1 4.6 %collective-permute-start.8 = (f32[8,384]{1,0:T(8,128)S(1)}, f32[8,384]{1,0:T(8,128)S(1)}, u32[]{:S(2)}, u32[]{:S(2)}) collective-permute-start(f32[8,384]{1,0:T(8,128)S(1)} %get-tuple-element.41.refs_0_), channel_id=1, source_target_pairs={{0,2},{1,3},{2,0},{3,1},{4,6},{5,7},{6,4},{7,5},{8,10},{9,11},{10,... | collective-permute-start | bytes 36872 | tf_op jit(solution)/shard_map/ppermute | solution.py:458
  67.1 5.5 %collective-permute-start.7 = (f32[8,384]{1,0:T(8,128)S(1)}, f32[8,384]{1,0:T(8,128)S(1)}, u32[]{:S(2)}, u32[]{:S(2)}) collective-permute-start(f32[8,384]{1,0:T(8,128)S(1)} %get-tuple-element.41.refs_0_), channel_id=1, source_target_pairs={{0,1},{1,2},{2,3},{3,0},{4,5},{5,6},{6,7},{7,4},{8,9},{9,10},{10,1... | collective-permute-start | bytes 36872 | tf_op jit(solution)/shard_map/ppermute | solution.py:458
  68.5 4.1 %copy-start.14 = (f32[8,384]{1,0:T(8,128)}, f32[8,384]{1,0:T(8,128)S(1)}, u32[]{:S(2)}) copy-start(f32[8,384]{1,0:T(8,128)S(1)} %collective-permute-done.9.refs_3_) | copy-start | bytes 36868
  (7 other events, 6.0 us)

commit v3 on v2

--- a/solution.py
+++ b/solution.py
@@ -15,10 +15,12 @@
 DOC_LINE = 4
 LAST_DOC_ID = 7
 TILE = 256
+CHAINS = 2
 F32 = jnp.float32
 BF16 = jnp.bfloat16
 HIGHEST = lax.Precision.HIGHEST
 IN_VMEM = pl.BlockSpec(memory_space=pltpu.VMEM)
+IN_HBM = pl.BlockSpec(memory_space=pltpu.HBM)
 PARAMS = pltpu.CompilerParams(vmem_limit_bytes=48 << 20)
 
 
@@ -69,26 +71,39 @@
     return sum(math.prod(s.shape) * jnp.dtype(s.dtype).itemsize for s in shapes)
 
 
-def pack_kernel(order, me_ref, q_ref, k_ref, v_ref, *out_refs):
-    for d, out_ref in zip(order, out_refs):
+def pack_kernel(order, me_ref, *refs):
+    ins, outs, (held_ref, in_sems, out_sems) = refs[:3], refs[3:-3], refs[-3:]
+    coming, going = [], []
+    for n, d in enumerate(order):
         lanes = pl.ds(pl.multiple_of(lax.bitwise_xor(me_ref[0], d) * LANES, LANES), LANES)
-        for i, ref in enumerate((q_ref, k_ref, v_ref)):
-            out_ref[i] = ref[:, lanes]
-
-
-def pack(me, q, k, v, order, pieces=3):
-    rows, width = q.shape
-    piece = rows // pieces
-    outs = [jax.ShapeDtypeStruct((3, rows, LANES), BF16)] * len(order)
+        for i, ref in enumerate(ins):
+            coming.append(
+                pltpu.make_async_copy(ref.at[:, lanes], held_ref.at[n, i], in_sems.at[3 * n + i])
+            )
+            coming[-1].start()
+    for n, out_ref in enumerate(outs):
+        for copy in coming[3 * n : 3 * n + 3]:
+            copy.wait()
+        going.append(pltpu.make_async_copy(held_ref.at[n], out_ref, out_sems.at[n]))
+        going[-1].start()
+    for copy in going:
+        copy.wait()
+
+
+def pack(me, q, k, v, order):
+    rows = q.shape[0]
+    n = len(order)
+    outs = [jax.ShapeDtypeStruct((3, rows, LANES), BF16)] * n
     return pl.pallas_call(
         functools.partial(pack_kernel, order),
-        grid_spec=pltpu.PrefetchScalarGridSpec(
-            num_scalar_prefetch=1,
-            grid=(pieces,),
-            in_specs=[pl.BlockSpec((piece, width), lambda r, me: (r, 0))] * 3,
-            out_specs=[pl.BlockSpec((3, piece, LANES), lambda r, me: (0, r, 0))] * len(order),
-        ),
+        in_specs=[pl.BlockSpec(memory_space=pltpu.SMEM)] + [IN_HBM] * 3,
+        out_specs=[IN_HBM] * n,
         out_shape=outs,
+        scratch_shapes=[
+            pltpu.VMEM((n, 3, rows, LANES), BF16),
+            pltpu.SemaphoreType.DMA((3 * n,)),
+            pltpu.SemaphoreType.DMA((n,)),
+        ],
         cost_estimate=pl.CostEstimate(flops=0, bytes_accessed=2 * moved(*outs), transcendentals=0),
         name="pack",
     )(me, q, k, v)
@@ -96,89 +111,121 @@
 
 def attend_kernel(order, rows, window, me_ref, *refs):
     came = refs[: len(order)]
-    held_ref, o_ref, q_ref, k_ref, v_ref, s_ref, p_ref, start_ref = refs[len(order) :]
+    held_ref, out_ref, q_ref, k_ref, v_ref, meta_ref, o_ref, s_ref, in_sems, out_sems = refs[
+        len(order) :
+    ]
     parts = len(order)
     per = rows // LANES
     factor = LANES ** (-0.5) * math.log2(math.e)
-    i = pl.program_id(0)
-
-    @pl.when(i == 0)
-    def _():
-        for d, ref in zip(order, came):
-            at = pl.ds(pl.multiple_of(lax.bitwise_xor(me_ref[0], d) * rows, LANES), rows)
-            q_ref[at, :] = ref[0]
-            k_ref[at, :] = ref[1]
-            v_ref[at, :LANES] = ref[2]
-        v_ref[:, LANES:] = jnp.ones((parts * rows, LANES), BF16)
-        docs = held_ref[:, LANES : LANES + META, :].astype(F32)
-        line = lax.broadcasted_iota(jnp.int32, docs.shape, 1)
-        used = (line >= DOC_LINE) & (line < DOC_LINE + per)
-        for d in range(LAST_DOC_ID):
-            start_ref[d] = jnp.sum(jnp.where(used & (docs < d + 1), 1.0, 0.0)).astype(jnp.int32)
+    meta_copy = pltpu.make_async_copy(
+        held_ref.at[:, pl.ds(LANES, META), :], meta_ref, in_sems.at[3 * parts]
+    )
+    meta_copy.start()
+    copies = []
+    for n, (d, ref) in enumerate(zip(order, came)):
+        at = pl.ds(pl.multiple_of(lax.bitwise_xor(me_ref[0], d) * rows, LANES), rows)
+        for j, target in enumerate((q_ref.at[at], k_ref.at[at], v_ref.at[at, pl.ds(0, LANES)])):
+            copies.append(pltpu.make_async_copy(ref.at[j], target, in_sems.at[3 * n + j]))
+            copies[-1].start()
+    v_ref[:, LANES:] = jnp.ones((parts * rows, LANES), BF16)
+    meta_copy.wait()
+    docs = meta_ref[...].astype(F32)
+    line = lax.broadcasted_iota(jnp.int32, docs.shape, 1)
+    used = (line >= DOC_LINE) & (line < DOC_LINE + per)
+    starts = [
+        jnp.sum(jnp.where(used & (docs < d), 1.0, 0.0)).astype(jnp.int32)
+        for d in range(1, LAST_DOC_ID + 1)
+    ]
+    for copy in copies:
+        copy.wait()
 
     wide = (TILE, LANES)
     lane = lax.broadcasted_iota(jnp.int32, wide, 1)
     sub = lax.broadcasted_iota(jnp.int32, wide, 0)
-    first = pl.multiple_of(i * TILE, TILE)
-    low, high = 0, 0
-    for d in range(LAST_DOC_ID):
-        low = jnp.where(first >= start_ref[d], start_ref[d], low)
-        high = jnp.where(first + TILE - 1 >= start_ref[d], start_ref[d], high)
-    count = i - low // TILE + 1
-
-    def run(n, mixed):
-        base = pl.multiple_of((i - (n - 1)) * TILE, TILE)
-        keys = pl.ds(base, n * TILE)
-        queries = q_ref[pl.ds(first, TILE), :]
-        if mixed:
-            begin = jnp.zeros(wide, jnp.int32)
-            for d in range(LAST_DOC_ID):
-                begin = jnp.where(sub >= start_ref[d] - first, start_ref[d], begin)
-            begin = begin - lane
-        else:
-            begin = low - lane
-        top = jnp.full(wide, MASKED, F32)
-        scores = nt_dot(queries, k_ref[keys, :])
-        for c in range(n * TILE // LANES):
-            at = head_at(c)
-            piece = scores[:, at]
-            if mixed or c < TILE // LANES:
-                piece = jnp.where(begin <= base + c * LANES, piece, MASKED)
-            ahead = c * LANES - (n - 1) * TILE
-            if ahead >= 0:
-                piece = jnp.where(lane - sub <= -ahead, piece, MASKED)
-            top = jnp.maximum(top, piece)
-            s_ref[:, at] = piece
-        row_max = jnp.max(top, axis=1, keepdims=True) * factor
-        for c in range(n * TILE // LANES):
-            at = head_at(c)
-            p_ref[:, at] = jnp.exp2(s_ref[:, at] * factor - row_max).astype(BF16)
-        total = jnp.dot(p_ref[:, : n * TILE], v_ref[keys, :], preferred_element_type=F32)
-        o_ref[...] = (total[:, :LANES] / total[:, LANES:]).astype(BF16)
-
-    for n in range(1, window + 1):
-        pl.when((count == n) & (low == high))(functools.partial(run, n, False))
-        pl.when((count == n) & (low != high))(functools.partial(run, n, True))
+    step = CHAINS * TILE
+
+    def body(i, carry):
+        first = pl.multiple_of(i * step, step)
+        low = 0
+        for s in starts:
+            low = jnp.where(first >= s, s, low)
+        count = (i + 1) * CHAINS - low // TILE
+
+        def run(n):
+            base = pl.multiple_of(first + step - n * TILE, TILE)
+            tops = {}
+
+            def score(chain):
+                tiles = n - CHAINS + 1 + chain
+                mine = pl.multiple_of(first + chain * TILE, TILE)
+                keys = pl.ds(base, tiles * TILE)
+                begin = jnp.zeros(wide, jnp.int32)
+                for s in starts:
+                    begin = jnp.where(sub >= s - mine, s, begin)
+                begin = begin - base - lane
+                top = jnp.full(wide, MASKED, F32)
+                queries = q_ref[pl.ds(mine, TILE), :]
+                for c in range(tiles * TILE // LANES):
+                    at = head_at(c)
+                    if c % 2 == 0:
+                        scores = nt_dot(queries, k_ref[pl.ds(pl.multiple_of(base + c * LANES, LANES), 2 * LANES), :])
+                    piece = jnp.where(begin <= c * LANES, scores[:, head_at(c % 2)], MASKED)
+                    ahead = c * LANES - (tiles - 1) * TILE
+                    if ahead >= 0:
+                        piece = jnp.where(lane - sub <= -ahead, piece, MASKED)
+                    top = jnp.maximum(top, piece)
+                    s_ref[chain, :, at] = piece
+                tops[chain] = jnp.max(top, axis=1, keepdims=True) * factor
+
+            def mix(chain):
+                tiles = n - CHAINS + 1 + chain
+                mine = pl.multiple_of(first + chain * TILE, TILE)
+                row_max = tops[chain]
+                total = jnp.zeros((TILE, 2 * LANES), F32)
+                for t in range(tiles):
+                    at = slice(t * TILE, (t + 1) * TILE)
+                    p = jnp.exp2(s_ref[chain, :, at] * factor - row_max).astype(BF16)
+                    keys = pl.ds(pl.multiple_of(base + t * TILE, TILE), TILE)
+                    total = total + jnp.dot(p, v_ref[keys, :], preferred_element_type=F32)
+                o_ref[pl.ds(mine, TILE), :] = (total[:, :LANES] / total[:, LANES:]).astype(BF16)
+
+            for chain in range(CHAINS):
+                score(chain)
+            for chain in range(CHAINS):
+                mix(chain)
+
+        for n in range(CHAINS, window + CHAINS):
+            pl.when(count == n)(functools.partial(run, n))
+        at = pl.ds(first, step)
+        pltpu.make_async_copy(o_ref.at[at], out_ref.at[at], out_sems.at[i]).start()
+        return carry
+
+    blocks = parts * rows // step
+    lax.fori_loop(0, blocks, body, 0)
+    for i in range(blocks):
+        at = pl.ds(i * step, step)
+        pltpu.make_async_copy(o_ref.at[at], out_ref.at[at], out_sems.at[i]).wait()
 
 
 def attend(me, came, held, order, longest):
     rows = came[0].shape[1]
     tokens = len(order) * rows
-    window = min((longest - 1 + TILE - 1) // TILE + 1, tokens // TILE)
+    window = min((longest - 1 + TILE - 1) // TILE + 1, tokens // TILE - CHAINS + 1)
     out = jax.ShapeDtypeStruct((tokens, LANES), BF16)
     return pl.pallas_call(
         functools.partial(attend_kernel, order, rows, window),
-        grid=(tokens // TILE,),
-        in_specs=[pl.BlockSpec(memory_space=pltpu.SMEM)] + [IN_VMEM] * (len(order) + 1),
-        out_specs=pl.BlockSpec((TILE, LANES), lambda i: (i, 0)),
+        in_specs=[pl.BlockSpec(memory_space=pltpu.SMEM)] + [IN_HBM] * (len(order) + 1),
+        out_specs=IN_HBM,
         out_shape=out,
         scratch_shapes=[
             pltpu.VMEM((tokens, LANES), BF16),
             pltpu.VMEM((tokens, LANES), BF16),
             pltpu.VMEM((tokens, 2 * LANES), BF16),
-            pltpu.VMEM((TILE, window * TILE), F32),
-            pltpu.VMEM((TILE, window * TILE), BF16),
-            pltpu.SMEM((LAST_DOC_ID,), jnp.int32),
+            pltpu.VMEM((len(order), META, LANES), BF16),
+            pltpu.VMEM((tokens, LANES), BF16),
+            pltpu.VMEM((CHAINS, TILE, (window + CHAINS - 1) * TILE), F32),
+            pltpu.SemaphoreType.DMA((3 * len(order) + 1,)),
+            pltpu.SemaphoreType.DMA((tokens // (CHAINS * TILE),)),
         ],
         cost_estimate=pl.CostEstimate(
             flops=2 * tokens * longest * LANES * 2,
@@ -257,31 +304,36 @@
     )(gates, doc_row, k, v)
 
 
-def carry_kernel(held_ref, out_ref):
-    parts = held_ref.shape[0]
+def carry_kernel(came_ref, out_ref, held_ref, sems):
+    parts = came_ref.shape[0]
+    copies = [pltpu.make_async_copy(came_ref.at[j], held_ref.at[j], sems.at[j]) for j in range(parts)]
+    for copy in copies:
+        copy.start()
     line = lax.broadcasted_iota(jnp.int32, (META, LANES), 0)
     state = jnp.zeros((LANES, LANES), F32)
     before = jnp.full((1, LANES), -1.0, F32)
     for j in range(parts):
         out_ref[j, :LANES] = state.astype(BF16)
         out_ref[j, LANES:] = jnp.where(line == 3, before, 0.0).astype(BF16)
+        copies[j].wait()
         meta = held_ref[j, LANES:].astype(F32)
         through = jnp.where(meta[2:3] == before, meta[0:1] + meta[1:2], 0.0)
         state = state * through + held_ref[j, :LANES].astype(F32)
         before = meta[3:4]
 
 
-def carry(held):
+def carry(came):
     return pl.pallas_call(
         carry_kernel,
-        in_specs=[IN_VMEM],
+        in_specs=[IN_HBM],
         out_specs=IN_VMEM,
-        out_shape=jax.ShapeDtypeStruct(held.shape, BF16),
+        out_shape=jax.ShapeDtypeStruct(came.shape, BF16),
+        scratch_shapes=[pltpu.VMEM(came.shape, BF16), pltpu.SemaphoreType.DMA((came.shape[0],))],
         cost_estimate=pl.CostEstimate(
-            flops=2 * held.size, bytes_accessed=2 * moved(held), transcendentals=0
+            flops=2 * came.size, bytes_accessed=2 * moved(came), transcendentals=0
         ),
         name="carry",
-    )(held)
+    )(came)
 
 
 def carry_gathered(block):
@@ -301,7 +353,9 @@
     return jnp.concatenate([state, tail], axis=1).astype(BF16)
 
 
-def inside_kernel(cum_ref, doc_ref, q_ref, k_ref, v_ref, raw_ref, column_ref, bias_ref):
+def inside_kernel(cum_ref, doc_ref, q_hbm, k_ref, v_ref, raw_ref, q_ref, sem, column_ref, bias_ref):
+    copy = pltpu.make_async_copy(q_hbm, q_ref, sem)
+    copy.start()
     heads, rows = cum_ref.shape
     count = rows // LANES
     column_ref[...] = columns(cum_ref[...])
@@ -314,6 +368,7 @@
             ok = doc_column == doc[:, head_at(b)]
             ok = ok & upto if a == b else ok
             bias_ref[head_at(a), head_at(b)] = jnp.where(ok, 0.0, MASKED)
+    copy.wait()
     for h in range(heads):
         at = head_at(h)
         row = cum_ref[h : h + 1, :]
@@ -333,10 +388,15 @@
     out = jax.ShapeDtypeStruct(q.shape, F32)
     return pl.pallas_call(
         inside_kernel,
-        in_specs=[IN_VMEM] * 5,
+        in_specs=[IN_VMEM, IN_VMEM, IN_HBM, IN_VMEM, IN_VMEM],
         out_specs=IN_VMEM,
         out_shape=out,
-        scratch_shapes=[pltpu.VMEM(q.shape, F32), pltpu.VMEM((rows, rows), F32)],
+        scratch_shapes=[
+            pltpu.VMEM(q.shape, BF16),
+            pltpu.SemaphoreType.DMA,
+            pltpu.VMEM(q.shape, F32),
+            pltpu.VMEM((rows, rows), F32),
+        ],
         cost_estimate=pl.CostEstimate(
             flops=3 * heads * rows * rows * LANES,
             bytes_accessed=moved(q, k, v, out),
@@ -347,7 +407,9 @@
     )(cumulated, doc_row, q, k, v)
 
 
-def incoming_kernel(cum_ref, doc_ref, q_ref, before_ref, raw_ref, out_ref, square_ref):
+def incoming_kernel(cum_ref, doc_ref, q_hbm, before_ref, raw_ref, out_ref, square_ref, q_ref, sem):
+    copy = pltpu.make_async_copy(q_hbm, q_ref, sem)
+    copy.start()
     heads, rows = cum_ref.shape
     factor = columns(jnp.exp(cum_ref[...]))
     doc = doc_ref[...].astype(F32)
@@ -357,6 +419,7 @@
         axis=0,
     )
     total = jnp.zeros((rows, LANES), F32)
+    copy.wait()
     for h in range(heads):
         at = head_at(h)
         came = jnp.dot(q_ref[:, at], before_ref[h, :LANES], preferred_element_type=F32)
@@ -371,9 +434,10 @@
     outs = [jax.ShapeDtypeStruct(q.shape, F32), jax.ShapeDtypeStruct((8, rows), F32)]
     return pl.pallas_call(
         incoming_kernel,
-        in_specs=[IN_VMEM] * 5,
+        in_specs=[IN_VMEM, IN_VMEM, IN_HBM, IN_VMEM, IN_VMEM],
         out_specs=[IN_VMEM] * 2,
         out_shape=outs,
+        scratch_shapes=[pltpu.VMEM(q.shape, BF16), pltpu.SemaphoreType.DMA],
         cost_estimate=pl.CostEstimate(
             flops=2 * heads * rows * LANES * LANES,
             bytes_accessed=moved(q, before, raw, *outs),
@@ -385,30 +449,40 @@
 
 
 def normalize_kernel(features, raw_ref, gain_ref, *refs):
-    *squares, out_ref = refs
+    *squares, out_ref, made_ref, sems = refs
     total = squares[0][...]
     for ref in squares[1:]:
         total = total + ref[...]
-    scale = column_of(lax.rsqrt(total / features + EPSILON)[0:1])
-    for h in range(raw_ref.shape[1] // LANES):
-        at = head_at(h)
-        out_ref[:, at] = (raw_ref[:, at] * scale * gain_ref[:, at]).astype(BF16)
+    scale = lax.rsqrt(total / features + EPSILON)
+    copies = []
+    for a in range(raw_ref.shape[0] // LANES):
+        lines = head_at(a)
+        column = column_of(scale[0:1, lines])
+        for h in range(raw_ref.shape[1] // LANES):
+            at = head_at(h)
+            made_ref[lines, at] = (raw_ref[lines, at] * column * gain_ref[:, at]).astype(BF16)
+        copies.append(pltpu.make_async_copy(made_ref.at[lines], out_ref.at[lines], sems.at[a]))
+        copies[-1].start()
+    for copy in copies:
+        copy.wait()
 
 
 def normalize(raw, gain_row, squares, features):
     rows, width = raw.shape
-    line = pl.BlockSpec((LANES, width), lambda r: (r, 0))
     out = jax.ShapeDtypeStruct((rows, width), BF16)
     return pl.pallas_call(
         functools.partial(normalize_kernel, features),
-        grid=(rows // LANES,),
-        in_specs=[line, pl.BlockSpec((1, width), lambda r: (0, 0))]
-        + [pl.BlockSpec((8, LANES), lambda r: (0, r))] * len(squares),
-        out_specs=line,
+        in_specs=[IN_VMEM] * (2 + len(squares)),
+        out_specs=IN_HBM,
         out_shape=out,
+        scratch_shapes=[
+            pltpu.VMEM((rows, width), BF16),
+            pltpu.SemaphoreType.DMA((rows // LANES,)),
+        ],
         cost_estimate=pl.CostEstimate(
             flops=3 * raw.size, bytes_accessed=moved(raw, out), transcendentals=rows
         ),
+        compiler_params=PARAMS,
         name="normalize",
     )(raw, gain_row, *squares)
 
@@ -432,17 +506,19 @@
             return lax.ppermute(x, "ctx", [(i, i ^ d) for i in range(size)])
 
         order = [d for d in range(size - 2, 0, -2)] + [d for d in range(size - 1, 0, -2)] + [0]
-        early = size // 2 - 1
+        first, second = size // 2 - 1, size // 2 + 1
         sent = pack(me, q_soft, k_soft, v_soft, order)
-        came = [swap(sent[i], order[i]) for i in range(early)]
+        came = [swap(x, d) for x, d in zip(sent[:first], order)]
         states, cumulated = local_state(after(k_lin, sent[-1]), v_lin, gate_log, doc_row)
         held_states = exchange(states)
-        late, _ = lax.optimization_barrier((sent[early:-1], states))
-        came += [swap(x, d) for x, d in zip(late, order[early:])]
+        middle, _ = lax.optimization_barrier((sent[first:second], states))
+        came += [swap(x, d) for x, d in zip(middle, order[first:])]
+        raw = inside(after(q_lin, states), k_lin, v_lin, cumulated, doc_row)
+        late, _, held_states = lax.optimization_barrier((sent[second:-1], raw, held_states))
+        came += [swap(x, d) for x, d in zip(late, order[second:])]
         passed = carry(held_states)
         before = exchange(passed)
-        raw = inside(after(q_lin, passed), k_lin, v_lin, cumulated, doc_row)
-        mixed = attend(me, [*came, after(sent[-1], raw)], held_states, order, rows * size // 2)
+        mixed = attend(me, [*came, after(sent[-1], passed)], held_states, order, rows * size // 2)
         back = exchange(mixed.reshape(size, rows, LANES))
         raw, square = incoming(q_lin, cumulated, doc_row, after(before, mixed), raw)
         soft_out = back.transpose(1, 0, 2).reshape(rows, heads * LANES)

time: 79.5 us -> 67.9 us (0.85)
  Pallas kernels: 29.1 us -> 21 us
  starting transfers between devices: 30 us -> 25.6 us
  waiting for transfers between devices: 11.5 us -> 14.6 us
  local copies, waits for them, and re-layouts: 7.24 us -> 5.23 us
    pallas_call x6, Pallas kernels: 27.7 us -> 19.6 us  [the longest x1 8.51 us: attend(): pl.pallas_call(functools.partial(attend_kernel, order, rows, window), in_...]
    ppermute x3, starting transfers between devices: 9.11 us -> 4.69 us  [on_device(): squares.append(lax.ppermute(square, 'head', turn))]
    all_to_all x3, waiting for transfers between devices: 0.86 us -> 3.84 us  [exchange(): return lax.all_to_all(x, 'ctx', split_axis=0, concat_axis=0, tiled=True)]
    unnamed x36 -> x20, local copies, waits for them, and re-layouts: 5.11 us -> 3.09 us
  transfers between devices with their start and end apart: 13 -> 13, of which waited for: 7 -> 8; matrix products, arithmetic and copies ran while one was open for 0% -> 0% of each run, Pallas kernels for 32% -> 27%
where the time goes in v3:
time: 67.9 us; the launch traced here: 67.2 us
  starting transfers between devices  25.6 us (38%)
  Pallas kernels  21 us (31%)
  waiting for transfers between devices  14.6 us (22%)
  local copies, waits for them, and re-layouts  5.23 us (8%)
  between operations  0.81 us (1%)
    all_to_all x3, starting transfers between devices, exchange(): return lax.all_to_all(x, 'ctx', split_axis=0, concat_axis=0, tiled=True)  11.4 us
    ppermute x7, starting transfers between devices, swap(): return lax.ppermute(x, 'ctx', [(i, i ^ d) for i in range(size)])  9.54 us
    pallas_call x1, Pallas kernels, attend(): pl.pallas_call(functools.partial(attend_kernel, order, rows, window), in_...  8.51 us
    ppermute x7, waiting for transfers between devices, swap(): return lax.ppermute(x, 'ctx', [(i, i ^ d) for i in range(size)])  6.24 us
    ppermute x3, starting transfers between devices, on_device(): squares.append(lax.ppermute(square, 'head', turn))  4.69 us
    ppermute x3, waiting for transfers between devices, on_device(): squares.append(lax.ppermute(square, 'head', turn))  4.47 us
    pallas_call x1, Pallas kernels, inside(): pl.pallas_call(inside_kernel, in_specs=[IN_VMEM, IN_VMEM, IN_HBM, IN_VMEM...  4.23 us
    all_to_all x3, waiting for transfers between devices, exchange(): return lax.all_to_all(x, 'ctx', split_axis=0, concat_axis=0, tiled=True)  3.84 us
  transfers between devices with their start and end apart: 13, of which 8 were waited for; matrix products, arithmetic and copies ran while one was open for 0% of the time, Pallas kernels for 27%

profile of v3, /device:TPU:0, one launch (start us, length us, event | category | flops | bytes accessed | tf_op | source)
XLA Modules:
  0.0 67.2 jit_solution(14194978678270913943)
XLA Ops:
  0.7 2.9 %pack.1 = (bf16[3,384,128]{2,1,0:T(8,128)(2,1)}, bf16[3,384,128]{2,1,0:T(8,128)(2,1)}, bf16[3,384,128]{2,1,0:T(8,128)(2,1)}, bf16[3,384,128]{2,1,0:T(8,128)(2,1)...) custom-call(s32[1]{0:T(128)} %bitcast.me_ref, ...), custom_call_target="tpu_custom_call" | custom-call | bytes 4718592 | tf_op jit(solution)/shard_map/pack/pallas_call | solution.py:97
  3.5 4.0 %collective-permute-start = (bf16[3,384,128]{2,1,0:T(8,128)(2,1)}, bf16[3,384,128]{2,1,0:T(8,128)(2,1)}, u32[]{:S(2)}, u32[]{:S(2)}) collective-permute-start(bf16[3,384,128]{2,1,0:T(8,128)(2,1)} %get-tuple-element.31), channel_id=1, source_target_pairs={{0,24},{4,28},{8,16},{12,20},{16,8},{20,12},{24,0},{28,4},{1,25},{... | collective-permute-start | bytes 884744 | tf_op jit(solution)/shard_map/ppermute | solution.py:506
  8.0 1.4 %local_state.1 = (bf16[8,144,128]{2,1,0:T(8,128)(2,1)}, f32[8,384]{1,0:T(8,128)S(1)}) custom-call(f32[8,384]{1,0:T(8,128)S(1)} %copy-done.6, s32[1,384]{1,0:T(1,128)S(1)} %reshape.19.doc_ref, bf16[384,1024]{1,0:T(8,128)(2,1)S(1)} %copy-done, bf16[384,1024]{1,0:T(8,128)(2,1)S(1)} %copy-done.1), custom_call_target="tpu_custom_call" | custom-call | flops 100663296 | bytes 1892352 | tf_op jit(solution)/shard_map/local_state/pallas_call | solution.py:292
  9.4 3.4 %all-to-all-start = ((bf16[8,144,128]{2,1,0:T(8,128)(2,1)}), bf16[8,144,128]{2,1,0:T(8,128)(2,1)S(1)}, u32[]{:S(2)}, u32[]{:S(2)}) async-start(bf16[8,144,128]{2,1,0:T(8,128)(2,1)} %get-tuple-element.28), calls=%async_computation | async-start | bytes 589824 | tf_op jit(solution)/shard_map/all_to_all | solution.py:495
  12.8 1.9 %collective-permute-start.2 = (bf16[3,384,128]{2,1,0:T(8,128)(2,1)}, bf16[3,384,128]{2,1,0:T(8,128)(2,1)}, u32[]{:S(2)}, u32[]{:S(2)}) collective-permute-start(bf16[3,384,128]{2,1,0:T(8,128)(2,1)} %get-tuple-element.33), channel_id=1, source_target_pairs={{0,8},{4,12},{8,0},{12,4},{16,24},{20,28},{24,16},{28,20},{1,9},{5... | collective-permute-start | bytes 884744 | tf_op jit(solution)/shard_map/ppermute | solution.py:506
  16.1 1.1 %copy-done.2 = bf16[384,1024]{1,0:T(8,128)(2,1)S(1)} copy-done((bf16[384,1024]{1,0:T(8,128)(2,1)S(1)}, bf16[384,1024]{1,0:T(8,128)(2,1)}, u32[]{:S(2)}) %copy-start.2) | copy-done | bytes 786456
  17.2 4.2 %inside.1.raw_ref = f32[384,1024]{1,0:T(8,128)S(1)} custom-call(f32[8,384]{1,0:T(8,128)S(1)} %get-tuple-element.25.cum_ref, s32[1,384]{1,0:T(1,128)S(1)} %reshape.19.doc_ref, bf16[384,1024]{1,0:T(8,128)(2,1)S(1)} %copy-done.2, bf16[384,1024]{1,0:T(8,128)(2,1)S(1)} %copy-done, bf16[384,1024]{1,0:T(8,128)(2,1)S(1)} %copy-done.1), custom_call_target="tpu_custom_call" | custom-call | flops 452984832 | bytes 3932160 | tf_op jit(solution)/shard_map/inside/pallas_call | solution.py:389
  21.5 2.8 %all-to-all-done.came_ref.refs_8_ = bf16[8,144,128]{2,1,0:T(8,128)(2,1)S(1)} async-done(((bf16[8,144,128]{2,1,0:T(8,128)(2,1)}), bf16[8,144,128]{2,1,0:T(8,128)(2,1)S(1)}, u32[]{:S(2)}, u32[]{:S(2)}) %all-to-all-start) | async-done | bytes 294944 | tf_op jit(solution)/shard_map/all_to_all | solution.py:495
  24.3 1.3 %collective-permute-start.5 = (bf16[3,384,128]{2,1,0:T(8,128)(2,1)}, bf16[3,384,128]{2,1,0:T(8,128)(2,1)S(1)}, u32[]{:S(2)}, u32[]{:S(2)}) collective-permute-start(bf16[3,384,128]{2,1,0:T(8,128)(2,1)} %get-tuple-element.38), channel_id=1, source_target_pairs={{0,12},{4,8},{8,4},{12,0},{16,28},{20,24},{24,20},{28,16},{1,13},{... | collective-permute-start | bytes 884744 | tf_op jit(solution)/shard_map/ppermute | solution.py:506
  26.1 1.7 %carry.1 = bf16[8,144,128]{2,1,0:T(8,128)(2,1)} custom-call(bf16[8,144,128]{2,1,0:T(8,128)(2,1)} %copy-done.4), custom_call_target="tpu_custom_call" | custom-call | flops 294912 | bytes 589824 | tf_op jit(solution)/shard_map/carry/pallas_call | solution.py:326
  27.8 3.6 %all-to-all-start.1 = ((bf16[8,144,128]{2,1,0:T(8,128)(2,1)}), bf16[8,144,128]{2,1,0:T(8,128)(2,1)S(1)}, u32[]{:S(2)}, u32[]{:S(2)}) async-start(bf16[8,144,128]{2,1,0:T(8,128)(2,1)} %carry.1), calls=%async_computation.1 | async-start | bytes 589824 | tf_op jit(solution)/shard_map/all_to_all | solution.py:495
  31.4 1.0 %collective-permute-done.3.refs_3_ = bf16[3,384,128]{2,1,0:T(8,128)(2,1)} collective-permute-done((bf16[3,384,128]{2,1,0:T(8,128)(2,1)}, bf16[3,384,128]{2,1,0:T(8,128)(2,1)}, u32[]{:S(2)}, u32[]{:S(2)}) %collective-permute-start.3) | collective-permute-done | bytes 294944 | tf_op jit(solution)/shard_map/ppermute | solution.py:506
  32.4 4.4 %collective-permute-done.4.refs_4_ = bf16[3,384,128]{2,1,0:T(8,128)(2,1)} collective-permute-done((bf16[3,384,128]{2,1,0:T(8,128)(2,1)}, bf16[3,384,128]{2,1,0:T(8,128)(2,1)}, u32[]{:S(2)}, u32[]{:S(2)}) %collective-permute-start.4) | collective-permute-done | bytes 294944 | tf_op jit(solution)/shard_map/ppermute | solution.py:506
  37.7 1.0 %copy-done.5 = bf16[8,144,128]{2,1,0:T(8,128)(2,1)S(1)} copy-done((bf16[8,144,128]{2,1,0:T(8,128)(2,1)S(1)}, bf16[8,144,128]{2,1,0:T(8,128)(2,1)}, u32[]{:S(2)}) %copy-start.5) | copy-done | bytes 294936
  38.6 1.0 %copy-done.8 = bf16[3,384,128]{2,1,0:T(8,128)(2,1)S(1)} copy-done((bf16[3,384,128]{2,1,0:T(8,128)(2,1)S(1)}, bf16[3,384,128]{2,1,0:T(8,128)(2,1)}, u32[]{:S(2)}) %copy-start.8) | copy-done | bytes 294936
  39.6 8.5 %attend.1 = bf16[3072,128]{1,0:T(8,128)(2,1)} custom-call(s32[1]{0:T(128)} %bitcast.me_ref, bf16[3,384,128]{2,1,0:T(8,128)(2,1)} %collective-permute-done.refs_0_, bf16[3,384,128]{2,1,0:T(8,128)(2,1)} %collective-permute-done.1.refs_1_, bf16[3,384,128]{2,1,0:T(8,128)(2,1)} %collective-permute-done.2.refs_2_, ...), custom_call_target="tpu_custom_call" | custom-call | flops 2415919104 | bytes 3440640 | tf_op jit(solution)/shard_map/attend/pallas_call | solution.py:215
  48.1 4.4 %all-to-all-start.2 = ((bf16[8,384,128]{2,1,0:T(8,128)(2,1)}), bf16[8,384,128]{2,1,0:T(8,128)(2,1)}, u32[]{:S(2)}, u32[]{:S(2)}) async-start(bf16[8,384,128]{2,1,0:T(8,128)(2,1)} %bitcast.2), calls=%async_computation.2 | async-start | bytes 1572864 | tf_op jit(solution)/shard_map/all_to_all | solution.py:495
  52.5 1.3 %incoming.1 = (f32[384,1024]{1,0:T(8,128)S(1)}, f32[8,384]{1,0:T(8,128)S(1)}) custom-call(f32[8,384]{1,0:T(8,128)S(1)} %get-tuple-element.25.cum_ref, s32[1,384]{1,0:T(1,128)S(1)} %reshape.19.doc_ref, bf16[384,1024]{1,0:T(8,128)(2,1)S(1)} %copy-done.3, bf16[8,144,128]{2,1,0:T(8,128)(2,1)S(1)} %all-to-all-done.1.before_ref, f32[384,1024]{1,0:T(8,128)S(1)} %inside.1.raw_ref), custom_call_target="tpu_custom_call" | custom-call | flops 100663296 | bytes 4239360 | tf_op jit(solution)/shard_map/incoming/pallas_call | solution.py:435
  53.8 3.7 %collective-permute-start.9 = (f32[8,384]{1,0:T(8,128)S(1)}, f32[8,384]{1,0:T(8,128)S(1)}, u32[]{:S(2)}, u32[]{:S(2)}) collective-permute-start(f32[8,384]{1,0:T(8,128)S(1)} %get-tuple-element.43.refs_0_), channel_id=1, source_target_pairs={{0,3},{1,0},{2,1},{3,2},{4,7},{5,4},{6,5},{7,6},{8,11},{9,8},{10,9... | collective-permute-start | bytes 36872 | tf_op jit(solution)/shard_map/ppermute | solution.py:534
  57.5 1.0 %collective-permute-start.7 = (f32[8,384]{1,0:T(8,128)S(1)}, f32[8,384]{1,0:T(8,128)S(1)}, u32[]{:S(2)}, u32[]{:S(2)}) collective-permute-start(f32[8,384]{1,0:T(8,128)S(1)} %get-tuple-element.43.refs_0_), channel_id=1, source_target_pairs={{0,1},{1,2},{2,3},{3,0},{4,5},{5,6},{6,7},{7,4},{8,9},{9,10},{10,1... | collective-permute-start | bytes 36872 | tf_op jit(solution)/shard_map/ppermute | solution.py:534
  58.9 3.3 %collective-permute-done.8.refs_2_ = f32[8,384]{1,0:T(8,128)S(1)} collective-permute-done((f32[8,384]{1,0:T(8,128)S(1)}, f32[8,384]{1,0:T(8,128)S(1)}, u32[]{:S(2)}, u32[]{:S(2)}) %collective-permute-start.8) | collective-permute-done | bytes 12320 | tf_op jit(solution)/shard_map/ppermute | solution.py:534
  63.0 1.1 %normalize.1 = bf16[384,1024]{1,0:T(8,128)(2,1)} custom-call(f32[384,1024]{1,0:T(8,128)S(1)} %get-tuple-element.42.raw_ref, f32[1,1024]{1,0:T(1,128)S(1)} %bitcast.9, f32[8,384]{1,0:T(8,128)S(1)} %get-tuple-element.43.refs_0_, f32[8,384]{1,0:T(8,128)S(1)} %collective-permute-done.7.refs_1_, f32[8,384]{1,0:T(8,128)S(1)} %collective-permute-done.8.refs_2_, ...), custom_call_target="tpu_custom_call" | custom-call | flops 1179648 | bytes 2359296 | tf_op jit(solution)/shard_map/normalize/pallas_call | solution.py:473
  64.1 1.0 %all-to-all-done.2 = bf16[8,384,128]{2,1,0:T(8,128)(2,1)} async-done(((bf16[8,384,128]{2,1,0:T(8,128)(2,1)}), bf16[8,384,128]{2,1,0:T(8,128)(2,1)}, u32[]{:S(2)}, u32[]{:S(2)}) %all-to-all-start.2) | async-done | bytes 786464 | tf_op jit(solution)/shard_map/all_to_all | solution.py:495
  65.1 2.1 %copy_bitcast_fusion = bf16[384,1024]{1,0:T(8,128)(2,1)} fusion(bf16[8,384,128]{2,1,0:T(8,128)(2,1)} %all-to-all-done.2), kind=kLoop, calls=%fused_computation | loop fusion | bytes 1572864 | tf_op jit(solution)/shard_map/reshape | solution.py:524
  (31 shorter events, 4.4 us)
Async XLA Ops:
  0.6 7.4 %copy-start.9 = (s32[384]{0:T(512)S(1)}, s32[384]{0:T(512)}, u32[]{:S(2)}) copy-start(s32[384]{0:T(512)} %param.17) | copy-start | bytes 4612
  0.6 7.4 %copy-start = (bf16[384,1024]{1,0:T(8,128)(2,1)S(1)}, bf16[384,1024]{1,0:T(8,128)(2,1)}, u32[]{:S(2)}) copy-start(bf16[384,1024]{1,0:T(8,128)(2,1)} %k_ref.2) | copy-start | bytes 2359300
  0.7 7.4 %copy-start.1 = (bf16[384,1024]{1,0:T(8,128)(2,1)S(1)}, bf16[384,1024]{1,0:T(8,128)(2,1)}, u32[]{:S(2)}) copy-start(bf16[384,1024]{1,0:T(8,128)(2,1)} %v_ref.3) | copy-start | bytes 2359300
  0.7 7.4 %copy-start.6 = (f32[8,384]{1,0:T(8,128)S(1)}, f32[8,384]{1,0:T(8,128)}, u32[]{:S(2)}) copy-start(f32[8,384]{1,0:T(8,128)} %gate_ref.1) | copy-start | bytes 36868
  3.5 20.8 %collective-permute-start = (bf16[3,384,128]{2,1,0:T(8,128)(2,1)}, bf16[3,384,128]{2,1,0:T(8,128)(2,1)}, u32[]{:S(2)}, u32[]{:S(2)}) collective-permute-start(bf16[3,384,128]{2,1,0:T(8,128)(2,1)} %get-tuple-element.31), channel_id=1, source_target_pairs={{0,24},{4,28},{8,16},{12,20},{16,8},{20,12},{24,0},{28,4},{1,25},{... | collective-permute-start | bytes 884744 | tf_op jit(solution)/shard_map/ppermute | solution.py:506
  7.5 18.1 %collective-permute-start.1 = (bf16[3,384,128]{2,1,0:T(8,128)(2,1)}, bf16[3,384,128]{2,1,0:T(8,128)(2,1)}, u32[]{:S(2)}, u32[]{:S(2)}) collective-permute-start(bf16[3,384,128]{2,1,0:T(8,128)(2,1)} %get-tuple-element.32), channel_id=1, source_target_pairs={{0,16},{4,20},{8,24},{12,28},{16,0},{20,4},{24,8},{28,12},{1,17},{... | collective-permute-start | bytes 884744 | tf_op jit(solution)/shard_map/ppermute | solution.py:506
  9.4 14.9 %all-to-all-start = ((bf16[8,144,128]{2,1,0:T(8,128)(2,1)}), bf16[8,144,128]{2,1,0:T(8,128)(2,1)S(1)}, u32[]{:S(2)}, u32[]{:S(2)}) async-start(bf16[8,144,128]{2,1,0:T(8,128)(2,1)} %get-tuple-element.28), calls=%async_computation | async-start | bytes 589824 | tf_op jit(solution)/shard_map/all_to_all | solution.py:495
  12.8 18.6 %collective-permute-start.2 = (bf16[3,384,128]{2,1,0:T(8,128)(2,1)}, bf16[3,384,128]{2,1,0:T(8,128)(2,1)}, u32[]{:S(2)}, u32[]{:S(2)}) collective-permute-start(bf16[3,384,128]{2,1,0:T(8,128)(2,1)} %get-tuple-element.33), channel_id=1, source_target_pairs={{0,8},{4,12},{8,0},{12,4},{16,24},{20,28},{24,16},{28,20},{1,9},{5... | collective-permute-start | bytes 884744 | tf_op jit(solution)/shard_map/ppermute | solution.py:506
  14.8 17.7 %collective-permute-start.3 = (bf16[3,384,128]{2,1,0:T(8,128)(2,1)}, bf16[3,384,128]{2,1,0:T(8,128)(2,1)}, u32[]{:S(2)}, u32[]{:S(2)}) collective-permute-start(bf16[3,384,128]{2,1,0:T(8,128)(2,1)} %get-tuple-element.36), channel_id=1, source_target_pairs={{0,28},{4,24},{8,20},{12,16},{16,12},{20,8},{24,4},{28,0},{1,29},{... | collective-permute-start | bytes 884744 | tf_op jit(solution)/shard_map/ppermute | solution.py:506
  15.7 21.1 %collective-permute-start.4 = (bf16[3,384,128]{2,1,0:T(8,128)(2,1)}, bf16[3,384,128]{2,1,0:T(8,128)(2,1)}, u32[]{:S(2)}, u32[]{:S(2)}) collective-permute-start(bf16[3,384,128]{2,1,0:T(8,128)(2,1)} %get-tuple-element.37), channel_id=1, source_target_pairs={{0,20},{4,16},{8,28},{12,24},{16,4},{20,0},{24,12},{28,8},{1,21},{... | collective-permute-start | bytes 884744 | tf_op jit(solution)/shard_map/ppermute | solution.py:506
  16.1 1.1 %copy-start.2 = (bf16[384,1024]{1,0:T(8,128)(2,1)S(1)}, bf16[384,1024]{1,0:T(8,128)(2,1)}, u32[]{:S(2)}) copy-start(bf16[384,1024]{1,0:T(8,128)(2,1)} %q_hbm.2) | copy-start | bytes 2359300
  24.3 1.8 %copy-start.4 = (bf16[8,144,128]{2,1,0:T(8,128)(2,1)}, bf16[8,144,128]{2,1,0:T(8,128)(2,1)S(1)}, u32[]{:S(2)}) copy-start(bf16[8,144,128]{2,1,0:T(8,128)(2,1)S(1)} %all-to-all-done.came_ref.refs_8_) | copy-start | bytes 884740
  24.3 13.4 %collective-permute-start.5 = (bf16[3,384,128]{2,1,0:T(8,128)(2,1)}, bf16[3,384,128]{2,1,0:T(8,128)(2,1)S(1)}, u32[]{:S(2)}, u32[]{:S(2)}) collective-permute-start(bf16[3,384,128]{2,1,0:T(8,128)(2,1)} %get-tuple-element.38), channel_id=1, source_target_pairs={{0,12},{4,8},{8,4},{12,0},{16,28},{20,24},{24,20},{28,16},{1,13},{... | collective-permute-start | bytes 884744 | tf_op jit(solution)/shard_map/ppermute | solution.py:506
  25.6 12.0 %collective-permute-start.6 = (bf16[3,384,128]{2,1,0:T(8,128)(2,1)}, bf16[3,384,128]{2,1,0:T(8,128)(2,1)S(1)}, u32[]{:S(2)}, u32[]{:S(2)}) collective-permute-start(bf16[3,384,128]{2,1,0:T(8,128)(2,1)} %get-tuple-element.39), channel_id=1, source_target_pairs={{0,4},{4,0},{8,12},{12,8},{16,20},{20,16},{24,28},{28,24},{1,5},{5... | collective-permute-start | bytes 884744 | tf_op jit(solution)/shard_map/ppermute | solution.py:506
  27.8 20.3 %all-to-all-start.1 = ((bf16[8,144,128]{2,1,0:T(8,128)(2,1)}), bf16[8,144,128]{2,1,0:T(8,128)(2,1)S(1)}, u32[]{:S(2)}, u32[]{:S(2)}) async-start(bf16[8,144,128]{2,1,0:T(8,128)(2,1)} %carry.1), calls=%async_computation.1 | async-start | bytes 589824 | tf_op jit(solution)/shard_map/all_to_all | solution.py:495
  37.7 1.0 %copy-start.5 = (bf16[8,144,128]{2,1,0:T(8,128)(2,1)S(1)}, bf16[8,144,128]{2,1,0:T(8,128)(2,1)}, u32[]{:S(2)}) copy-start(bf16[8,144,128]{2,1,0:T(8,128)(2,1)} %copy-done.4) | copy-start | bytes 884740
  38.6 1.0 %copy-start.8 = (bf16[3,384,128]{2,1,0:T(8,128)(2,1)S(1)}, bf16[3,384,128]{2,1,0:T(8,128)(2,1)}, u32[]{:S(2)}) copy-start(bf16[3,384,128]{2,1,0:T(8,128)(2,1)} %get-tuple-element.40.refs_7_) | copy-start | bytes 884740
  48.1 4.4 %copy-start.3 = (bf16[384,1024]{1,0:T(8,128)(2,1)S(1)}, bf16[384,1024]{1,0:T(8,128)(2,1)}, u32[]{:S(2)}) copy-start(bf16[384,1024]{1,0:T(8,128)(2,1)} %q_hbm.2) | copy-start | bytes 2359300
  48.1 17.0 %all-to-all-start.2 = ((bf16[8,384,128]{2,1,0:T(8,128)(2,1)}), bf16[8,384,128]{2,1,0:T(8,128)(2,1)}, u32[]{:S(2)}, u32[]{:S(2)}) async-start(bf16[8,384,128]{2,1,0:T(8,128)(2,1)} %bitcast.2), calls=%async_computation.2 | async-start | bytes 1572864 | tf_op jit(solution)/shard_map/all_to_all | solution.py:495
  52.5 10.5 %copy-start.7 = (f32[1024]{0:T(1024)S(1)}, f32[1024]{0:T(1024)}, u32[]{:S(2)}) copy-start(f32[1024]{0:T(1024)} %param.13) | copy-start | bytes 12292
  53.8 5.1 %collective-permute-start.9 = (f32[8,384]{1,0:T(8,128)S(1)}, f32[8,384]{1,0:T(8,128)S(1)}, u32[]{:S(2)}, u32[]{:S(2)}) collective-permute-start(f32[8,384]{1,0:T(8,128)S(1)} %get-tuple-element.43.refs_0_), channel_id=1, source_target_pairs={{0,3},{1,0},{2,1},{3,2},{4,7},{5,4},{6,5},{7,6},{8,11},{9,8},{10,9... | collective-permute-start | bytes 36872 | tf_op jit(solution)/shard_map/ppermute | solution.py:534
  57.5 4.7 %collective-permute-start.8 = (f32[8,384]{1,0:T(8,128)S(1)}, f32[8,384]{1,0:T(8,128)S(1)}, u32[]{:S(2)}, u32[]{:S(2)}) collective-permute-start(f32[8,384]{1,0:T(8,128)S(1)} %get-tuple-element.43.refs_0_), channel_id=1, source_target_pairs={{0,2},{1,3},{2,0},{3,1},{4,6},{5,7},{6,4},{7,5},{8,10},{9,11},{10,... | collective-permute-start | bytes 36872 | tf_op jit(solution)/shard_map/ppermute | solution.py:534
  57.5 5.5 %collective-permute-start.7 = (f32[8,384]{1,0:T(8,128)S(1)}, f32[8,384]{1,0:T(8,128)S(1)}, u32[]{:S(2)}, u32[]{:S(2)}) collective-permute-start(f32[8,384]{1,0:T(8,128)S(1)} %get-tuple-element.43.refs_0_), channel_id=1, source_target_pairs={{0,1},{1,2},{2,3},{3,0},{4,5},{5,6},{6,7},{7,4},{8,9},{9,10},{10,1... | collective-permute-start | bytes 36872 | tf_op jit(solution)/shard_map/ppermute | solution.py:534

commit v4 on v3

--- a/solution.py
+++ b/solution.py
@@ -16,12 +16,13 @@
 LAST_DOC_ID = 7
 TILE = 256
 CHAINS = 2
+VMEM_MB = 16
 F32 = jnp.float32
 BF16 = jnp.bfloat16
 HIGHEST = lax.Precision.HIGHEST
 IN_VMEM = pl.BlockSpec(memory_space=pltpu.VMEM)
 IN_HBM = pl.BlockSpec(memory_space=pltpu.HBM)
-PARAMS = pltpu.CompilerParams(vmem_limit_bytes=48 << 20)
+PARAMS = pltpu.CompilerParams(vmem_limit_bytes=VMEM_MB << 20)
 
 
 def nt_dot(a, b, precision=None):
@@ -111,16 +112,10 @@
 
 def attend_kernel(order, rows, window, me_ref, *refs):
     came = refs[: len(order)]
-    held_ref, out_ref, q_ref, k_ref, v_ref, meta_ref, o_ref, s_ref, in_sems, out_sems = refs[
-        len(order) :
-    ]
+    doc_ref, out_ref, q_ref, k_ref, v_ref, o_ref, s_ref, in_sems, out_sems = refs[len(order) :]
     parts = len(order)
     per = rows // LANES
     factor = LANES ** (-0.5) * math.log2(math.e)
-    meta_copy = pltpu.make_async_copy(
-        held_ref.at[:, pl.ds(LANES, META), :], meta_ref, in_sems.at[3 * parts]
-    )
-    meta_copy.start()
     copies = []
     for n, (d, ref) in enumerate(zip(order, came)):
         at = pl.ds(pl.multiple_of(lax.bitwise_xor(me_ref[0], d) * rows, LANES), rows)
@@ -128,8 +123,7 @@
             copies.append(pltpu.make_async_copy(ref.at[j], target, in_sems.at[3 * n + j]))
             copies[-1].start()
     v_ref[:, LANES:] = jnp.ones((parts * rows, LANES), BF16)
-    meta_copy.wait()
-    docs = meta_ref[...].astype(F32)
+    docs = doc_ref[...].astype(F32)
     line = lax.broadcasted_iota(jnp.int32, docs.shape, 1)
     used = (line >= DOC_LINE) & (line < DOC_LINE + per)
     starts = [
@@ -207,34 +201,78 @@
         pltpu.make_async_copy(o_ref.at[at], out_ref.at[at], out_sems.at[i]).wait()
 
 
-def attend(me, came, held, order, longest):
+def attend(me, came, docs, order, longest):
     rows = came[0].shape[1]
     tokens = len(order) * rows
     window = min((longest - 1 + TILE - 1) // TILE + 1, tokens // TILE - CHAINS + 1)
     out = jax.ShapeDtypeStruct((tokens, LANES), BF16)
     return pl.pallas_call(
         functools.partial(attend_kernel, order, rows, window),
-        in_specs=[pl.BlockSpec(memory_space=pltpu.SMEM)] + [IN_HBM] * (len(order) + 1),
+        in_specs=[pl.BlockSpec(memory_space=pltpu.SMEM)] + [IN_HBM] * len(order) + [IN_VMEM],
         out_specs=IN_HBM,
         out_shape=out,
         scratch_shapes=[
             pltpu.VMEM((tokens, LANES), BF16),
             pltpu.VMEM((tokens, LANES), BF16),
             pltpu.VMEM((tokens, 2 * LANES), BF16),
-            pltpu.VMEM((len(order), META, LANES), BF16),
             pltpu.VMEM((tokens, LANES), BF16),
             pltpu.VMEM((CHAINS, TILE, (window + CHAINS - 1) * TILE), F32),
-            pltpu.SemaphoreType.DMA((3 * len(order) + 1,)),
+            pltpu.SemaphoreType.DMA((3 * len(order),)),
             pltpu.SemaphoreType.DMA((tokens // (CHAINS * TILE),)),
         ],
         cost_estimate=pl.CostEstimate(
             flops=2 * tokens * longest * LANES * 2,
-            bytes_accessed=moved(*came, held, out),
+            bytes_accessed=moved(*came, out),
             transcendentals=tokens * longest // 2,
         ),
         compiler_params=PARAMS,
         name="attend",
-    )(me, *came, held)
+    )(me, *came, docs)
+
+
+def unpack_kernel(came_ref, out_ref, held_ref, in_sems, out_sems):
+    heads, rows = came_ref.shape[0], came_ref.shape[1]
+    pieces = rows // LANES
+    coming = [
+        [
+            pltpu.make_async_copy(
+                came_ref.at[h, head_at(a)], held_ref.at[head_at(a), head_at(h)], in_sems.at[a, h]
+            )
+            for h in range(heads)
+        ]
+        for a in range(pieces)
+    ]
+    going = [
+        pltpu.make_async_copy(held_ref.at[head_at(a)], out_ref.at[head_at(a)], out_sems.at[a])
+        for a in range(pieces)
+    ]
+    for a in range(pieces):
+        for copy in coming[a]:
+            copy.start()
+    for a in range(pieces):
+        for copy in coming[a]:
+            copy.wait()
+        going[a].start()
+    for copy in going:
+        copy.wait()
+
+
+def unpack(came):
+    heads, rows = came.shape[0], came.shape[1]
+    out = jax.ShapeDtypeStruct((rows, heads * LANES), BF16)
+    return pl.pallas_call(
+        unpack_kernel,
+        in_specs=[IN_HBM],
+        out_specs=IN_HBM,
+        out_shape=out,
+        scratch_shapes=[
+            pltpu.VMEM(out.shape, BF16),
+            pltpu.SemaphoreType.DMA((rows // LANES, heads)),
+            pltpu.SemaphoreType.DMA((rows // LANES,)),
+        ],
+        cost_estimate=pl.CostEstimate(flops=0, bytes_accessed=2 * moved(out), transcendentals=0),
+        name="unpack",
+    )(came)
 
 
 def attend_gathered(q, k, v, doc_ids, heads):
@@ -304,7 +342,7 @@
     )(gates, doc_row, k, v)
 
 
-def carry_kernel(came_ref, out_ref, held_ref, sems):
+def carry_kernel(came_ref, out_ref, doc_ref, held_ref, sems):
     parts = came_ref.shape[0]
     copies = [pltpu.make_async_copy(came_ref.at[j], held_ref.at[j], sems.at[j]) for j in range(parts)]
     for copy in copies:
@@ -316,6 +354,7 @@
         out_ref[j, :LANES] = state.astype(BF16)
         out_ref[j, LANES:] = jnp.where(line == 3, before, 0.0).astype(BF16)
         copies[j].wait()
+        doc_ref[j] = held_ref[j, LANES:]
         meta = held_ref[j, LANES:].astype(F32)
         through = jnp.where(meta[2:3] == before, meta[0:1] + meta[1:2], 0.0)
         state = state * through + held_ref[j, :LANES].astype(F32)
@@ -323,15 +362,20 @@
 
 
 def carry(came):
+    parts = came.shape[0]
     return pl.pallas_call(
         carry_kernel,
         in_specs=[IN_HBM],
-        out_specs=IN_VMEM,
-        out_shape=jax.ShapeDtypeStruct(came.shape, BF16),
+        out_specs=[IN_VMEM] * 2,
+        out_shape=[
+            jax.ShapeDtypeStruct(came.shape, BF16),
+            jax.ShapeDtypeStruct((parts, META, LANES), BF16),
+        ],
         scratch_shapes=[pltpu.VMEM(came.shape, BF16), pltpu.SemaphoreType.DMA((came.shape[0],))],
         cost_estimate=pl.CostEstimate(
             flops=2 * came.size, bytes_accessed=2 * moved(came), transcendentals=0
         ),
+        compiler_params=PARAMS,
         name="carry",
     )(came)
 
@@ -513,15 +557,15 @@
         held_states = exchange(states)
         middle, _ = lax.optimization_barrier((sent[first:second], states))
         came += [swap(x, d) for x, d in zip(middle, order[first:])]
-        raw = inside(after(q_lin, states), k_lin, v_lin, cumulated, doc_row)
+        raw = inside(q_lin, k_lin, v_lin, cumulated, doc_row)
         late, _, held_states = lax.optimization_barrier((sent[second:-1], raw, held_states))
         came += [swap(x, d) for x, d in zip(late, order[second:])]
-        passed = carry(held_states)
+        passed, docs = carry(held_states)
         before = exchange(passed)
-        mixed = attend(me, [*came, after(sent[-1], passed)], held_states, order, rows * size // 2)
+        mixed = attend(me, [*came, sent[-1]], docs, order, rows * size // 2)
         back = exchange(mixed.reshape(size, rows, LANES))
         raw, square = incoming(q_lin, cumulated, doc_row, after(before, mixed), raw)
-        soft_out = back.transpose(1, 0, 2).reshape(rows, heads * LANES)
+        soft_out = unpack(back)
     else:
         states, cumulated = local_state(k_lin, v_lin, gate_log, doc_row)
         raw = inside(q_lin, k_lin, v_lin, cumulated, doc_row)

time: 67.9 us -> 67.4 us (level)
  local copies, waits for them, and re-layouts: 5.23 us -> 2.13 us
  Pallas kernels: 21 us -> 23.1 us
    reshape x1 -> x0, local copies, waits for them, and re-layouts: 2.13 us -> none  [on_device(): soft_out = back.transpose(1, 0, 2).reshape(rows, heads * LANES)]
    pallas_call x1 -> x2, Pallas kernels: 1.68 us -> 3.27 us  [the longest x1 2.02 us: unpack(): pl.pallas_call(unpack_kernel, in_specs=[IN_HBM], out_specs=IN_HBM, out_sh...]
    unnamed x20 -> x16, local copies, waits for them, and re-layouts: 3.09 us -> 2.12 us
where the time goes in v4:
time: 67.4 us; the launch traced here: 66.8 us
  starting transfers between devices  25.6 us (38%)
  Pallas kernels  23.1 us (34%)
  waiting for transfers between devices  15 us (22%)
  local copies, waits for them, and re-layouts  2.13 us (3%)
  between operations  0.97 us (1%)
    all_to_all x3, starting transfers between devices, exchange(): return lax.all_to_all(x, 'ctx', split_axis=0, concat_axis=0, tiled=True)  11.4 us
    ppermute x7, starting transfers between devices, swap(): return lax.ppermute(x, 'ctx', [(i, i ^ d) for i in range(size)])  9.54 us
    pallas_call x1, Pallas kernels, attend(): pl.pallas_call(functools.partial(attend_kernel, order, rows, window), in_...  9 us
    ppermute x7, waiting for transfers between devices, swap(): return lax.ppermute(x, 'ctx', [(i, i ^ d) for i in range(size)])  6.68 us
    ppermute x3, starting transfers between devices, on_device(): squares.append(lax.ppermute(square, 'head', turn))  4.71 us
    ppermute x3, waiting for transfers between devices, on_device(): squares.append(lax.ppermute(square, 'head', turn))  4.46 us
    pallas_call x1, Pallas kernels, inside(): pl.pallas_call(inside_kernel, in_specs=[IN_VMEM, IN_VMEM, IN_HBM, IN_VMEM...  4.23 us
    all_to_all x3, waiting for transfers between devices, exchange(): return lax.all_to_all(x, 'ctx', split_axis=0, concat_axis=0, tiled=True)  3.82 us
  transfers between devices with their start and end apart: 13, of which 8 were waited for; matrix products, arithmetic and copies ran while one was open for 0% of the time, Pallas kernels for 27%

profile of v4, /device:TPU:0, one launch (start us, length us, event | category | flops | bytes accessed | tf_op | source)
XLA Modules:
  0.0 66.8 jit_solution(11852902121235500919)
XLA Ops:
  0.7 2.9 %pack.1 = (bf16[3,384,128]{2,1,0:T(8,128)(2,1)}, bf16[3,384,128]{2,1,0:T(8,128)(2,1)}, bf16[3,384,128]{2,1,0:T(8,128)(2,1)}, bf16[3,384,128]{2,1,0:T(8,128)(2,1)...) custom-call(s32[1]{0:T(128)} %bitcast.me_ref, ...), custom_call_target="tpu_custom_call" | custom-call | bytes 4718592 | tf_op jit(solution)/shard_map/pack/pallas_call | solution.py:98
  3.5 4.0 %collective-permute-start = (bf16[3,384,128]{2,1,0:T(8,128)(2,1)}, bf16[3,384,128]{2,1,0:T(8,128)(2,1)}, u32[]{:S(2)}, u32[]{:S(2)}) collective-permute-start(bf16[3,384,128]{2,1,0:T(8,128)(2,1)} %get-tuple-element.31), channel_id=1, source_target_pairs={{0,24},{4,28},{8,16},{12,20},{16,8},{20,12},{24,0},{28,4},{1,25},{... | collective-permute-start | bytes 884744 | tf_op jit(solution)/shard_map/ppermute | solution.py:550
  8.0 1.4 %local_state.1 = (bf16[8,144,128]{2,1,0:T(8,128)(2,1)}, f32[8,384]{1,0:T(8,128)S(1)}) custom-call(f32[8,384]{1,0:T(8,128)S(1)} %copy-done.4, s32[1,384]{1,0:T(1,128)S(1)} %reshape.16.doc_ref, bf16[384,1024]{1,0:T(8,128)(2,1)S(1)} %copy-done, bf16[384,1024]{1,0:T(8,128)(2,1)S(1)} %copy-done.1), custom_call_target="tpu_custom_call" | custom-call | flops 100663296 | bytes 1892352 | tf_op jit(solution)/shard_map/local_state/pallas_call | solution.py:330
  9.4 3.4 %all-to-all-start = ((bf16[8,144,128]{2,1,0:T(8,128)(2,1)}), bf16[8,144,128]{2,1,0:T(8,128)(2,1)S(1)}, u32[]{:S(2)}, u32[]{:S(2)}) async-start(bf16[8,144,128]{2,1,0:T(8,128)(2,1)} %get-tuple-element.28), calls=%async_computation | async-start | bytes 589824 | tf_op jit(solution)/shard_map/all_to_all | solution.py:539
  12.8 1.9 %collective-permute-start.2 = (bf16[3,384,128]{2,1,0:T(8,128)(2,1)}, bf16[3,384,128]{2,1,0:T(8,128)(2,1)}, u32[]{:S(2)}, u32[]{:S(2)}) collective-permute-start(bf16[3,384,128]{2,1,0:T(8,128)(2,1)} %get-tuple-element.33), channel_id=1, source_target_pairs={{0,8},{4,12},{8,0},{12,4},{16,24},{20,28},{24,16},{28,20},{1,9},{5... | collective-permute-start | bytes 884744 | tf_op jit(solution)/shard_map/ppermute | solution.py:550
  14.8 0.9 %collective-permute-start.3 = (bf16[3,384,128]{2,1,0:T(8,128)(2,1)}, bf16[3,384,128]{2,1,0:T(8,128)(2,1)}, u32[]{:S(2)}, u32[]{:S(2)}) collective-permute-start(bf16[3,384,128]{2,1,0:T(8,128)(2,1)} %get-tuple-element.36), channel_id=1, source_target_pairs={{0,28},{4,24},{8,20},{12,16},{16,12},{20,8},{24,4},{28,0},{1,29},{... | collective-permute-start | bytes 884744 | tf_op jit(solution)/shard_map/ppermute | solution.py:550
  16.1 1.1 %copy-done.2 = bf16[384,1024]{1,0:T(8,128)(2,1)S(1)} copy-done((bf16[384,1024]{1,0:T(8,128)(2,1)S(1)}, bf16[384,1024]{1,0:T(8,128)(2,1)}, u32[]{:S(2)}) %copy-start.2) | copy-done | bytes 786456
  17.2 4.2 %inside.1.raw_ref = f32[384,1024]{1,0:T(8,128)S(1)} custom-call(f32[8,384]{1,0:T(8,128)S(1)} %get-tuple-element.25.cum_ref, s32[1,384]{1,0:T(1,128)S(1)} %reshape.16.doc_ref, bf16[384,1024]{1,0:T(8,128)(2,1)S(1)} %copy-done.2, bf16[384,1024]{1,0:T(8,128)(2,1)S(1)} %copy-done, bf16[384,1024]{1,0:T(8,128)(2,1)S(1)} %copy-done.1), custom_call_target="tpu_custom_call" | custom-call | flops 452984832 | bytes 3932160 | tf_op jit(solution)/shard_map/inside/pallas_call | solution.py:433
  21.5 2.8 %all-to-all-done.came_ref = bf16[8,144,128]{2,1,0:T(8,128)(2,1)S(1)} async-done(((bf16[8,144,128]{2,1,0:T(8,128)(2,1)}), bf16[8,144,128]{2,1,0:T(8,128)(2,1)S(1)}, u32[]{:S(2)}, u32[]{:S(2)}) %all-to-all-start) | async-done | bytes 294944 | tf_op jit(solution)/shard_map/all_to_all | solution.py:539
  24.3 1.3 %collective-permute-start.5 = (bf16[3,384,128]{2,1,0:T(8,128)(2,1)}, bf16[3,384,128]{2,1,0:T(8,128)(2,1)S(1)}, u32[]{:S(2)}, u32[]{:S(2)}) collective-permute-start(bf16[3,384,128]{2,1,0:T(8,128)(2,1)} %get-tuple-element.38), channel_id=1, source_target_pairs={{0,12},{4,8},{8,4},{12,0},{16,28},{20,24},{24,20},{28,16},{1,13},{... | collective-permute-start | bytes 884744 | tf_op jit(solution)/shard_map/ppermute | solution.py:550
  26.1 1.2 %carry.1 = (bf16[8,144,128]{2,1,0:T(8,128)(2,1)}, bf16[8,16,128]{2,1,0:T(8,128)(2,1)S(1)}) custom-call(bf16[8,144,128]{2,1,0:T(8,128)(2,1)S(1)} %all-to-all-done.came_ref), custom_call_target="tpu_custom_call" | custom-call | flops 294912 | bytes 589824 | tf_op jit(solution)/shard_map/carry/pallas_call | solution.py:366
  27.4 3.6 %all-to-all-start.1 = ((bf16[8,144,128]{2,1,0:T(8,128)(2,1)}), bf16[8,144,128]{2,1,0:T(8,128)(2,1)S(1)}, u32[]{:S(2)}, u32[]{:S(2)}) async-start(bf16[8,144,128]{2,1,0:T(8,128)(2,1)} %get-tuple-element.30), calls=%async_computation.1 | async-start | bytes 589824 | tf_op jit(solution)/shard_map/all_to_all | solution.py:539
  31.0 1.4 %collective-permute-done.3.refs_3_ = bf16[3,384,128]{2,1,0:T(8,128)(2,1)} collective-permute-done((bf16[3,384,128]{2,1,0:T(8,128)(2,1)}, bf16[3,384,128]{2,1,0:T(8,128)(2,1)}, u32[]{:S(2)}, u32[]{:S(2)}) %collective-permute-start.3) | collective-permute-done | bytes 294944 | tf_op jit(solution)/shard_map/ppermute | solution.py:550
  32.4 4.4 %collective-permute-done.4.refs_4_ = bf16[3,384,128]{2,1,0:T(8,128)(2,1)} collective-permute-done((bf16[3,384,128]{2,1,0:T(8,128)(2,1)}, bf16[3,384,128]{2,1,0:T(8,128)(2,1)}, u32[]{:S(2)}, u32[]{:S(2)}) %collective-permute-start.4) | collective-permute-done | bytes 294944 | tf_op jit(solution)/shard_map/ppermute | solution.py:550
  37.7 1.0 %copy-done.6 = bf16[3,384,128]{2,1,0:T(8,128)(2,1)S(1)} copy-done((bf16[3,384,128]{2,1,0:T(8,128)(2,1)S(1)}, bf16[3,384,128]{2,1,0:T(8,128)(2,1)}, u32[]{:S(2)}) %copy-start.6) | copy-done | bytes 294936
  38.6 9.0 %attend.1 = bf16[3072,128]{1,0:T(8,128)(2,1)} custom-call(s32[1]{0:T(128)} %bitcast.me_ref, bf16[3,384,128]{2,1,0:T(8,128)(2,1)} %collective-permute-done.refs_0_, bf16[3,384,128]{2,1,0:T(8,128)(2,1)} %collective-permute-done.1.refs_1_, bf16[3,384,128]{2,1,0:T(8,128)(2,1)} %collective-permute-done.2.refs_2_, ...), custom_call_target="tpu_custom_call" | custom-call | flops 2415919104 | bytes 3145728 | tf_op jit(solution)/shard_map/attend/pallas_call | solution.py:209
  47.7 4.4 %all-to-all-start.2 = ((bf16[8,384,128]{2,1,0:T(8,128)(2,1)}), bf16[8,384,128]{2,1,0:T(8,128)(2,1)}, u32[]{:S(2)}, u32[]{:S(2)}) async-start(bf16[8,384,128]{2,1,0:T(8,128)(2,1)} %bitcast.2), calls=%async_computation.2 | async-start | bytes 1572864 | tf_op jit(solution)/shard_map/all_to_all | solution.py:539
  52.0 1.3 %incoming.1 = (f32[384,1024]{1,0:T(8,128)S(1)}, f32[8,384]{1,0:T(8,128)S(1)}) custom-call(f32[8,384]{1,0:T(8,128)S(1)} %get-tuple-element.25.cum_ref, s32[1,384]{1,0:T(1,128)S(1)} %reshape.16.doc_ref, bf16[384,1024]{1,0:T(8,128)(2,1)S(1)} %copy-done.3, bf16[8,144,128]{2,1,0:T(8,128)(2,1)S(1)} %all-to-all-done.1.before_ref, f32[384,1024]{1,0:T(8,128)S(1)} %inside.1.raw_ref), custom_call_target="tpu_custom_call" | custom-call | flops 100663296 | bytes 4239360 | tf_op jit(solution)/shard_map/incoming/pallas_call | solution.py:479
  53.3 3.7 %collective-permute-start.9 = (f32[8,384]{1,0:T(8,128)S(1)}, f32[8,384]{1,0:T(8,128)S(1)}, u32[]{:S(2)}, u32[]{:S(2)}) collective-permute-start(f32[8,384]{1,0:T(8,128)S(1)} %get-tuple-element.43.refs_0_), channel_id=1, source_target_pairs={{0,3},{1,0},{2,1},{3,2},{4,7},{5,4},{6,5},{7,6},{8,11},{9,8},{10,9... | collective-permute-start | bytes 36872 | tf_op jit(solution)/shard_map/ppermute | solution.py:578
  57.0 1.0 %collective-permute-start.7 = (f32[8,384]{1,0:T(8,128)S(1)}, f32[8,384]{1,0:T(8,128)S(1)}, u32[]{:S(2)}, u32[]{:S(2)}) collective-permute-start(f32[8,384]{1,0:T(8,128)S(1)} %get-tuple-element.43.refs_0_), channel_id=1, source_target_pairs={{0,1},{1,2},{2,3},{3,0},{4,5},{5,6},{6,7},{7,4},{8,9},{9,10},{10,1... | collective-permute-start | bytes 36872 | tf_op jit(solution)/shard_map/ppermute | solution.py:578
  58.4 3.3 %collective-permute-done.8.refs_2_ = f32[8,384]{1,0:T(8,128)S(1)} collective-permute-done((f32[8,384]{1,0:T(8,128)S(1)}, f32[8,384]{1,0:T(8,128)S(1)}, u32[]{:S(2)}, u32[]{:S(2)}) %collective-permute-start.8) | collective-permute-done | bytes 12320 | tf_op jit(solution)/shard_map/ppermute | solution.py:578
  62.5 1.1 %normalize.1 = bf16[384,1024]{1,0:T(8,128)(2,1)} custom-call(f32[384,1024]{1,0:T(8,128)S(1)} %get-tuple-element.42.raw_ref, f32[1,1024]{1,0:T(1,128)S(1)} %bitcast.3, f32[8,384]{1,0:T(8,128)S(1)} %get-tuple-element.43.refs_0_, f32[8,384]{1,0:T(8,128)S(1)} %collective-permute-done.7.refs_1_, f32[8,384]{1,0:T(8,128)S(1)} %collective-permute-done.8.refs_2_, ...), custom_call_target="tpu_custom_call" | custom-call | flops 1179648 | bytes 2359296 | tf_op jit(solution)/shard_map/normalize/pallas_call | solution.py:517
  63.6 1.0 %all-to-all-done.2.came_ref = bf16[8,384,128]{2,1,0:T(8,128)(2,1)} async-done(((bf16[8,384,128]{2,1,0:T(8,128)(2,1)}), bf16[8,384,128]{2,1,0:T(8,128)(2,1)}, u32[]{:S(2)}, u32[]{:S(2)}) %all-to-all-start.2) | async-done | bytes 786464 | tf_op jit(solution)/shard_map/all_to_all | solution.py:539
  64.6 2.0 %unpack.1 = bf16[384,1024]{1,0:T(8,128)(2,1)} custom-call(bf16[8,384,128]{2,1,0:T(8,128)(2,1)} %all-to-all-done.2.came_ref), custom_call_target="tpu_custom_call" | custom-call | bytes 1572864 | tf_op jit(solution)/shard_map/unpack/pallas_call | solution.py:263
  (27 shorter events, 3.4 us)
Async XLA Ops:
  0.6 7.4 %copy-start.7 = (s32[384]{0:T(512)S(1)}, s32[384]{0:T(512)}, u32[]{:S(2)}) copy-start(s32[384]{0:T(512)} %param.17) | copy-start | bytes 4612
  0.6 7.4 %copy-start = (bf16[384,1024]{1,0:T(8,128)(2,1)S(1)}, bf16[384,1024]{1,0:T(8,128)(2,1)}, u32[]{:S(2)}) copy-start(bf16[384,1024]{1,0:T(8,128)(2,1)} %k_ref.2) | copy-start | bytes 2359300
  0.7 7.4 %copy-start.1 = (bf16[384,1024]{1,0:T(8,128)(2,1)S(1)}, bf16[384,1024]{1,0:T(8,128)(2,1)}, u32[]{:S(2)}) copy-start(bf16[384,1024]{1,0:T(8,128)(2,1)} %v_ref.3) | copy-start | bytes 2359300
  0.7 7.4 %copy-start.4 = (f32[8,384]{1,0:T(8,128)S(1)}, f32[8,384]{1,0:T(8,128)}, u32[]{:S(2)}) copy-start(f32[8,384]{1,0:T(8,128)} %gate_ref.1) | copy-start | bytes 36868
  3.5 20.8 %collective-permute-start = (bf16[3,384,128]{2,1,0:T(8,128)(2,1)}, bf16[3,384,128]{2,1,0:T(8,128)(2,1)}, u32[]{:S(2)}, u32[]{:S(2)}) collective-permute-start(bf16[3,384,128]{2,1,0:T(8,128)(2,1)} %get-tuple-element.31), channel_id=1, source_target_pairs={{0,24},{4,28},{8,16},{12,20},{16,8},{20,12},{24,0},{28,4},{1,25},{... | collective-permute-start | bytes 884744 | tf_op jit(solution)/shard_map/ppermute | solution.py:550
  7.5 18.1 %collective-permute-start.1 = (bf16[3,384,128]{2,1,0:T(8,128)(2,1)}, bf16[3,384,128]{2,1,0:T(8,128)(2,1)}, u32[]{:S(2)}, u32[]{:S(2)}) collective-permute-start(bf16[3,384,128]{2,1,0:T(8,128)(2,1)} %get-tuple-element.32), channel_id=1, source_target_pairs={{0,16},{4,20},{8,24},{12,28},{16,0},{20,4},{24,8},{28,12},{1,17},{... | collective-permute-start | bytes 884744 | tf_op jit(solution)/shard_map/ppermute | solution.py:550
  9.4 14.9 %all-to-all-start = ((bf16[8,144,128]{2,1,0:T(8,128)(2,1)}), bf16[8,144,128]{2,1,0:T(8,128)(2,1)S(1)}, u32[]{:S(2)}, u32[]{:S(2)}) async-start(bf16[8,144,128]{2,1,0:T(8,128)(2,1)} %get-tuple-element.28), calls=%async_computation | async-start | bytes 589824 | tf_op jit(solution)/shard_map/all_to_all | solution.py:539
  12.8 18.1 %collective-permute-start.2 = (bf16[3,384,128]{2,1,0:T(8,128)(2,1)}, bf16[3,384,128]{2,1,0:T(8,128)(2,1)}, u32[]{:S(2)}, u32[]{:S(2)}) collective-permute-start(bf16[3,384,128]{2,1,0:T(8,128)(2,1)} %get-tuple-element.33), channel_id=1, source_target_pairs={{0,8},{4,12},{8,0},{12,4},{16,24},{20,28},{24,16},{28,20},{1,9},{5... | collective-permute-start | bytes 884744 | tf_op jit(solution)/shard_map/ppermute | solution.py:550
  14.8 17.7 %collective-permute-start.3 = (bf16[3,384,128]{2,1,0:T(8,128)(2,1)}, bf16[3,384,128]{2,1,0:T(8,128)(2,1)}, u32[]{:S(2)}, u32[]{:S(2)}) collective-permute-start(bf16[3,384,128]{2,1,0:T(8,128)(2,1)} %get-tuple-element.36), channel_id=1, source_target_pairs={{0,28},{4,24},{8,20},{12,16},{16,12},{20,8},{24,4},{28,0},{1,29},{... | collective-permute-start | bytes 884744 | tf_op jit(solution)/shard_map/ppermute | solution.py:550
  15.7 21.1 %collective-permute-start.4 = (bf16[3,384,128]{2,1,0:T(8,128)(2,1)}, bf16[3,384,128]{2,1,0:T(8,128)(2,1)}, u32[]{:S(2)}, u32[]{:S(2)}) collective-permute-start(bf16[3,384,128]{2,1,0:T(8,128)(2,1)} %get-tuple-element.37), channel_id=1, source_target_pairs={{0,20},{4,16},{8,28},{12,24},{16,4},{20,0},{24,12},{28,8},{1,21},{... | collective-permute-start | bytes 884744 | tf_op jit(solution)/shard_map/ppermute | solution.py:550
  16.1 1.1 %copy-start.2 = (bf16[384,1024]{1,0:T(8,128)(2,1)S(1)}, bf16[384,1024]{1,0:T(8,128)(2,1)}, u32[]{:S(2)}) copy-start(bf16[384,1024]{1,0:T(8,128)(2,1)} %q_hbm.3) | copy-start | bytes 2359300
  24.3 13.4 %collective-permute-start.5 = (bf16[3,384,128]{2,1,0:T(8,128)(2,1)}, bf16[3,384,128]{2,1,0:T(8,128)(2,1)S(1)}, u32[]{:S(2)}, u32[]{:S(2)}) collective-permute-start(bf16[3,384,128]{2,1,0:T(8,128)(2,1)} %get-tuple-element.38), channel_id=1, source_target_pairs={{0,12},{4,8},{8,4},{12,0},{16,28},{20,24},{24,20},{28,16},{1,13},{... | collective-permute-start | bytes 884744 | tf_op jit(solution)/shard_map/ppermute | solution.py:550
  25.6 12.0 %collective-permute-start.6 = (bf16[3,384,128]{2,1,0:T(8,128)(2,1)}, bf16[3,384,128]{2,1,0:T(8,128)(2,1)S(1)}, u32[]{:S(2)}, u32[]{:S(2)}) collective-permute-start(bf16[3,384,128]{2,1,0:T(8,128)(2,1)} %get-tuple-element.39), channel_id=1, source_target_pairs={{0,4},{4,0},{8,12},{12,8},{16,20},{20,16},{24,28},{28,24},{1,5},{5... | collective-permute-start | bytes 884744 | tf_op jit(solution)/shard_map/ppermute | solution.py:550
  27.4 20.3 %all-to-all-start.1 = ((bf16[8,144,128]{2,1,0:T(8,128)(2,1)}), bf16[8,144,128]{2,1,0:T(8,128)(2,1)S(1)}, u32[]{:S(2)}, u32[]{:S(2)}) async-start(bf16[8,144,128]{2,1,0:T(8,128)(2,1)} %get-tuple-element.30), calls=%async_computation.1 | async-start | bytes 589824 | tf_op jit(solution)/shard_map/all_to_all | solution.py:539
  37.7 1.0 %copy-start.6 = (bf16[3,384,128]{2,1,0:T(8,128)(2,1)S(1)}, bf16[3,384,128]{2,1,0:T(8,128)(2,1)}, u32[]{:S(2)}) copy-start(bf16[3,384,128]{2,1,0:T(8,128)(2,1)} %get-tuple-element.23.refs_7_) | copy-start | bytes 884740
  47.6 4.4 %copy-start.3 = (bf16[384,1024]{1,0:T(8,128)(2,1)S(1)}, bf16[384,1024]{1,0:T(8,128)(2,1)}, u32[]{:S(2)}) copy-start(bf16[384,1024]{1,0:T(8,128)(2,1)} %q_hbm.3) | copy-start | bytes 2359300
  47.7 17.0 %all-to-all-start.2 = ((bf16[8,384,128]{2,1,0:T(8,128)(2,1)}), bf16[8,384,128]{2,1,0:T(8,128)(2,1)}, u32[]{:S(2)}, u32[]{:S(2)}) async-start(bf16[8,384,128]{2,1,0:T(8,128)(2,1)} %bitcast.2), calls=%async_computation.2 | async-start | bytes 1572864 | tf_op jit(solution)/shard_map/all_to_all | solution.py:539
  52.0 10.5 %copy-start.5 = (f32[1024]{0:T(1024)S(1)}, f32[1024]{0:T(1024)}, u32[]{:S(2)}) copy-start(f32[1024]{0:T(1024)} %param.13) | copy-start | bytes 12292
  53.3 5.1 %collective-permute-start.9 = (f32[8,384]{1,0:T(8,128)S(1)}, f32[8,384]{1,0:T(8,128)S(1)}, u32[]{:S(2)}, u32[]{:S(2)}) collective-permute-start(f32[8,384]{1,0:T(8,128)S(1)} %get-tuple-element.43.refs_0_), channel_id=1, source_target_pairs={{0,3},{1,0},{2,1},{3,2},{4,7},{5,4},{6,5},{7,6},{8,11},{9,8},{10,9... | collective-permute-start | bytes 36872 | tf_op jit(solution)/shard_map/ppermute | solution.py:578
  57.0 4.7 %collective-permute-start.8 = (f32[8,384]{1,0:T(8,128)S(1)}, f32[8,384]{1,0:T(8,128)S(1)}, u32[]{:S(2)}, u32[]{:S(2)}) collective-permute-start(f32[8,384]{1,0:T(8,128)S(1)} %get-tuple-element.43.refs_0_), channel_id=1, source_target_pairs={{0,2},{1,3},{2,0},{3,1},{4,6},{5,7},{6,4},{7,5},{8,10},{9,11},{10,... | collective-permute-start | bytes 36872 | tf_op jit(solution)/shard_map/ppermute | solution.py:578
  57.0 5.5 %collective-permute-start.7 = (f32[8,384]{1,0:T(8,128)S(1)}, f32[8,384]{1,0:T(8,128)S(1)}, u32[]{:S(2)}, u32[]{:S(2)}) collective-permute-start(f32[8,384]{1,0:T(8,128)S(1)} %get-tuple-element.43.refs_0_), channel_id=1, source_target_pairs={{0,1},{1,2},{2,3},{3,0},{4,5},{5,6},{6,7},{7,4},{8,9},{9,10},{10,1... | collective-permute-start | bytes 36872 | tf_op jit(solution)/shard_map/ppermute | solution.py:578

commit v5 on v4

--- a/solution.py
+++ b/solution.py
@@ -140,19 +140,19 @@
 
     def body(i, carry):
         first = pl.multiple_of(i * step, step)
-        low = 0
+        low, low_next = 0, 0
         for s in starts:
             low = jnp.where(first >= s, s, low)
+            low_next = jnp.where(first + TILE >= s, s, low_next)
         count = (i + 1) * CHAINS - low // TILE
 
-        def run(n):
-            base = pl.multiple_of(first + step - n * TILE, TILE)
+        def run(counts):
             tops = {}
 
             def score(chain):
-                tiles = n - CHAINS + 1 + chain
+                tiles = counts[chain]
                 mine = pl.multiple_of(first + chain * TILE, TILE)
-                keys = pl.ds(base, tiles * TILE)
+                base = pl.multiple_of(mine + TILE - tiles * TILE, TILE)
                 begin = jnp.zeros(wide, jnp.int32)
                 for s in starts:
                     begin = jnp.where(sub >= s - mine, s, begin)
@@ -172,8 +172,9 @@
                 tops[chain] = jnp.max(top, axis=1, keepdims=True) * factor
 
             def mix(chain):
-                tiles = n - CHAINS + 1 + chain
+                tiles = counts[chain]
                 mine = pl.multiple_of(first + chain * TILE, TILE)
+                base = pl.multiple_of(mine + TILE - tiles * TILE, TILE)
                 row_max = tops[chain]
                 total = jnp.zeros((TILE, 2 * LANES), F32)
                 for t in range(tiles):
@@ -188,8 +189,12 @@
             for chain in range(CHAINS):
                 mix(chain)
 
-        for n in range(CHAINS, window + CHAINS):
-            pl.when(count == n)(functools.partial(run, n))
+        for n in range(2, window + 2):
+            if n < 4:
+                pl.when(count == n)(functools.partial(run, (n - 1, n)))
+            else:
+                pl.when((count == n) & (low == low_next))(functools.partial(run, (n - 1, n)))
+                pl.when((count == n) & (low != low_next))(functools.partial(run, (n - 1, 2)))
         at = pl.ds(first, step)
         pltpu.make_async_copy(o_ref.at[at], out_ref.at[at], out_sems.at[i]).start()
         return carry

time: 67.4 us -> 66.7 us (0.990)
  Pallas kernels: 23.1 us -> 22.4 us
    pallas_call x1, Pallas kernels: 9 us -> 8.31 us  [attend(): pl.pallas_call(functools.partial(attend_kernel, order, rows, window), in_...]
where the time goes in v5:
time: 66.7 us; the launch traced here: 66.1 us
  starting transfers between devices  25.4 us (38%)
  Pallas kernels  22.4 us (34%)
  waiting for transfers between devices  15.2 us (23%)
  local copies, waits for them, and re-layouts  2.13 us (3%)
  between operations  0.97 us (1%)
    all_to_all x3, starting transfers between devices, exchange(): return lax.all_to_all(x, 'ctx', split_axis=0, concat_axis=0, tiled=True)  11.2 us
    ppermute x7, starting transfers between devices, swap(): return lax.ppermute(x, 'ctx', [(i, i ^ d) for i in range(size)])  9.54 us
    pallas_call x1, Pallas kernels, attend(): pl.pallas_call(functools.partial(attend_kernel, order, rows, window), in_...  8.31 us
    ppermute x7, waiting for transfers between devices, swap(): return lax.ppermute(x, 'ctx', [(i, i ^ d) for i in range(size)])  6.86 us
    ppermute x3, starting transfers between devices, on_device(): squares.append(lax.ppermute(square, 'head', turn))  4.68 us
    ppermute x3, waiting for transfers between devices, on_device(): squares.append(lax.ppermute(square, 'head', turn))  4.48 us
    pallas_call x1, Pallas kernels, inside(): pl.pallas_call(inside_kernel, in_specs=[IN_VMEM, IN_VMEM, IN_HBM, IN_VMEM...  4.23 us
    all_to_all x3, waiting for transfers between devices, exchange(): return lax.all_to_all(x, 'ctx', split_axis=0, concat_axis=0, tiled=True)  3.83 us
  transfers between devices with their start and end apart: 13, of which 8 were waited for; matrix products, arithmetic and copies ran while one was open for 0% of the time, Pallas kernels for 27%

profile of v5, /device:TPU:0, one launch (start us, length us, event | category | flops | bytes accessed | tf_op | source)
XLA Modules:
  0.0 66.1 jit_solution(6743991446627314419)
XLA Ops:
  0.7 2.9 %pack.1 = (bf16[3,384,128]{2,1,0:T(8,128)(2,1)}, bf16[3,384,128]{2,1,0:T(8,128)(2,1)}, bf16[3,384,128]{2,1,0:T(8,128)(2,1)}, bf16[3,384,128]{2,1,0:T(8,128)(2,1)...) custom-call(s32[1]{0:T(128)} %bitcast.me_ref, ...), custom_call_target="tpu_custom_call" | custom-call | bytes 4718592 | tf_op jit(solution)/shard_map/pack/pallas_call | solution.py:98
  3.5 4.0 %collective-permute-start = (bf16[3,384,128]{2,1,0:T(8,128)(2,1)}, bf16[3,384,128]{2,1,0:T(8,128)(2,1)}, u32[]{:S(2)}, u32[]{:S(2)}) collective-permute-start(bf16[3,384,128]{2,1,0:T(8,128)(2,1)} %get-tuple-element.31), channel_id=1, source_target_pairs={{0,24},{4,28},{8,16},{12,20},{16,8},{20,12},{24,0},{28,4},{1,25},{... | collective-permute-start | bytes 884744 | tf_op jit(solution)/shard_map/ppermute | solution.py:555
  8.0 1.4 %local_state.1 = (bf16[8,144,128]{2,1,0:T(8,128)(2,1)}, f32[8,384]{1,0:T(8,128)S(1)}) custom-call(f32[8,384]{1,0:T(8,128)S(1)} %copy-done.4, s32[1,384]{1,0:T(1,128)S(1)} %reshape.16.doc_ref, bf16[384,1024]{1,0:T(8,128)(2,1)S(1)} %copy-done, bf16[384,1024]{1,0:T(8,128)(2,1)S(1)} %copy-done.1), custom_call_target="tpu_custom_call" | custom-call | flops 100663296 | bytes 1892352 | tf_op jit(solution)/shard_map/local_state/pallas_call | solution.py:335
  9.4 3.4 %all-to-all-start = ((bf16[8,144,128]{2,1,0:T(8,128)(2,1)}), bf16[8,144,128]{2,1,0:T(8,128)(2,1)S(1)}, u32[]{:S(2)}, u32[]{:S(2)}) async-start(bf16[8,144,128]{2,1,0:T(8,128)(2,1)} %get-tuple-element.28), calls=%async_computation | async-start | bytes 589824 | tf_op jit(solution)/shard_map/all_to_all | solution.py:544
  12.8 1.9 %collective-permute-start.2 = (bf16[3,384,128]{2,1,0:T(8,128)(2,1)}, bf16[3,384,128]{2,1,0:T(8,128)(2,1)}, u32[]{:S(2)}, u32[]{:S(2)}) collective-permute-start(bf16[3,384,128]{2,1,0:T(8,128)(2,1)} %get-tuple-element.33), channel_id=1, source_target_pairs={{0,8},{4,12},{8,0},{12,4},{16,24},{20,28},{24,16},{28,20},{1,9},{5... | collective-permute-start | bytes 884744 | tf_op jit(solution)/shard_map/ppermute | solution.py:555
  14.8 0.9 %collective-permute-start.3 = (bf16[3,384,128]{2,1,0:T(8,128)(2,1)}, bf16[3,384,128]{2,1,0:T(8,128)(2,1)}, u32[]{:S(2)}, u32[]{:S(2)}) collective-permute-start(bf16[3,384,128]{2,1,0:T(8,128)(2,1)} %get-tuple-element.36), channel_id=1, source_target_pairs={{0,28},{4,24},{8,20},{12,16},{16,12},{20,8},{24,4},{28,0},{1,29},{... | collective-permute-start | bytes 884744 | tf_op jit(solution)/shard_map/ppermute | solution.py:555
  16.1 1.1 %copy-done.2 = bf16[384,1024]{1,0:T(8,128)(2,1)S(1)} copy-done((bf16[384,1024]{1,0:T(8,128)(2,1)S(1)}, bf16[384,1024]{1,0:T(8,128)(2,1)}, u32[]{:S(2)}) %copy-start.2) | copy-done | bytes 786456
  17.2 4.2 %inside.1.raw_ref = f32[384,1024]{1,0:T(8,128)S(1)} custom-call(f32[8,384]{1,0:T(8,128)S(1)} %get-tuple-element.25.cum_ref, s32[1,384]{1,0:T(1,128)S(1)} %reshape.16.doc_ref, bf16[384,1024]{1,0:T(8,128)(2,1)S(1)} %copy-done.2, bf16[384,1024]{1,0:T(8,128)(2,1)S(1)} %copy-done, bf16[384,1024]{1,0:T(8,128)(2,1)S(1)} %copy-done.1), custom_call_target="tpu_custom_call" | custom-call | flops 452984832 | bytes 3932160 | tf_op jit(solution)/shard_map/inside/pallas_call | solution.py:438
  21.5 2.8 %all-to-all-done.came_ref = bf16[8,144,128]{2,1,0:T(8,128)(2,1)S(1)} async-done(((bf16[8,144,128]{2,1,0:T(8,128)(2,1)}), bf16[8,144,128]{2,1,0:T(8,128)(2,1)S(1)}, u32[]{:S(2)}, u32[]{:S(2)}) %all-to-all-start) | async-done | bytes 294944 | tf_op jit(solution)/shard_map/all_to_all | solution.py:544
  24.3 1.3 %collective-permute-start.5 = (bf16[3,384,128]{2,1,0:T(8,128)(2,1)}, bf16[3,384,128]{2,1,0:T(8,128)(2,1)S(1)}, u32[]{:S(2)}, u32[]{:S(2)}) collective-permute-start(bf16[3,384,128]{2,1,0:T(8,128)(2,1)} %get-tuple-element.38), channel_id=1, source_target_pairs={{0,12},{4,8},{8,4},{12,0},{16,28},{20,24},{24,20},{28,16},{1,13},{... | collective-permute-start | bytes 884744 | tf_op jit(solution)/shard_map/ppermute | solution.py:555
  26.1 1.2 %carry.1 = (bf16[8,144,128]{2,1,0:T(8,128)(2,1)}, bf16[8,16,128]{2,1,0:T(8,128)(2,1)S(1)}) custom-call(bf16[8,144,128]{2,1,0:T(8,128)(2,1)S(1)} %all-to-all-done.came_ref), custom_call_target="tpu_custom_call" | custom-call | flops 294912 | bytes 589824 | tf_op jit(solution)/shard_map/carry/pallas_call | solution.py:371
  27.4 3.4 %all-to-all-start.1 = ((bf16[8,144,128]{2,1,0:T(8,128)(2,1)}), bf16[8,144,128]{2,1,0:T(8,128)(2,1)S(1)}, u32[]{:S(2)}, u32[]{:S(2)}) async-start(bf16[8,144,128]{2,1,0:T(8,128)(2,1)} %get-tuple-element.30), calls=%async_computation.1 | async-start | bytes 589824 | tf_op jit(solution)/shard_map/all_to_all | solution.py:544
  30.8 1.6 %collective-permute-done.3.refs_3_ = bf16[3,384,128]{2,1,0:T(8,128)(2,1)} collective-permute-done((bf16[3,384,128]{2,1,0:T(8,128)(2,1)}, bf16[3,384,128]{2,1,0:T(8,128)(2,1)}, u32[]{:S(2)}, u32[]{:S(2)}) %collective-permute-start.3) | collective-permute-done | bytes 294944 | tf_op jit(solution)/shard_map/ppermute | solution.py:555
  32.4 4.4 %collective-permute-done.4.refs_4_ = bf16[3,384,128]{2,1,0:T(8,128)(2,1)} collective-permute-done((bf16[3,384,128]{2,1,0:T(8,128)(2,1)}, bf16[3,384,128]{2,1,0:T(8,128)(2,1)}, u32[]{:S(2)}, u32[]{:S(2)}) %collective-permute-start.4) | collective-permute-done | bytes 294944 | tf_op jit(solution)/shard_map/ppermute | solution.py:555
  37.7 1.0 %copy-done.6 = bf16[3,384,128]{2,1,0:T(8,128)(2,1)S(1)} copy-done((bf16[3,384,128]{2,1,0:T(8,128)(2,1)S(1)}, bf16[3,384,128]{2,1,0:T(8,128)(2,1)}, u32[]{:S(2)}) %copy-start.6) | copy-done | bytes 294936
  38.6 8.3 %attend.1 = bf16[3072,128]{1,0:T(8,128)(2,1)} custom-call(s32[1]{0:T(128)} %bitcast.me_ref, bf16[3,384,128]{2,1,0:T(8,128)(2,1)} %collective-permute-done.refs_0_, bf16[3,384,128]{2,1,0:T(8,128)(2,1)} %collective-permute-done.1.refs_1_, bf16[3,384,128]{2,1,0:T(8,128)(2,1)} %collective-permute-done.2.refs_2_, ...), custom_call_target="tpu_custom_call" | custom-call | flops 2415919104 | bytes 3145728 | tf_op jit(solution)/shard_map/attend/pallas_call | solution.py:214
  47.0 4.4 %all-to-all-start.2 = ((bf16[8,384,128]{2,1,0:T(8,128)(2,1)}), bf16[8,384,128]{2,1,0:T(8,128)(2,1)}, u32[]{:S(2)}, u32[]{:S(2)}) async-start(bf16[8,384,128]{2,1,0:T(8,128)(2,1)} %bitcast.2), calls=%async_computation.2 | async-start | bytes 1572864 | tf_op jit(solution)/shard_map/all_to_all | solution.py:544
  51.3 1.3 %incoming.1 = (f32[384,1024]{1,0:T(8,128)S(1)}, f32[8,384]{1,0:T(8,128)S(1)}) custom-call(f32[8,384]{1,0:T(8,128)S(1)} %get-tuple-element.25.cum_ref, s32[1,384]{1,0:T(1,128)S(1)} %reshape.16.doc_ref, bf16[384,1024]{1,0:T(8,128)(2,1)S(1)} %copy-done.3, bf16[8,144,128]{2,1,0:T(8,128)(2,1)S(1)} %all-to-all-done.1.before_ref, f32[384,1024]{1,0:T(8,128)S(1)} %inside.1.raw_ref), custom_call_target="tpu_custom_call" | custom-call | flops 100663296 | bytes 4239360 | tf_op jit(solution)/shard_map/incoming/pallas_call | solution.py:484
  52.6 3.7 %collective-permute-start.9 = (f32[8,384]{1,0:T(8,128)S(1)}, f32[8,384]{1,0:T(8,128)S(1)}, u32[]{:S(2)}, u32[]{:S(2)}) collective-permute-start(f32[8,384]{1,0:T(8,128)S(1)} %get-tuple-element.43.refs_0_), channel_id=1, source_target_pairs={{0,3},{1,0},{2,1},{3,2},{4,7},{5,4},{6,5},{7,6},{8,11},{9,8},{10,9... | collective-permute-start | bytes 36872 | tf_op jit(solution)/shard_map/ppermute | solution.py:583
  56.3 1.0 %collective-permute-start.7 = (f32[8,384]{1,0:T(8,128)S(1)}, f32[8,384]{1,0:T(8,128)S(1)}, u32[]{:S(2)}, u32[]{:S(2)}) collective-permute-start(f32[8,384]{1,0:T(8,128)S(1)} %get-tuple-element.43.refs_0_), channel_id=1, source_target_pairs={{0,1},{1,2},{2,3},{3,0},{4,5},{5,6},{6,7},{7,4},{8,9},{9,10},{10,1... | collective-permute-start | bytes 36872 | tf_op jit(solution)/shard_map/ppermute | solution.py:583
  57.7 3.3 %collective-permute-done.8.refs_2_ = f32[8,384]{1,0:T(8,128)S(1)} collective-permute-done((f32[8,384]{1,0:T(8,128)S(1)}, f32[8,384]{1,0:T(8,128)S(1)}, u32[]{:S(2)}, u32[]{:S(2)}) %collective-permute-start.8) | collective-permute-done | bytes 12320 | tf_op jit(solution)/shard_map/ppermute | solution.py:583
  61.8 1.1 %normalize.1 = bf16[384,1024]{1,0:T(8,128)(2,1)} custom-call(f32[384,1024]{1,0:T(8,128)S(1)} %get-tuple-element.42.raw_ref, f32[1,1024]{1,0:T(1,128)S(1)} %bitcast.3, f32[8,384]{1,0:T(8,128)S(1)} %get-tuple-element.43.refs_0_, f32[8,384]{1,0:T(8,128)S(1)} %collective-permute-done.7.refs_1_, f32[8,384]{1,0:T(8,128)S(1)} %collective-permute-done.8.refs_2_, ...), custom_call_target="tpu_custom_call" | custom-call | flops 1179648 | bytes 2359296 | tf_op jit(solution)/shard_map/normalize/pallas_call | solution.py:522
  62.9 1.0 %all-to-all-done.2.came_ref = bf16[8,384,128]{2,1,0:T(8,128)(2,1)} async-done(((bf16[8,384,128]{2,1,0:T(8,128)(2,1)}), bf16[8,384,128]{2,1,0:T(8,128)(2,1)}, u32[]{:S(2)}, u32[]{:S(2)}) %all-to-all-start.2) | async-done | bytes 786464 | tf_op jit(solution)/shard_map/all_to_all | solution.py:544
  63.9 2.0 %unpack.1 = bf16[384,1024]{1,0:T(8,128)(2,1)} custom-call(bf16[8,384,128]{2,1,0:T(8,128)(2,1)} %all-to-all-done.2.came_ref), custom_call_target="tpu_custom_call" | custom-call | bytes 1572864 | tf_op jit(solution)/shard_map/unpack/pallas_call | solution.py:268
  (27 shorter events, 3.4 us)
Async XLA Ops:
  0.6 7.4 %copy-start.7 = (s32[384]{0:T(512)S(1)}, s32[384]{0:T(512)}, u32[]{:S(2)}) copy-start(s32[384]{0:T(512)} %param.17) | copy-start | bytes 4612
  0.6 7.4 %copy-start = (bf16[384,1024]{1,0:T(8,128)(2,1)S(1)}, bf16[384,1024]{1,0:T(8,128)(2,1)}, u32[]{:S(2)}) copy-start(bf16[384,1024]{1,0:T(8,128)(2,1)} %k_ref.2) | copy-start | bytes 2359300
  0.7 7.4 %copy-start.1 = (bf16[384,1024]{1,0:T(8,128)(2,1)S(1)}, bf16[384,1024]{1,0:T(8,128)(2,1)}, u32[]{:S(2)}) copy-start(bf16[384,1024]{1,0:T(8,128)(2,1)} %v_ref.3) | copy-start | bytes 2359300
  0.7 7.4 %copy-start.4 = (f32[8,384]{1,0:T(8,128)S(1)}, f32[8,384]{1,0:T(8,128)}, u32[]{:S(2)}) copy-start(f32[8,384]{1,0:T(8,128)} %gate_ref.1) | copy-start | bytes 36868
  3.5 20.8 %collective-permute-start = (bf16[3,384,128]{2,1,0:T(8,128)(2,1)}, bf16[3,384,128]{2,1,0:T(8,128)(2,1)}, u32[]{:S(2)}, u32[]{:S(2)}) collective-permute-start(bf16[3,384,128]{2,1,0:T(8,128)(2,1)} %get-tuple-element.31), channel_id=1, source_target_pairs={{0,24},{4,28},{8,16},{12,20},{16,8},{20,12},{24,0},{28,4},{1,25},{... | collective-permute-start | bytes 884744 | tf_op jit(solution)/shard_map/ppermute | solution.py:555
  7.5 18.1 %collective-permute-start.1 = (bf16[3,384,128]{2,1,0:T(8,128)(2,1)}, bf16[3,384,128]{2,1,0:T(8,128)(2,1)}, u32[]{:S(2)}, u32[]{:S(2)}) collective-permute-start(bf16[3,384,128]{2,1,0:T(8,128)(2,1)} %get-tuple-element.32), channel_id=1, source_target_pairs={{0,16},{4,20},{8,24},{12,28},{16,0},{20,4},{24,8},{28,12},{1,17},{... | collective-permute-start | bytes 884744 | tf_op jit(solution)/shard_map/ppermute | solution.py:555
  9.4 14.9 %all-to-all-start = ((bf16[8,144,128]{2,1,0:T(8,128)(2,1)}), bf16[8,144,128]{2,1,0:T(8,128)(2,1)S(1)}, u32[]{:S(2)}, u32[]{:S(2)}) async-start(bf16[8,144,128]{2,1,0:T(8,128)(2,1)} %get-tuple-element.28), calls=%async_computation | async-start | bytes 589824 | tf_op jit(solution)/shard_map/all_to_all | solution.py:544
  12.8 18.0 %collective-permute-start.2 = (bf16[3,384,128]{2,1,0:T(8,128)(2,1)}, bf16[3,384,128]{2,1,0:T(8,128)(2,1)}, u32[]{:S(2)}, u32[]{:S(2)}) collective-permute-start(bf16[3,384,128]{2,1,0:T(8,128)(2,1)} %get-tuple-element.33), channel_id=1, source_target_pairs={{0,8},{4,12},{8,0},{12,4},{16,24},{20,28},{24,16},{28,20},{1,9},{5... | collective-permute-start | bytes 884744 | tf_op jit(solution)/shard_map/ppermute | solution.py:555
  14.8 17.7 %collective-permute-start.3 = (bf16[3,384,128]{2,1,0:T(8,128)(2,1)}, bf16[3,384,128]{2,1,0:T(8,128)(2,1)}, u32[]{:S(2)}, u32[]{:S(2)}) collective-permute-start(bf16[3,384,128]{2,1,0:T(8,128)(2,1)} %get-tuple-element.36), channel_id=1, source_target_pairs={{0,28},{4,24},{8,20},{12,16},{16,12},{20,8},{24,4},{28,0},{1,29},{... | collective-permute-start | bytes 884744 | tf_op jit(solution)/shard_map/ppermute | solution.py:555
  15.7 21.1 %collective-permute-start.4 = (bf16[3,384,128]{2,1,0:T(8,128)(2,1)}, bf16[3,384,128]{2,1,0:T(8,128)(2,1)}, u32[]{:S(2)}, u32[]{:S(2)}) collective-permute-start(bf16[3,384,128]{2,1,0:T(8,128)(2,1)} %get-tuple-element.37), channel_id=1, source_target_pairs={{0,20},{4,16},{8,28},{12,24},{16,4},{20,0},{24,12},{28,8},{1,21},{... | collective-permute-start | bytes 884744 | tf_op jit(solution)/shard_map/ppermute | solution.py:555
  16.1 1.1 %copy-start.2 = (bf16[384,1024]{1,0:T(8,128)(2,1)S(1)}, bf16[384,1024]{1,0:T(8,128)(2,1)}, u32[]{:S(2)}) copy-start(bf16[384,1024]{1,0:T(8,128)(2,1)} %q_hbm.3) | copy-start | bytes 2359300
  24.3 13.4 %collective-permute-start.5 = (bf16[3,384,128]{2,1,0:T(8,128)(2,1)}, bf16[3,384,128]{2,1,0:T(8,128)(2,1)S(1)}, u32[]{:S(2)}, u32[]{:S(2)}) collective-permute-start(bf16[3,384,128]{2,1,0:T(8,128)(2,1)} %get-tuple-element.38), channel_id=1, source_target_pairs={{0,12},{4,8},{8,4},{12,0},{16,28},{20,24},{24,20},{28,16},{1,13},{... | collective-permute-start | bytes 884744 | tf_op jit(solution)/shard_map/ppermute | solution.py:555
  25.6 12.0 %collective-permute-start.6 = (bf16[3,384,128]{2,1,0:T(8,128)(2,1)}, bf16[3,384,128]{2,1,0:T(8,128)(2,1)S(1)}, u32[]{:S(2)}, u32[]{:S(2)}) collective-permute-start(bf16[3,384,128]{2,1,0:T(8,128)(2,1)} %get-tuple-element.39), channel_id=1, source_target_pairs={{0,4},{4,0},{8,12},{12,8},{16,20},{20,16},{24,28},{28,24},{1,5},{5... | collective-permute-start | bytes 884744 | tf_op jit(solution)/shard_map/ppermute | solution.py:555
  27.4 19.6 %all-to-all-start.1 = ((bf16[8,144,128]{2,1,0:T(8,128)(2,1)}), bf16[8,144,128]{2,1,0:T(8,128)(2,1)S(1)}, u32[]{:S(2)}, u32[]{:S(2)}) async-start(bf16[8,144,128]{2,1,0:T(8,128)(2,1)} %get-tuple-element.30), calls=%async_computation.1 | async-start | bytes 589824 | tf_op jit(solution)/shard_map/all_to_all | solution.py:544
  37.7 1.0 %copy-start.6 = (bf16[3,384,128]{2,1,0:T(8,128)(2,1)S(1)}, bf16[3,384,128]{2,1,0:T(8,128)(2,1)}, u32[]{:S(2)}) copy-start(bf16[3,384,128]{2,1,0:T(8,128)(2,1)} %get-tuple-element.23.refs_7_) | copy-start | bytes 884740
  46.9 4.4 %copy-start.3 = (bf16[384,1024]{1,0:T(8,128)(2,1)S(1)}, bf16[384,1024]{1,0:T(8,128)(2,1)}, u32[]{:S(2)}) copy-start(bf16[384,1024]{1,0:T(8,128)(2,1)} %q_hbm.3) | copy-start | bytes 2359300
  47.0 17.0 %all-to-all-start.2 = ((bf16[8,384,128]{2,1,0:T(8,128)(2,1)}), bf16[8,384,128]{2,1,0:T(8,128)(2,1)}, u32[]{:S(2)}, u32[]{:S(2)}) async-start(bf16[8,384,128]{2,1,0:T(8,128)(2,1)} %bitcast.2), calls=%async_computation.2 | async-start | bytes 1572864 | tf_op jit(solution)/shard_map/all_to_all | solution.py:544
  51.3 10.5 %copy-start.5 = (f32[1024]{0:T(1024)S(1)}, f32[1024]{0:T(1024)}, u32[]{:S(2)}) copy-start(f32[1024]{0:T(1024)} %param.13) | copy-start | bytes 12292
  52.6 5.1 %collective-permute-start.9 = (f32[8,384]{1,0:T(8,128)S(1)}, f32[8,384]{1,0:T(8,128)S(1)}, u32[]{:S(2)}, u32[]{:S(2)}) collective-permute-start(f32[8,384]{1,0:T(8,128)S(1)} %get-tuple-element.43.refs_0_), channel_id=1, source_target_pairs={{0,3},{1,0},{2,1},{3,2},{4,7},{5,4},{6,5},{7,6},{8,11},{9,8},{10,9... | collective-permute-start | bytes 36872 | tf_op jit(solution)/shard_map/ppermute | solution.py:583
  56.3 4.7 %collective-permute-start.8 = (f32[8,384]{1,0:T(8,128)S(1)}, f32[8,384]{1,0:T(8,128)S(1)}, u32[]{:S(2)}, u32[]{:S(2)}) collective-permute-start(f32[8,384]{1,0:T(8,128)S(1)} %get-tuple-element.43.refs_0_), channel_id=1, source_target_pairs={{0,2},{1,3},{2,0},{3,1},{4,6},{5,7},{6,4},{7,5},{8,10},{9,11},{10,... | collective-permute-start | bytes 36872 | tf_op jit(solution)/shard_map/ppermute | solution.py:583
  56.3 5.5 %collective-permute-start.7 = (f32[8,384]{1,0:T(8,128)S(1)}, f32[8,384]{1,0:T(8,128)S(1)}, u32[]{:S(2)}, u32[]{:S(2)}) collective-permute-start(f32[8,384]{1,0:T(8,128)S(1)} %get-tuple-element.43.refs_0_), channel_id=1, source_target_pairs={{0,1},{1,2},{2,3},{3,0},{4,5},{5,6},{6,7},{7,4},{8,9},{9,10},{10,1... | collective-permute-start | bytes 36872 | tf_op jit(solution)/shard_map/ppermute | solution.py:583
